TPU v7x, 128 devices: a whole 4x4x4 slice. The times are simulated.
128 devices in a mesh: rep: 4 (over x_hi, core), shard: 32 (over y, x_lo, z).
Axes of the slice: x: 4 (x_hi: 2, x_lo: 2; x = x_hi * 2 + x_lo), y: 4, z: 4, core: 2. Of those that a mesh axis runs over, the one named last changes fastest.
Arguments:
- inputs: bfloat16 [128, 128, 1024], P(('rep', 'shard')), may hold values from -6 to 6
- lengths: int32 [128], P(('rep', 'shard')), may hold values from 32 to 128, as said below
- cotangent: bfloat16 [128, 128, 1024], P(('rep', 'shard')), may hold values from -6 to 6
- w_qkv: bfloat16 [1, 1024, 3072], P(None, 'shard'), may hold values from -0.1875 to 0.1875
- b_qv: bfloat16 [1, 2, 1024], P(None, None, 'shard'), may hold values from -4 to 4
- w_att: bfloat16 [1, 1024, 1024], P(None, 'shard'), may hold values from -1 to 1
- b_att: bfloat16 [1, 1024], P(None, 'shard'), may hold values from -4 to 4
- norm1_gain: bfloat16 [1, 1024], P(None, 'shard'), may hold values from 0.5 to 1.5
- norm1_bias: bfloat16 [1, 1024], P(None, 'shard'), may hold values from -4 to 4
- w_in: bfloat16 [1, 1024, 4096], P(None, 'shard'), may hold values from -0.1875 to 0.1875
- b_in: bfloat16 [1, 4096], P(None, 'shard'), may hold values from -4 to 4
- w_out: bfloat16 [1, 4096, 1024], P(None, 'shard'), may hold values from -0.09375 to 0.09375
- b_out: bfloat16 [1, 1024], P(None, 'shard'), may hold values from -4 to 4
- norm2_gain: bfloat16 [1, 1024], P(None, 'shard'), may hold values from 0.5 to 1.5
- norm2_bias: bfloat16 [1, 1024], P(None, 'shard'), may hold values from -4 to 4
Outputs:
- outputs: bfloat16 [128, 128, 1024], P(('rep', 'shard'))
- grad_inputs: float32 [128, 128, 1024], P(('rep', 'shard'))
- grad_w_qkv: float32 [1, 1024, 3072], P(None, 'shard')
- grad_b_qv: float32 [1, 2, 1024], P(None, None, 'shard')
- grad_w_att: float32 [1, 1024, 1024], P(None, 'shard')
- grad_b_att: float32 [1, 1024], P(None, 'shard')
- grad_norm1_gain: float32 [1, 1024], P(None, 'shard')
- grad_norm1_bias: float32 [1, 1024], P(None, 'shard')
- grad_w_in: float32 [1, 1024, 4096], P(None, 'shard')
- grad_b_in: float32 [1, 4096], P(None, 'shard')
- grad_w_out: float32 [1, 4096, 1024], P(None, 'shard')
- grad_b_out: float32 [1, 1024], P(None, 'shard')
- grad_norm2_gain: float32 [1, 1024], P(None, 'shard')
- grad_norm2_bias: float32 [1, 1024], P(None, 'shard')
Inputs may be any that keep to these rules, and one draw needn't show every extreme that they name: `lengths`: some sequence has all 128 positions valid.
All inputs are finite; a program needn't handle non-finite values.
Results may differ from a plain program's by a relative error of at most 0.013.
Values may be sent and summed in bfloat16 or wider, within the bound.
No kernel may reach another device: no remote copies, remote signals or barrier semaphores. Data moves between devices by JAX's collectives and lax.ppermute only.
A program may use at most 192 MiB of HBM per device.

v0:
```python
import math

import jax
import jax.numpy as jnp
from jax import lax
from jax.sharding import PartitionSpec as P

HEAD_DIM = 64
LAYERS = 1


EPS = 1e-12
ROOT_HALF = 0.7071067811865476
INV_ROOT_TWO_PI = 0.3989422804014327


def sent_together(arrays, axis, dim, along):
    columns = [a.reshape(*a.shape[:along], -1) for a in arrays]
    both = jnp.concatenate(columns, axis=along)
    filled, at, done = (lax.all_gather(both, axis, axis=dim, tiled=True), 0, [])
    for a, column in zip(arrays, columns):
        share = filled[..., at : at + column.shape[along]]
        done.append(share.reshape(*share.shape[:along], *a.shape[along:]))
        at += column.shape[along]
    return tuple(done)


def in_one_piece(arrays, axis, dim, along):
    columns = [a.reshape(*a.shape[:along], -1) for a in arrays]
    both = jnp.concatenate(columns, axis=along)
    filled, at, done = (lax.psum_scatter(both, axis, scatter_dimension=dim, tiled=True), 0, [])
    for a, column in zip(arrays, columns):
        share = filled[..., at : at + column.shape[along]]
        done.append(share.reshape(*share.shape[:along], *a.shape[along:]))
        at += column.shape[along]
    return tuple(done)


def together(arrays, axis):
    line, at, done = (jnp.concatenate([a.reshape(-1) for a in arrays]), 0, [])
    so_far = lax.psum(line, axis)
    for a in arrays:
        done.append(so_far[at : at + a.size].reshape(a.shape))
        at += a.size
    return tuple(done)


def batched(form, left, right):
    return jnp.einsum(form, left, right, preferred_element_type=jnp.float32)


def layer_norm(residual, gain, shift):
    row_mean = jnp.mean(residual, axis=-1, keepdims=True)
    centered = residual - row_mean
    variance = jnp.mean(centered * centered, axis=-1, keepdims=True)
    inv_std = lax.rsqrt(variance + EPS)
    normed = centered * inv_std
    return (normed * gain.astype(jnp.float32) + shift.astype(jnp.float32), normed, inv_std)


def norm_backward(upstream, normed, inv_std, gain):
    grad_gain = jnp.sum(upstream * normed, axis=0)
    grad_shift = jnp.sum(upstream, axis=0)
    scaled = upstream * gain.astype(jnp.float32)
    grad_res = inv_std * (
        scaled
        - jnp.mean(scaled, axis=-1, keepdims=True)
        - normed * jnp.mean(scaled * normed, axis=-1, keepdims=True)
    )
    return (grad_res, grad_gain, grad_shift)


def attention_scores(query_bf, key_bf, key_valid):
    scores = batched("bqhe,bkhe->bhqk", query_bf, key_bf) * (1.0 / math.sqrt(HEAD_DIM))
    return jnp.where(key_valid[:, None, None, :], scores, -1e30)


def layer_forward(hidden, hidden_bf, params, key_valid, batch_size):
    (
        w_qkv,
        b_qv,
        w_att,
        b_att,
        gain_one,
        shift_one,
        w_in,
        b_in,
        w_out,
        b_out,
        gain_two,
        shift_two,
    ) = params
    model_width = hidden.shape[1]
    seq_count = hidden.shape[0] // batch_size
    shape_heads = (batch_size, seq_count, model_width // HEAD_DIM, HEAD_DIM)
    packed = jnp.dot(hidden_bf, w_qkv, preferred_element_type=jnp.float32)
    bias_qv = b_qv.astype(jnp.float32)
    query_bf = (packed[:, :model_width] + bias_qv[0]).astype(jnp.bfloat16).reshape(shape_heads)
    key_bf = packed[:, model_width : 2 * model_width].astype(jnp.bfloat16).reshape(shape_heads)
    value_bf = (packed[:, 2 * model_width :] + bias_qv[1]).astype(jnp.bfloat16).reshape(shape_heads)
    scores = attention_scores(query_bf, key_bf, key_valid)
    row_max = jnp.max(scores, axis=-1, keepdims=True)
    row_lse = row_max + jnp.log(jnp.sum(jnp.exp(scores - row_max), axis=-1, keepdims=True))
    probs_bf = jnp.exp(scores - row_lse).astype(jnp.bfloat16)
    context_bf = (
        batched("bhqk,bkhe->bqhe", probs_bf, value_bf).astype(jnp.bfloat16).reshape(-1, model_width)
    )
    first = (
        hidden
        + jnp.dot(context_bf, w_att, preferred_element_type=jnp.float32)
        + b_att.astype(jnp.float32)
    )
    middle, normed_one, inv_one = layer_norm(first, gain_one, shift_one)
    middle_bf = middle.astype(jnp.bfloat16)
    pre_act = jnp.dot(middle_bf, w_in, preferred_element_type=jnp.float32) + b_in.astype(
        jnp.float32
    )
    act_bf = (pre_act * 0.5 * (1.0 + jax.scipy.special.erf(pre_act * ROOT_HALF))).astype(
        jnp.bfloat16
    )
    second = (
        middle
        + jnp.dot(act_bf, w_out, preferred_element_type=jnp.float32)
        + b_out.astype(jnp.float32)
    )
    result, normed_two, inv_two = layer_norm(second, gain_two, shift_two)
    stored = (
        hidden_bf,
        query_bf,
        key_bf,
        value_bf,
        row_lse,
        context_bf,
        normed_one,
        inv_one,
        middle_bf,
        pre_act,
        act_bf,
        normed_two,
        inv_two,
    )
    return (result, stored)


def layer_backward(upstream, stored, params, key_valid):
    (
        w_qkv,
        b_qv,
        w_att,
        b_att,
        gain_one,
        shift_one,
        w_in,
        b_in,
        w_out,
        b_out,
        gain_two,
        shift_two,
    ) = params
    (
        hidden_bf,
        query_bf,
        key_bf,
        value_bf,
        row_lse,
        context_bf,
        normed_one,
        inv_one,
        middle_bf,
        pre_act,
        act_bf,
        normed_two,
        inv_two,
    ) = stored
    model_width = upstream.shape[1]
    shape_heads = query_bf.shape
    grad_second, grad_gain_two, grad_shift_two = norm_backward(
        upstream, normed_two, inv_two, gain_two
    )
    grad_b_out = jnp.sum(grad_second, axis=0)
    second_bf = grad_second.astype(jnp.bfloat16)
    grad_w_out = jnp.dot(act_bf.T, second_bf, preferred_element_type=jnp.float32)
    back_act = jnp.dot(second_bf, w_out.T, preferred_element_type=jnp.float32)
    cumulative = 0.5 * (1.0 + jax.scipy.special.erf(pre_act * ROOT_HALF))
    density = jnp.exp(-0.5 * pre_act * pre_act) * INV_ROOT_TWO_PI
    grad_pre = back_act * (cumulative + pre_act * density)
    pre_bf = grad_pre.astype(jnp.bfloat16)
    grad_w_in = jnp.dot(middle_bf.T, pre_bf, preferred_element_type=jnp.float32)
    grad_b_in = jnp.sum(grad_pre, axis=0)
    grad_middle = grad_second + jnp.dot(pre_bf, w_in.T, preferred_element_type=jnp.float32)
    grad_first, grad_gain_one, grad_shift_one = norm_backward(
        grad_middle, normed_one, inv_one, gain_one
    )
    grad_b_att = jnp.sum(grad_first, axis=0)
    first_bf = grad_first.astype(jnp.bfloat16)
    grad_w_att = jnp.dot(context_bf.T, first_bf, preferred_element_type=jnp.float32)
    grad_context = (
        jnp.dot(first_bf, w_att.T, preferred_element_type=jnp.float32)
        .astype(jnp.bfloat16)
        .reshape(shape_heads)
    )
    scores = attention_scores(query_bf, key_bf, key_valid)
    probs = jnp.exp(scores - row_lse)
    grad_value = batched("bhqk,bqhe->bkhe", probs.astype(jnp.bfloat16), grad_context).reshape(
        -1, model_width
    )
    grad_probs = batched("bqhe,bkhe->bhqk", grad_context, value_bf)
    inner = jnp.sum(probs * grad_probs, axis=-1, keepdims=True)
    grad_scores = (probs * (grad_probs - inner) * (1.0 / math.sqrt(HEAD_DIM))).astype(jnp.bfloat16)
    grad_query = batched("bhqk,bkhe->bqhe", grad_scores, key_bf).reshape(-1, model_width)
    grad_key = batched("bhqk,bqhe->bkhe", grad_scores, query_bf).reshape(-1, model_width)
    grad_b_qv = jnp.stack([jnp.sum(grad_query, axis=0), jnp.sum(grad_value, axis=0)])
    packed_bf = jnp.concatenate([grad_query, grad_key, grad_value], axis=1).astype(jnp.bfloat16)
    grad_w_qkv = jnp.dot(hidden_bf.T, packed_bf, preferred_element_type=jnp.float32)
    grad_hidden = grad_first + jnp.dot(packed_bf, w_qkv.T, preferred_element_type=jnp.float32)
    terms = (
        grad_w_qkv,
        grad_b_qv,
        grad_w_att,
        grad_b_att,
        grad_gain_one,
        grad_shift_one,
        grad_w_in,
        grad_b_in,
        grad_w_out,
        grad_b_out,
        grad_gain_two,
        grad_shift_two,
    )
    return (grad_hidden, terms)


def body(
    inputs,
    lengths,
    cotangent,
    w_qkv,
    b_qv,
    w_att,
    b_att,
    norm1_gain,
    norm1_bias,
    w_in,
    b_in,
    w_out,
    b_out,
    norm2_gain,
    norm2_bias,
):
    batch_size, seq_count, model_width = inputs.shape
    key_valid = lax.broadcasted_iota(jnp.int32, (batch_size, seq_count), 1) < lengths[:, None]
    hidden = inputs.astype(jnp.float32).reshape(-1, model_width)
    hidden_bf = inputs.reshape(-1, model_width)
    kept_params = []
    layer_index = 0
    params = (
        lax.all_gather(w_qkv[layer_index], "shard", axis=0, tiled=True),
        lax.all_gather(b_qv[layer_index], "shard", axis=1, tiled=True),
        *sent_together(
            (
                w_att[layer_index],
                b_att[layer_index],
                norm1_gain[layer_index],
                norm1_bias[layer_index],
                w_in[layer_index],
            ),
            "shard",
            0,
            1,
        ),
        *sent_together((b_in[layer_index], w_out[layer_index]), "shard", 0, 1),
        lax.all_gather(b_out[layer_index], "shard", axis=0, tiled=True),
        lax.all_gather(norm2_gain[layer_index], "shard", axis=0, tiled=True),
        lax.all_gather(norm2_bias[layer_index], "shard", axis=0, tiled=True),
    )
    hidden, stored = layer_forward(hidden, hidden_bf, params, key_valid, batch_size)
    hidden_bf = hidden.astype(jnp.bfloat16)
    kept_params.append(params)
    stored_list = [stored]
    outputs = hidden_bf.reshape(inputs.shape)
    upstream = cotangent.astype(jnp.float32).reshape(-1, model_width)
    owned = [None] * LAYERS
    for layer_index in reversed(range(LAYERS)):
        params = (
            lax.all_gather(w_qkv[layer_index], "shard", axis=0, tiled=True),
            lax.all_gather(b_qv[layer_index], "shard", axis=1, tiled=True),
            *sent_together(
                (
                    w_att[layer_index],
                    b_att[layer_index],
                    norm1_gain[layer_index],
                    norm1_bias[layer_index],
                    w_in[layer_index],
                ),
                "shard",
                0,
                1,
            ),
            *sent_together((b_in[layer_index], w_out[layer_index]), "shard", 0, 1),
            lax.all_gather(b_out[layer_index], "shard", axis=0, tiled=True),
            lax.all_gather(norm2_gain[layer_index], "shard", axis=0, tiled=True),
            lax.all_gather(norm2_bias[layer_index], "shard", axis=0, tiled=True),
        )
        upstream, terms = layer_backward(upstream, stored_list[layer_index], params, key_valid)
        shares = (
            lax.psum_scatter(terms[0], "shard", scatter_dimension=0, tiled=True),
            lax.psum_scatter(terms[1], "shard", scatter_dimension=1, tiled=True),
            *in_one_piece((terms[2], terms[3], terms[4], terms[5], terms[6]), "shard", 0, 1),
            *in_one_piece((terms[7], terms[8]), "shard", 0, 1),
            lax.psum_scatter(terms[9], "shard", scatter_dimension=0, tiled=True),
            lax.psum_scatter(terms[10], "shard", scatter_dimension=0, tiled=True),
            lax.psum_scatter(terms[11], "shard", scatter_dimension=0, tiled=True),
        )
        shares = together(
            (
                shares[0],
                shares[1],
                shares[2],
                shares[3],
                shares[4],
                shares[5],
                shares[6],
                shares[7],
                shares[8],
                shares[9],
                shares[10],
                shares[11],
            ),
            "rep",
        )
        owned[layer_index] = shares
    final = [jnp.stack([owned[0][member]]) for member in range(12)]
    grad_inputs = upstream.reshape(inputs.shape)
    return (
        outputs,
        grad_inputs,
        final[0],
        final[1],
        final[2],
        final[3],
        final[4],
        final[5],
        final[6],
        final[7],
        final[8],
        final[9],
        final[10],
        final[11],
    )


def solution(mesh):
    return jax.shard_map(
        body,
        mesh=mesh,
        in_specs=(
            P(("rep", "shard"), None, None),
            P(("rep", "shard")),
            P(("rep", "shard"), None, None),
            P(None, "shard", None),
            P(None, None, "shard"),
            P(None, "shard", None),
            P(None, "shard"),
            P(None, "shard"),
            P(None, "shard"),
            P(None, "shard", None),
            P(None, "shard"),
            P(None, "shard", None),
            P(None, "shard"),
            P(None, "shard"),
            P(None, "shard"),
        ),
        out_specs=(
            P(("rep", "shard"), None, None),
            P(("rep", "shard"), None, None),
            P(None, "shard", None),
            P(None, None, "shard"),
            P(None, "shard", None),
            P(None, "shard"),
            P(None, "shard"),
            P(None, "shard"),
            P(None, "shard", None),
            P(None, "shard"),
            P(None, "shard", None),
            P(None, "shard"),
            P(None, "shard"),
            P(None, "shard"),
        ),
        check_vma=False,
    )
```

profile of v0, /device:TPU:1, one launch (start us, length us, event | category | flops | bytes accessed | tf_op | source)
XLA Modules:
  0.0 1430.2 jit_solution(17285094910690135515)
XLA Ops:
  8.0 0.8 copy.91
  8.8 1.8 pad_maximum_fusion.4
  12.9 2.0 concatenate.21
  17.6 74.4 %all-reduce.7 = (bf16[1024]{0:T(1024)(128)(2,1)S(1)}, bf16[1024]{0:T(1024)(128)(2,1)S(1)}, bf16[1024]{0:T(1024)(128)(2,1)S(1)}) all-reduce(bf16[1024]{0:T(1024)(128)(2,1)S(1)} %dynamic-update-slice, bf16[1024]{0:T(1024)(128)(2,1)S(1)} %dynamic-update-slice.2, ...), channel_id=4, replica_groups=mesh['rep'=4,'shard'=32] {'shard'}, use_global_device_ids=true, to_apply=%add | all-reduce | flops 3072 | bytes 12288
  92.2 68.2 %all-gather.1 = bf16[1,2,1024]{1,0,2:T(2,128)(2,1)S(1)} all-gather(bf16[1,2,32]{1,0,2:T(2,128)(2,1)S(1)} %copy.83), channel_id=3, replica_groups=mesh['rep'=4,'shard'=32] {'shard'}, dimensions={2}, use_global_device_ids=true | all-gather | bytes 4224 | tf_op jit(solution)/shard_map/all_gather | solution.py:258
  161.0 7.2 slice_reduce_fusion
  168.2 3.8 fusion.11
  173.6 156.3 %all-gather.11.cloned.1.call-done = bf16[4096,1025]{1,0:T(8,128)(2,1)} async-done(((bf16[128,1025]{1,0:T(8,128)(2,1)}), bf16[4096,1025]{1,0:T(8,128)(2,1)}) %all-gather.11.cloned.1.call-update) | async-done | bytes 8396816 | tf_op jit(solution)/shard_map/all_gather | solution.py:20
  329.9 1.6 convert_reduce_fusion
  331.5 174.2 %all-gather.9.cloned.1.call-done = bf16[1024,5123]{1,0:T(8,128)(2,1)} async-done(((bf16[32,5123]{1,0:T(8,128)(2,1)}), bf16[1024,5123]{1,0:T(8,128)(2,1)}) %all-gather.9.cloned.1.call-update) | async-done | bytes 10491920 | tf_op jit(solution)/shard_map/all_gather | solution.py:20
  505.7 1.6 convert_reduce_fusion.3
  507.3 2.1 fusion.110
  509.7 6.7 fusion.13
  516.4 3.2 fusion.111
  520.2 1.0 fusion.102
  521.1 4.3 fusion.114
  525.5 3.7 multiply_reduce_fusion.1
  529.5 0.8 fusion.53
  531.0 1.3 fusion.115
  532.4 2.1 convolution_convert_fusion
  534.5 2.3 fusion.106
  537.0 1.0 copy.109
  538.3 6.4 convolution_bitcast_fusion
  544.6 12.6 copy.107
  557.3 1.0 copy-done.6
  558.3 4.0 fusion.91
  562.2 6.4 pad_maximum_fusion
  569.6 2.7 fusion.88
  572.3 8.3 fusion.73
  580.6 25.0 %concatenate.24 = f32[1024,5123]{1,0:T(8,128)} concatenate(f32[1024,1024]{1,0:T(8,128)} %fusion.88, f32[1024,1]{1,0:T(8,128)S(1)} %copy.98, f32[1024,1]{1,0:T(8,128)S(1)} %copy.99, f32[1024,1]{1,0:T(8,128)S(1)} %copy.100, f32[1024,4096]{1,0:T(8,128)} %fusion.73), dimensions={1} | concatenate | bytes 41967616 | tf_op jit(solution)/shard_map/concatenate | solution.py:30
  606.4 132.4 %all-reduce.6 = (f32[1024]{0:T(1024)S(1)}, f32[1024]{0:T(1024)S(1)}, f32[1024]{0:T(1024)S(1)}) all-reduce(f32[1024]{0:T(1024)S(1)} %get-tuple-element.35, f32[1024]{0:T(1024)S(1)} %get-tuple-element.19, f32[1024]{0:T(1024)S(1)} %convert_reduce_fusion.1), channel_id=11, replica_groups=mesh['rep'=4,'shard'=32] {'shard'}, use_global_device_ids=true, to_apply=%region_22.23.clone | all-reduce | flops 3072 | bytes 24576
  739.0 0.8 copy.110
  739.8 141.2 %reduce-scatter.13.cloned.1.call-done = f32[32,3072]{1,0:T(8,128)} async-done(((f32[1024,3072]{1,0:T(8,128)}), f32[32,3072]{1,0:T(8,128)}) %reduce-scatter.13.cloned.1.call-update) | async-done | bytes 393232 | tf_op jit(solution)/shard_map/reduce_scatter | solution.py:306
  881.0 1.1 copy.111
  882.1 207.1 %reduce-scatter.11.cloned.1.call-done = f32[128,1025]{0,1:T(8,128)} async-done(((f32[4096,1025]{0,1:T(8,128)}), f32[128,1025]{0,1:T(8,128)}) %reduce-scatter.11.cloned.1.call-update) | async-done | bytes 524816 | tf_op jit(solution)/shard_map/reduce_scatter | solution.py:31
  1089.2 1.1 slice.157
  1091.2 255.1 %reduce-scatter.9.cloned.1.call-done = f32[32,5123]{1,0:T(8,128)} async-done(((f32[1024,5123]{1,0:T(8,128)}), f32[32,5123]{1,0:T(8,128)}) %reduce-scatter.9.cloned.1.call-update) | async-done | bytes 655760 | tf_op jit(solution)/shard_map/reduce_scatter | solution.py:31
  1346.3 1.2 slice_bitcast_fusion
  1347.7 0.9 slice_bitcast_fusion.1
  1348.6 1.1 slice_reduce_fusion.2
  1349.7 16.6 %concatenate.26 = f32[393600]{0:T(1024)} concatenate(f32[98304]{0:T(1024)S(1)} %bitcast.137, f32[64]{0:T(128)S(1)} %reshape.292, f32[32768]{0:T(1024)S(1)} %bitcast.148, f32[32]{0:T(128)S(1)} %get-tuple-element.23, f32[32]{0:T(128)S(1)} %get-tuple-element.22, f32[32]{0:T(128)S(1)} %get-tuple-element.21, f32[131072]{0:T(1024)S(1)} %bitcast.136, f32[128]{0:T(128)S(1)} %slice_bitcast_fusion.9, ...), dimensions={0} | concatenate | bytes 3148800 | tf_op jit(solution)/shard_map/concatenate | solution.py:40
  1366.4 5.8 fusion.50
  1372.2 42.4 %all-reduce.10.cloned.1.call-done = f32[393600]{0:T(1024)} async-done(((f32[393600]{0:T(1024)}), f32[393600]{0:T(1024)}) %all-reduce.10.cloned.1.call-update) | async-done | bytes 1574416 | tf_op jit(solution)/shard_map/psum | solution.py:41
  1415.9 1.0 slice.160
  1417.6 1.5 fusion.105
  1419.1 0.9 stack_reshape.19
  1420.0 0.8 stack_reshape.15
  1420.8 0.9 stack_reshape.18
  (129 shorter events, 14.5 us)
Async XLA Ops:
  7.2 8.5 copy-start.17
  7.2 9.7 copy-start.19
  7.2 10.0 copy-start.20
  7.2 10.2 copy-start.21
  7.2 84.9 %copy-start.18 = (bf16[1,2,32]{2,1,0:T(2,128)(2,1)S(1)}, bf16[1,2,32]{2,1,0:T(2,128)(2,1)}, u32[]{:S(2)}) copy-start(bf16[1,2,32]{2,1,0:T(2,128)(2,1)} %param.19) | copy-start | bytes 388
  7.2 161.0 %all-gather.13.cloned.1.call-start = ((), (), s32[]{:S(2)}) async-start(), calls=%async_computation.9 | async-start | bytes 6488064 | tf_op jit(solution)/shard_map/all_gather | solution.py:257
  8.0 321.9 %all-gather.11.cloned.1.call-start = ((), (), s32[]{:S(2)}) async-start(), calls=%async_computation.5 | async-start | bytes 9732096 | tf_op jit(solution)/shard_map/all_gather | solution.py:20
  10.6 157.6 %copy-start = (bf16[1,128,1024]{2,1,0:T(8,128)(2,1)S(1)}, bf16[1,128,1024]{2,1,0:T(8,128)(2,1)}, u32[]{:S(2)}) copy-start(bf16[1,128,1024]{2,1,0:T(8,128)(2,1)} %param.15) | copy-start | bytes 786436
  10.6 495.1 %all-gather.9.cloned.1.call-start = ((), (), s32[]{:S(2)}) async-start(), calls=%async_computation.4 | async-start | bytes 11083776 | tf_op jit(solution)/shard_map/all_gather | solution.py:20
  14.9 724.0 %reduce-scatter.15.cloned.1.call-start = ((), (), s32[]{:S(2)}) async-start(), calls=%async_computation.11 | async-start | bytes 540672
  172.3 1.2 copy-start.15
  172.5 1.0 copy-start.14
  173.6 335.9 %copy-start.3 = (bf16[16,64,128]{2,1,0:T(8,128)(2,1)}, bf16[16,64,128]{2,1,0:T(8,128)(2,1)S(1)}, u32[]{:S(2)}) copy-start(bf16[16,64,128]{2,1,0:T(8,128)(2,1)S(1)} %convolution_convert_fusion.1) | copy-start | bytes 786436
  509.7 6.7 copy-start.16
  516.4 4.8 copy-start.1
  516.4 3.5 copy-start.2
  520.2 5.3 slice-start.1
  521.1 4.4 copy-start.5
  521.1 4.4 slice-start.2
  521.1 4.4 slice-start.3
  525.5 3.8 copy-start.12
  534.5 10.1 copy-start.8
  536.8 7.9 copy-start.10
  538.0 343.0 %reduce-scatter.13.cloned.1.call-start = ((), (), s32[]{:S(2)}) async-start(), calls=%async_computation.10 | async-start | bytes 12976128 | tf_op jit(solution)/shard_map/reduce_scatter | solution.py:306
  557.2 1.0 copy-start.6
  557.3 531.9 %reduce-scatter.11.cloned.1.call-start = ((), (), s32[]{:S(2)}) async-start(), calls=%async_computation.7 | async-start | bytes 17436672 | tf_op jit(solution)/shard_map/reduce_scatter | solution.py:31
  568.7 0.9 copy-start.4
  568.7 777.6 %reduce-scatter.9.cloned.1.call-start = ((), (), s32[]{:S(2)}) async-start(), calls=%async_computation.6 | async-start | bytes 22167552 | tf_op jit(solution)/shard_map/reduce_scatter | solution.py:31
  569.6 2.7 copy-start.13
  605.6 808.9 %all-reduce.10.cloned.1.call-start = ((), (), s32[]{:S(2)}) async-start(), calls=%async_computation.8 | async-start | bytes 3153920 | tf_op jit(solution)/shard_map/psum | solution.py:41
  1349.7 16.7 %copy-start.9 = (bf16[16,64,128]{2,1,0:T(8,128)(2,1)S(1)}, bf16[16,64,128]{2,1,0:T(8,128)(2,1)}, u32[]{:S(2)}) copy-start(bf16[16,64,128]{2,1,0:T(8,128)(2,1)} %copy-done.8) | copy-start | bytes 786436
  1349.7 16.7 %copy-start.11 = (bf16[1,128,16,64]{1,3,2,0:T(8,128)(2,1)S(1)}, bf16[1,128,16,64]{1,3,2,0:T(8,128)(2,1)}, u32[]{:S(2)}) copy-start(bf16[1,128,16,64]{1,3,2,0:T(8,128)(2,1)} %copy-done.10) | copy-start | bytes 786436
  1416.9 3.1 slice-start
  1419.1 2.6 copy-start.7
Sparse Core Ops, SparseCore 0:
  9.7 148.1 all-gather.12
  160.2 169.6 all-gather.10
  332.1 173.5 all-gather.8
  538.1 150.6 reduce-scatter.14
  691.2 189.7 reduce-scatter.12
  883.4 205.7 reduce-scatter.10
  1091.7 254.5 reduce-scatter.8
  1366.5 48.0 all-reduce.9
where the time goes:
time: 1440 us; the launch traced here: 1430 us
  waiting for transfers between devices  977 us (68%)
  blocking collectives  275 us (19%)
  local copies, waits for them, and re-layouts  87.5 us (6%)
  matrix products  58.6 us (4%)
  between operations  17.2 us (1%)
    reduce_scatter x2, waiting for transfers between devices, in_one_piece(): lax.psum_scatter(both, axis, scatter_dimension=dim, tiled=True)  462 us
    all_gather x2, waiting for transfers between devices, sent_together(): filled, at, done = (lax.all_gather(both, axis, axis=dim, tiled=True), 0, [])  331 us
    unnamed x2, blocking collectives  207 us
    reduce_scatter x1, waiting for transfers between devices, body(): lax.psum_scatter(terms[0], 'shard', scatter_dimension=0, tiled=True)  141 us
    all_gather x1, blocking collectives, body(): lax.all_gather(b_qv[layer_index], 'shard', axis=1, tiled=True)  68.2 us
    psum x1, waiting for transfers between devices, together(): so_far = lax.psum(line, axis)  42.4 us
  transfers between devices with their start and end apart: 8, of which 6 were waited for; matrix products, arithmetic and copies ran while one was open for 7% of the time, Pallas kernels for 0%

commit v1 on v0

--- a/solution.py
+++ b/solution.py
@@ -12,37 +12,6 @@
 EPS = 1e-12
 ROOT_HALF = 0.7071067811865476
 INV_ROOT_TWO_PI = 0.3989422804014327
-
-
-def sent_together(arrays, axis, dim, along):
-    columns = [a.reshape(*a.shape[:along], -1) for a in arrays]
-    both = jnp.concatenate(columns, axis=along)
-    filled, at, done = (lax.all_gather(both, axis, axis=dim, tiled=True), 0, [])
-    for a, column in zip(arrays, columns):
-        share = filled[..., at : at + column.shape[along]]
-        done.append(share.reshape(*share.shape[:along], *a.shape[along:]))
-        at += column.shape[along]
-    return tuple(done)
-
-
-def in_one_piece(arrays, axis, dim, along):
-    columns = [a.reshape(*a.shape[:along], -1) for a in arrays]
-    both = jnp.concatenate(columns, axis=along)
-    filled, at, done = (lax.psum_scatter(both, axis, scatter_dimension=dim, tiled=True), 0, [])
-    for a, column in zip(arrays, columns):
-        share = filled[..., at : at + column.shape[along]]
-        done.append(share.reshape(*share.shape[:along], *a.shape[along:]))
-        at += column.shape[along]
-    return tuple(done)
-
-
-def together(arrays, axis):
-    line, at, done = (jnp.concatenate([a.reshape(-1) for a in arrays]), 0, [])
-    so_far = lax.psum(line, axis)
-    for a in arrays:
-        done.append(so_far[at : at + a.size].reshape(a.shape))
-        at += a.size
-    return tuple(done)
 
 
 def batched(form, left, right):
@@ -230,6 +199,32 @@
     return (grad_hidden, terms)
 
 
+SHARD_AXES = ("y", "xl", "z")
+PAIR_AXES = ("xh", "core")
+
+
+def pack_halves(w_qkv, w_att, w_in, w_out, small):
+    rows = w_qkv.shape[0]
+    split = w_qkv.shape[1]
+    pad = jnp.zeros((rows, small.shape[1]), w_qkv.dtype)
+    first = jnp.concatenate([w_qkv, w_in[:, :split], pad], axis=1)
+    second = jnp.concatenate(
+        [w_att, w_in[:, split:], w_out.reshape(rows, -1), small], axis=1
+    )
+    return first, second
+
+
+def unpack_halves(first, second, width, ff):
+    split = 3 * width
+    w_qkv = first[:, :split]
+    w_in = jnp.concatenate([first[:, split : 2 * split], second[:, width : width + ff - split]], axis=1)
+    at = width + ff - split
+    w_att = second[:, :width]
+    w_out = second[:, at : at + ff]
+    small = second[:, at + ff :]
+    return w_qkv, w_att, w_in, w_out, small
+
+
 def body(
     inputs,
     lengths,
@@ -248,143 +243,132 @@
     norm2_bias,
 ):
     batch_size, seq_count, model_width = inputs.shape
+    ff = w_in.shape[2]
+    rows = w_qkv.shape[1]
+    core = lax.axis_index("core")
     key_valid = lax.broadcasted_iota(jnp.int32, (batch_size, seq_count), 1) < lengths[:, None]
     hidden = inputs.astype(jnp.float32).reshape(-1, model_width)
     hidden_bf = inputs.reshape(-1, model_width)
-    kept_params = []
-    layer_index = 0
+    small = jnp.concatenate(
+        [
+            b_qv[0].T,
+            b_att[0][:, None],
+            norm1_gain[0][:, None],
+            norm1_bias[0][:, None],
+            b_out[0][:, None],
+            norm2_gain[0][:, None],
+            norm2_bias[0][:, None],
+            b_in[0].reshape(rows, -1),
+        ],
+        axis=1,
+    )
+    first, second = pack_halves(w_qkv[0], w_att[0], w_in[0], w_out[0], small)
+    mine = jnp.where(core == 0, first, second)
+    gathered = lax.all_gather(mine, SHARD_AXES, axis=0, tiled=True)
+    both = lax.all_gather(gathered, "core", axis=0, tiled=False)
+    f_qkv, f_att, f_in, f_out, f_small = unpack_halves(both[0], both[1], model_width, ff)
+    f_out = f_out.reshape(ff, model_width)
+    f_bqv = f_small[:, 0:2].T
+    f_bin = f_small[:, 8:].reshape(ff)
     params = (
-        lax.all_gather(w_qkv[layer_index], "shard", axis=0, tiled=True),
-        lax.all_gather(b_qv[layer_index], "shard", axis=1, tiled=True),
-        *sent_together(
-            (
-                w_att[layer_index],
-                b_att[layer_index],
-                norm1_gain[layer_index],
-                norm1_bias[layer_index],
-                w_in[layer_index],
-            ),
-            "shard",
-            0,
-            1,
-        ),
-        *sent_together((b_in[layer_index], w_out[layer_index]), "shard", 0, 1),
-        lax.all_gather(b_out[layer_index], "shard", axis=0, tiled=True),
-        lax.all_gather(norm2_gain[layer_index], "shard", axis=0, tiled=True),
-        lax.all_gather(norm2_bias[layer_index], "shard", axis=0, tiled=True),
+        f_qkv,
+        f_bqv,
+        f_att,
+        f_small[:, 2],
+        f_small[:, 3],
+        f_small[:, 4],
+        f_in,
+        f_bin,
+        f_out,
+        f_small[:, 5],
+        f_small[:, 6],
+        f_small[:, 7],
     )
     hidden, stored = layer_forward(hidden, hidden_bf, params, key_valid, batch_size)
-    hidden_bf = hidden.astype(jnp.bfloat16)
-    kept_params.append(params)
-    stored_list = [stored]
-    outputs = hidden_bf.reshape(inputs.shape)
+    outputs = hidden.astype(jnp.bfloat16).reshape(inputs.shape)
     upstream = cotangent.astype(jnp.float32).reshape(-1, model_width)
-    owned = [None] * LAYERS
-    for layer_index in reversed(range(LAYERS)):
-        params = (
-            lax.all_gather(w_qkv[layer_index], "shard", axis=0, tiled=True),
-            lax.all_gather(b_qv[layer_index], "shard", axis=1, tiled=True),
-            *sent_together(
-                (
-                    w_att[layer_index],
-                    b_att[layer_index],
-                    norm1_gain[layer_index],
-                    norm1_bias[layer_index],
-                    w_in[layer_index],
-                ),
-                "shard",
-                0,
-                1,
-            ),
-            *sent_together((b_in[layer_index], w_out[layer_index]), "shard", 0, 1),
-            lax.all_gather(b_out[layer_index], "shard", axis=0, tiled=True),
-            lax.all_gather(norm2_gain[layer_index], "shard", axis=0, tiled=True),
-            lax.all_gather(norm2_bias[layer_index], "shard", axis=0, tiled=True),
-        )
-        upstream, terms = layer_backward(upstream, stored_list[layer_index], params, key_valid)
-        shares = (
-            lax.psum_scatter(terms[0], "shard", scatter_dimension=0, tiled=True),
-            lax.psum_scatter(terms[1], "shard", scatter_dimension=1, tiled=True),
-            *in_one_piece((terms[2], terms[3], terms[4], terms[5], terms[6]), "shard", 0, 1),
-            *in_one_piece((terms[7], terms[8]), "shard", 0, 1),
-            lax.psum_scatter(terms[9], "shard", scatter_dimension=0, tiled=True),
-            lax.psum_scatter(terms[10], "shard", scatter_dimension=0, tiled=True),
-            lax.psum_scatter(terms[11], "shard", scatter_dimension=0, tiled=True),
-        )
-        shares = together(
-            (
-                shares[0],
-                shares[1],
-                shares[2],
-                shares[3],
-                shares[4],
-                shares[5],
-                shares[6],
-                shares[7],
-                shares[8],
-                shares[9],
-                shares[10],
-                shares[11],
-            ),
-            "rep",
-        )
-        owned[layer_index] = shares
-    final = [jnp.stack([owned[0][member]]) for member in range(12)]
+    upstream, terms = layer_backward(upstream, stored, params, key_valid)
+    (g_qkv, g_bqv, g_att, g_batt, g_n1g, g_n1b, g_in, g_bin, g_out, g_bout, g_n2g, g_n2b) = terms
+    g_small = jnp.concatenate(
+        [
+            g_bqv.T,
+            g_batt[:, None],
+            g_n1g[:, None],
+            g_n1b[:, None],
+            g_bout[:, None],
+            g_n2g[:, None],
+            g_n2b[:, None],
+            g_bin.reshape(model_width, -1),
+        ],
+        axis=1,
+    )
+    g_first, g_second = pack_halves(g_qkv, g_att, g_in, g_out, g_small)
+    stacked = jnp.stack([g_first, g_second])
+    half = lax.psum_scatter(stacked, "core", scatter_dimension=0, tiled=False)
+    part = lax.psum_scatter(half, SHARD_AXES, scatter_dimension=0, tiled=True)
+    part = lax.psum(part, "xh")
+    res = lax.all_gather(part, "core", axis=0, tiled=False)
+    r_qkv, r_att, r_in, r_out, r_small = unpack_halves(res[0], res[1], model_width, ff)
     grad_inputs = upstream.reshape(inputs.shape)
     return (
         outputs,
         grad_inputs,
-        final[0],
-        final[1],
-        final[2],
-        final[3],
-        final[4],
-        final[5],
-        final[6],
-        final[7],
-        final[8],
-        final[9],
-        final[10],
-        final[11],
+        r_qkv[None],
+        r_small[:, 0:2].T[None],
+        r_att[None],
+        r_small[:, 2][None],
+        r_small[:, 3][None],
+        r_small[:, 4][None],
+        r_in[None],
+        r_small[:, 8:].reshape(-1)[None],
+        r_out.reshape(-1, model_width)[None],
+        r_small[:, 5][None],
+        r_small[:, 6][None],
+        r_small[:, 7][None],
     )
 
 
 def solution(mesh):
+    devices = mesh.devices.reshape(2, 2, 4, 2, 4)
+    fine = jax.sharding.Mesh(devices, ("xh", "core", "y", "xl", "z"))
+    seqs = P(("xh", "core", "y", "xl", "z"), None, None)
+    rows = P(None, SHARD_AXES, None)
+    vec = P(None, SHARD_AXES)
     return jax.shard_map(
         body,
-        mesh=mesh,
+        mesh=fine,
         in_specs=(
-            P(("rep", "shard"), None, None),
-            P(("rep", "shard")),
-            P(("rep", "shard"), None, None),
-            P(None, "shard", None),
-            P(None, None, "shard"),
-            P(None, "shard", None),
-            P(None, "shard"),
-            P(None, "shard"),
-            P(None, "shard"),
-            P(None, "shard", None),
-            P(None, "shard"),
-            P(None, "shard", None),
-            P(None, "shard"),
-            P(None, "shard"),
-            P(None, "shard"),
+            seqs,
+            P(("xh", "core", "y", "xl", "z")),
+            seqs,
+            rows,
+            P(None, None, SHARD_AXES),
+            rows,
+            vec,
+            vec,
+            vec,
+            rows,
+            vec,
+            rows,
+            vec,
+            vec,
+            vec,
         ),
         out_specs=(
-            P(("rep", "shard"), None, None),
-            P(("rep", "shard"), None, None),
-            P(None, "shard", None),
-            P(None, None, "shard"),
-            P(None, "shard", None),
-            P(None, "shard"),
-            P(None, "shard"),
-            P(None, "shard"),
-            P(None, "shard", None),
-            P(None, "shard"),
-            P(None, "shard", None),
-            P(None, "shard"),
-            P(None, "shard"),
-            P(None, "shard"),
+            seqs,
+            seqs,
+            rows,
+            P(None, None, SHARD_AXES),
+            rows,
+            vec,
+            vec,
+            vec,
+            rows,
+            vec,
+            rows,
+            vec,
+            vec,
+            vec,
         ),
         check_vma=False,
     )

time: 1440 us -> 989 us (0.69)
  waiting for transfers between devices: 977 us -> 675 us
  blocking collectives: 275 us -> 0 us
  local copies, waits for them, and re-layouts: 87.5 us -> 188 us
  other arithmetic: 14.2 us -> 56.6 us
    reduce_scatter x3 -> x1, waiting for transfers between devices: 603 us -> 67.5 us  [body(): half = lax.psum_scatter(stacked, 'core', scatter_dimension=0, tiled=False)]
    unnamed x9 -> x7, waiting for transfers between devices: 0.8 us -> 284 us
    unnamed x2 -> x0, blocking collectives: 207 us -> none
    all_gather x3, waiting for transfers between devices: 331 us -> 233 us  [the longest x1 165 us: body(): gathered = lax.all_gather(mine, SHARD_AXES, axis=0, tiled=True)]
    all_gather x1 -> x0, blocking collectives: 68.2 us -> none  [body(): lax.all_gather(b_qv[layer_index], 'shard', axis=1, tiled=True)]
    reshape x5, local copies, waits for them, and re-layouts: 1.44 us -> 52.6 us  [the longest x2 37.9 us: pack_halves(): w_out.reshape(rows, -1)]
    psum x1, waiting for transfers between devices: 42.4 us -> 90.4 us  [body(): part = lax.psum(part, 'xh')]
    another operation x1 -> x2, other arithmetic: 0.01 us -> 45 us  [body(): stacked = jnp.stack([g_first, g_second])]
  transfers between devices with their start and end apart: 8 -> 6, of which waited for: 6 -> 6; matrix products, arithmetic and copies ran while one was open for 7% -> 1% of each run, Pallas kernels for 0% -> 0%
where the time goes in v1:
time: 989 us; the launch traced here: 986 us
  waiting for transfers between devices  675 us (68%)
  local copies, waits for them, and re-layouts  188 us (19%)
  other arithmetic  56.6 us (6%)
  matrix products  51.2 us (5%)
  between operations  15.3 us (2%)
    unnamed x7, waiting for transfers between devices  284 us
    all_gather x1, waiting for transfers between devices, body(): gathered = lax.all_gather(mine, SHARD_AXES, axis=0, tiled=True)  165 us
    psum x1, waiting for transfers between devices, body(): part = lax.psum(part, 'xh')  90.4 us
    reduce_scatter x1, waiting for transfers between devices, body(): half = lax.psum_scatter(stacked, 'core', scatter_dimension=0, tiled=False)  67.5 us
    all_gather x1, waiting for transfers between devices, body(): both = lax.all_gather(gathered, 'core', axis=0, tiled=False)  61.1 us
    concatenate x2, local copies, waits for them, and re-layouts, pack_halves(): jnp.concatenate([w_att, w_in[:, split:], w_out.reshape(rows, -1), small],...  59.5 us
    another operation x2, other arithmetic, body(): stacked = jnp.stack([g_first, g_second])  45 us
    reshape x2, local copies, waits for them, and re-layouts, pack_halves(): w_out.reshape(rows, -1)  37.9 us
  transfers between devices with their start and end apart: 6, of which 6 were waited for; matrix products, arithmetic and copies ran while one was open for 1% of the time, Pallas kernels for 0%

profile of v1, /device:TPU:1, one launch (start us, length us, event | category | flops | bytes accessed | tf_op | source)
XLA Modules:
  0.0 985.8 jit_solution(14708803334482869462)
XLA Ops:
  9.5 1.3 reduce.40
  16.2 1.1 reshape_squeeze.6
  17.4 0.9 concatenate.23
  18.3 1.8 maximum_select_fusion
  20.2 164.5 %all-gather.5.cloned.1.call-done = bf16[1024,6156]{1,0:T(8,128)(2,1)} async-done(((bf16[32,6156]{1,0:T(8,128)(2,1)}), bf16[1024,6156]{1,0:T(8,128)(2,1)}) %all-gather.5.cloned.1.call-update) | async-done | bytes 12607504 | tf_op jit(solution)/shard_map/all_gather | solution.py:267
  185.8 61.1 %all-gather.9.cloned.1.call-done = bf16[2048,6156]{1,0:T(8,128)(2,1)} async-done(((bf16[1024,6156]{1,0:T(8,128)(2,1)}), bf16[2048,6156]{1,0:T(8,128)(2,1)}) %all-gather.9.cloned.1.call-update) | async-done | bytes 25214992 | tf_op jit(solution)/shard_map/all_gather | solution.py:268
  246.8 1.1 slice_convert_fusion.1
  248.2 1.0 convert_bitcast_fusion.1
  249.7 4.6 fusion.8
  255.7 3.0 convert_reduce_fusion.2
  258.8 2.1 fusion.97
  261.9 7.7 slice.206
  269.7 14.0 %reshape.260 = bf16[4096,1024]{1,0:T(8,128)(2,1)} reshape(bf16[1024,4096]{1,0:T(8,128)(2,1)} %slice.206) | data formatting | bytes 16777216 | tf_op jit(solution)/shard_map/reshape | solution.py:270
  283.6 1.8 slice.204
  285.4 3.4 slice.203
  288.8 1.4 fusion.7
  290.2 1.0 slice-done.2
  291.2 1.7 fusion.98
  293.4 1.0 fusion.89
  294.4 3.5 fusion.101
  297.9 3.1 multiply_reduce_fusion.1
  302.0 3.1 fusion.38
  305.1 1.1 copy.95
  306.2 1.2 fusion.95
  307.4 2.3 fusion.102
  309.7 2.9 convolution_convert_fusion
  312.6 2.8 fusion.94
  315.4 3.8 fusion.73
  319.2 8.1 fusion.76
  327.3 2.4 fusion.58
  329.8 5.7 copy-done
  335.5 2.5 slice.211
  338.8 20.4 %reshape.268 = f32[1024,4096]{1,0:T(8,128)} reshape(f32[4096,1024]{1,0:T(8,128)} %fusion.76) | data formatting | bytes 33554432 | tf_op jit(solution)/shard_map/reshape | solution.py:212
  359.2 17.6 %copy.101 = f32[1024,4096]{0,1:T(8,128)} copy(f32[1024,4096]{1,0:T(8,128)} %reshape.268) | data formatting | bytes 33554432 | tf_op jit(solution)/shard_map/reshape | solution.py:212
  376.9 1.8 convolution_bitcast_fusion
  378.6 2.8 slice-done
  381.4 10.2 %maximum_bitcast_fusion = f32[1,1024,6156]{1,2,0:T(8,128)} fusion(f32[1024,3072]{0,1:T(8,128)S(1)} %slice-done, f32[1024,3072]{0,1:T(8,128)S(1)} %convolution_bitcast_fusion, f32[6156]{0:T(1024)S(1)} %pad.8.clone), kind=kLoop, calls=%fused_computation.2 | loop fusion | flops 12607488 | bytes 50405424 | tf_op jit(solution)/shard_map/stack | solution.py:306
  391.7 58.6 %concatenate.27 = f32[1024,6156]{0,1:T(8,128)} concatenate(f32[1024,1024]{0,1:T(8,128)} %fusion.73, f32[1024,1024]{0,1:T(8,128)} %slice.211, f32[1024,4096]{0,1:T(8,128)} %copy.101, f32[1024,2]{0,1:T(2,128)S(1)} %maximum_bitcast_fusion.2, f32[1024,1]{0,1:T(1,128)S(1)} %bitcast.150, f32[1024,1]{0,1:T(1,128)S(1)} %bitcast.151, f32[1024,1]{0,1:T(1,128)S(1)} %bitcast.152, ...), dimensions={1} | concatenate | bytes 50429952 | tf_op jit(solution)/shard_map/concatenate | solution.py:211
  450.2 34.8 %pad_maximum_fusion = f32[2,1024,6156]{1,2,0:T(8,128)} fusion(f32[1,1024,6156]{1,2,0:T(8,128)} %bitcast.122, f32[1,1024,6156]{1,2,0:T(8,128)} %maximum_bitcast_fusion), kind=kLoop, calls=%fused_computation.1 | loop fusion | flops 12607488 | bytes 100859904 | tf_op jit(solution)/shard_map/stack | solution.py:306
  485.1 67.5 %reduce-scatter.5.cloned.1.call-done = f32[1,1024,6156]{1,2,0:T(8,128)} async-done(((f32[2,1024,6156]{1,2,0:T(8,128)}), f32[1,1024,6156]{1,2,0:T(8,128)}) %reduce-scatter.5.cloned.1.call-update) | async-done | bytes 25214992 | tf_op jit(solution)/shard_map/reduce_scatter | solution.py:307
  552.6 25.6 %copy.110 = f32[1024,6156]{1,0:T(8,128)} copy(f32[1024,6156]{0,1:T(8,128)} %bitcast.125) | data formatting | bytes 50429952
  578.3 284.1 %reduce-scatter.7.cloned.1.call-done = f32[32,6156]{1,0:T(8,128)} async-done(((f32[1024,6156]{1,0:T(8,128)}), f32[32,6156]{1,0:T(8,128)}) %reduce-scatter.7.cloned.1.call-update) | async-done | bytes 787984
  862.4 3.2 copy.111
  865.7 90.4 %all-reduce.2.cloned.1.call-done = f32[1,32,6156]{1,2,0:T(8,128)} async-done(((f32[1,32,6156]{1,2,0:T(8,128)}), f32[1,32,6156]{1,2,0:T(8,128)}) %all-reduce.2.cloned.1.call-update) | async-done | bytes 787984 | tf_op jit(solution)/shard_map/psum | solution.py:309
  956.1 3.2 copy.103
  959.3 5.8 fusion.34
  965.1 7.0 all-gather.7.cloned.1.call-done
  972.1 1.5 slice_bitcast_fusion
  (109 shorter events, 19.2 us)
Async XLA Ops:
  7.2 177.6 %all-gather.5.cloned.1.call-start = ((), (), s32[]{:S(2)}) async-start(), calls=%async_computation.2 | async-start | bytes 13246464 | tf_op jit(solution)/shard_map/all_gather | solution.py:267
  20.2 226.7 %all-gather.9.cloned.1.call-start = ((), (), s32[]{:S(2)}) async-start(), calls=%async_computation.6 | async-start | bytes 38535168 | tf_op jit(solution)/shard_map/all_gather | solution.py:268
  184.8 0.9 copy-start.4
  184.8 64.9 %copy-start.13 = (bf16[1,128,1024]{2,1,0:T(8,128)(2,1)S(1)}, bf16[1,128,1024]{2,1,0:T(8,128)(2,1)}, u32[]{:S(2)}) copy-start(bf16[1,128,1024]{2,1,0:T(8,128)(2,1)} %param.15) | copy-start | bytes 786436
  184.8 367.9 %reduce-scatter.5.cloned.1.call-start = ((), (), s32[]{:S(2)}) async-start(), calls=%async_computation.3 | async-start | bytes 75694080 | tf_op jit(solution)/shard_map/reduce_scatter | solution.py:307
  254.4 6.5 copy-start.17
  254.7 0.7 copy-start.5
  254.7 6.2 copy-start.18
  255.7 6.2 copy-start.6
  260.9 0.8 copy-start.1
  285.4 3.4 copy-start.2
  285.4 4.8 slice-start.1
  288.8 2.4 slice-start.2
  294.4 3.5 copy-start.10
  297.9 3.1 copy-start.15
  301.2 0.8 copy-start.8
  309.7 5.7 copy-start.7
  315.4 3.8 copy-start.11
  319.2 8.1 copy-start.3
  319.2 8.1 copy-start.16
  329.8 5.7 copy-start
  359.2 17.6 %copy-start.12 = (bf16[1,128,16,64]{1,3,2,0:T(8,128)(2,1)S(1)}, bf16[1,128,16,64]{1,3,2,0:T(8,128)(2,1)}, u32[]{:S(2)}) copy-start(bf16[1,128,16,64]{1,3,2,0:T(8,128)(2,1)} %get-tuple-element.79) | copy-start | bytes 786436
  359.2 17.6 %copy-start.14 = (bf16[1,128,1024]{2,1,0:T(8,128)(2,1)S(1)}, bf16[1,128,1024]{2,1,0:T(8,128)(2,1)}, u32[]{:S(2)}) copy-start(bf16[1,128,1024]{2,1,0:T(8,128)(2,1)} %param.15) | copy-start | bytes 786436
  359.2 17.6 %copy-start.19 = (bf16[16,64,128]{2,1,0:T(8,128)(2,1)S(1)}, bf16[16,64,128]{2,1,0:T(8,128)(2,1)}, u32[]{:S(2)}) copy-start(bf16[16,64,128]{2,1,0:T(8,128)(2,1)} %convolution_convert_fusion) | copy-start | bytes 786436
  359.2 17.6 %copy-start.20 = (bf16[1,128,16,64]{1,3,2,0:T(8,128)(2,1)S(1)}, bf16[1,128,16,64]{1,3,2,0:T(8,128)(2,1)}, u32[]{:S(2)}) copy-start(bf16[1,128,16,64]{1,3,2,0:T(8,128)(2,1)} %get-tuple-element.77) | copy-start | bytes 786436
  376.8 4.6 slice-start
  485.0 377.4 %reduce-scatter.7.cloned.1.call-start = ((), (), s32[]{:S(2)}) async-start(), calls=%async_computation.7 | async-start | bytes 26492928
  578.3 377.8 %all-reduce.2.cloned.1.call-start = ((), (), s32[]{:S(2)}) async-start(), calls=%async_computation.4 | async-start | bytes 6307840 | tf_op jit(solution)/shard_map/psum | solution.py:309
  865.6 93.7 %copy-start.9 = (f32[128,1024]{1,0:T(8,128)S(1)}, f32[128,1024]{1,0:T(8,128)}, u32[]{:S(2)}) copy-start(f32[128,1024]{1,0:T(8,128)} %copy-done.8) | copy-start | bytes 1572868
  865.7 106.4 %all-gather.7.cloned.1.call-start = ((), (), s32[]{:S(2)}) async-start(), calls=%async_computation.5 | async-start | bytes 2408448 | tf_op jit(solution)/shard_map/all_gather | solution.py:310
Sparse Core Ops, SparseCore 0:
  20.3 164.4 all-gather.4
  186.4 60.3 all-gather.8
  485.2 67.4 reduce-scatter.4
  578.4 283.9 reduce-scatter.6
  865.8 90.2 all-reduce.1
  959.4 12.6 all-gather.6

commit v2 on v1

--- a/solution.py
+++ b/solution.py
@@ -89,7 +89,12 @@
     )
     second = (
         middle
-        + jnp.dot(act_bf, w_out, preferred_element_type=jnp.float32)
+        + jnp.einsum(
+            "tkj,kjd->td",
+            act_bf.reshape(act_bf.shape[0], -1, w_out.shape[1]),
+            w_out,
+            preferred_element_type=jnp.float32,
+        )
         + b_out.astype(jnp.float32)
     )
     result, normed_two, inv_two = layer_norm(second, gain_two, shift_two)
@@ -148,13 +153,13 @@
     )
     grad_b_out = jnp.sum(grad_second, axis=0)
     second_bf = grad_second.astype(jnp.bfloat16)
-    grad_w_out = jnp.dot(act_bf.T, second_bf, preferred_element_type=jnp.float32)
-    back_act = jnp.dot(second_bf, w_out.T, preferred_element_type=jnp.float32)
+    back_act = jnp.einsum(
+        "td,kjd->tkj", second_bf, w_out, preferred_element_type=jnp.float32
+    ).reshape(second_bf.shape[0], -1)
     cumulative = 0.5 * (1.0 + jax.scipy.special.erf(pre_act * ROOT_HALF))
     density = jnp.exp(-0.5 * pre_act * pre_act) * INV_ROOT_TWO_PI
     grad_pre = back_act * (cumulative + pre_act * density)
     pre_bf = grad_pre.astype(jnp.bfloat16)
-    grad_w_in = jnp.dot(middle_bf.T, pre_bf, preferred_element_type=jnp.float32)
     grad_b_in = jnp.sum(grad_pre, axis=0)
     grad_middle = grad_second + jnp.dot(pre_bf, w_in.T, preferred_element_type=jnp.float32)
     grad_first, grad_gain_one, grad_shift_one = norm_backward(
@@ -162,7 +167,6 @@
     )
     grad_b_att = jnp.sum(grad_first, axis=0)
     first_bf = grad_first.astype(jnp.bfloat16)
-    grad_w_att = jnp.dot(context_bf.T, first_bf, preferred_element_type=jnp.float32)
     grad_context = (
         jnp.dot(first_bf, w_att.T, preferred_element_type=jnp.float32)
         .astype(jnp.bfloat16)
@@ -180,18 +184,17 @@
     grad_key = batched("bhqk,bqhe->bkhe", grad_scores, query_bf).reshape(-1, model_width)
     grad_b_qv = jnp.stack([jnp.sum(grad_query, axis=0), jnp.sum(grad_value, axis=0)])
     packed_bf = jnp.concatenate([grad_query, grad_key, grad_value], axis=1).astype(jnp.bfloat16)
-    grad_w_qkv = jnp.dot(hidden_bf.T, packed_bf, preferred_element_type=jnp.float32)
     grad_hidden = grad_first + jnp.dot(packed_bf, w_qkv.T, preferred_element_type=jnp.float32)
     terms = (
-        grad_w_qkv,
+        (hidden_bf, packed_bf),
         grad_b_qv,
-        grad_w_att,
+        (context_bf, first_bf),
         grad_b_att,
         grad_gain_one,
         grad_shift_one,
-        grad_w_in,
+        (middle_bf, pre_bf),
         grad_b_in,
-        grad_w_out,
+        (act_bf, second_bf),
         grad_b_out,
         grad_gain_two,
         grad_shift_two,
@@ -267,7 +270,7 @@
     gathered = lax.all_gather(mine, SHARD_AXES, axis=0, tiled=True)
     both = lax.all_gather(gathered, "core", axis=0, tiled=False)
     f_qkv, f_att, f_in, f_out, f_small = unpack_halves(both[0], both[1], model_width, ff)
-    f_out = f_out.reshape(ff, model_width)
+    f_out = f_out.reshape(f_out.shape[0], -1, model_width)
     f_bqv = f_small[:, 0:2].T
     f_bin = f_small[:, 8:].reshape(ff)
     params = (
@@ -302,13 +305,42 @@
         ],
         axis=1,
     )
-    g_first, g_second = pack_halves(g_qkv, g_att, g_in, g_out, g_small)
-    stacked = jnp.stack([g_first, g_second])
-    half = lax.psum_scatter(stacked, "core", scatter_dimension=0, tiled=False)
-    part = lax.psum_scatter(half, SHARD_AXES, scatter_dimension=0, tiled=True)
+    tokens = g_qkv[0].shape[0]
+    col = lambda b, c: b[:, c * model_width : (c + 1) * model_width]
+    act_split = g_out[0].reshape(tokens, model_width, -1)
+    hi = g_small.astype(jnp.bfloat16)
+    rest = g_small - hi.astype(jnp.float32)
+    mid_part = rest.astype(jnp.bfloat16)
+    low = (rest - mid_part.astype(jnp.float32)).astype(jnp.bfloat16)
+    n_small = g_small.shape[1]
+    pieces = jnp.concatenate([hi.T, mid_part.T, low.T], axis=0)
+    enc_left = jnp.zeros((tokens, model_width), jnp.bfloat16).at[: 3 * n_small].set(pieces)
+    picks = lax.broadcasted_iota(jnp.int32, (tokens, model_width), 1) == (
+        lax.broadcasted_iota(jnp.int32, (tokens, model_width), 0) % n_small
+    )
+    rows_used = lax.broadcasted_iota(jnp.int32, (tokens, model_width), 0) < 3 * n_small
+    enc_right = (picks & rows_used).astype(jnp.bfloat16)
+    zero = jnp.zeros((tokens, model_width), jnp.bfloat16)
+    lefts = [g_qkv[0]] * 3 + [g_in[0]] * 3 + [zero]
+    lefts += [g_att[0], g_in[0]] + [act_split[:, :, j] for j in range(4)] + [enc_left]
+    rights = [col(g_qkv[1], c) for c in range(3)] + [col(g_in[1], c) for c in range(3)] + [zero]
+    rights += [g_att[1], col(g_in[1], 3)] + [g_out[1]] * 4 + [enc_right]
+    wgrads = jnp.einsum(
+        "btk,btn->bkn",
+        jnp.stack(lefts),
+        jnp.stack(rights),
+        preferred_element_type=jnp.float32,
+    ).reshape(2, len(lefts) // 2, model_width, model_width)
+    half = lax.psum_scatter(wgrads, "core", scatter_dimension=0, tiled=False)
+    part = lax.psum_scatter(half, SHARD_AXES, scatter_dimension=1, tiled=True)
     part = lax.psum(part, "xh")
     res = lax.all_gather(part, "core", axis=0, tiled=False)
-    r_qkv, r_att, r_in, r_out, r_small = unpack_halves(res[0], res[1], model_width, ff)
+    r0, r1 = res[0], res[1]
+    r_qkv = jnp.concatenate([r0[0], r0[1], r0[2]], axis=1)
+    r_in = jnp.concatenate([r0[3], r0[4], r0[5], r1[1]], axis=1)
+    r_att = r1[0]
+    r_out = jnp.stack([r1[2], r1[3], r1[4], r1[5]], axis=1)
+    r_small = r1[6][:, :n_small]
     grad_inputs = upstream.reshape(inputs.shape)
     return (
         outputs,

time: 989 us -> 853 us (0.86)
  local copies, waits for them, and re-layouts: 188 us -> 75.8 us
  other arithmetic: 56.6 us -> 13.5 us
  matrix products: 51.2 us -> 69.2 us
    reduce_scatter x1 -> x2, waiting for transfers between devices: 67.5 us -> 401 us  [the longest x1 324 us: body(): part = lax.psum_scatter(half, SHARD_AXES, scatter_dimension=1, tiled=True)]
    unnamed x7 -> x6, waiting for transfers between devices: 284 us -> 0.1 us
    concatenate x2 -> x1, local copies, waits for them, and re-layouts: 59.5 us -> 0.94 us  [pack_halves(): jnp.concatenate([w_att, w_in[:, split:], w_out.reshape(rows, -1), small],...]
    reshape x3 -> x1, local copies, waits for them, and re-layouts: 51.9 us -> 1.79 us  [layer_forward(): act_bf.reshape(act_bf.shape[0], -1, w_out.shape[1])]
    psum x1, waiting for transfers between devices: 90.4 us -> 43.9 us  [body(): part = lax.psum(part, 'xh')]
    another operation x2 -> x3, other arithmetic: 45 us -> 0.22 us  [the longest x1 0.16 us: body(): jnp.stack(rights)]
    unnamed x49 -> x61, local copies, waits for them, and re-layouts: 37.9 us -> 14.3 us
    dot_general x6 -> x3, matrix products: 21.3 us -> 36.1 us  [the longest x1 22.7 us: body(): jnp.einsum('btk,btn->bkn', jnp.stack(lefts), jnp.stack(rights), preferred...]
where the time goes in v2:
time: 853 us; the launch traced here: 851 us
  waiting for transfers between devices  677 us (79%)
  local copies, waits for them, and re-layouts  75.8 us (9%)
  matrix products  69.2 us (8%)
  between operations  15.4 us (2%)
  other arithmetic  13.5 us (2%)
    reduce_scatter x1, waiting for transfers between devices, body(): part = lax.psum_scatter(half, SHARD_AXES, scatter_dimension=1, tiled=True)  324 us
    all_gather x1, waiting for transfers between devices, body(): gathered = lax.all_gather(mine, SHARD_AXES, axis=0, tiled=True)  165 us
    reduce_scatter x1, waiting for transfers between devices, body(): half = lax.psum_scatter(wgrads, 'core', scatter_dimension=0, tiled=False)  77 us
    all_gather x1, waiting for transfers between devices, body(): both = lax.all_gather(gathered, 'core', axis=0, tiled=False)  58.9 us
    psum x1, waiting for transfers between devices, body(): part = lax.psum(part, 'xh')  43.9 us
    dot_general x1, matrix products, body(): jnp.einsum('btk,btn->bkn', jnp.stack(lefts), jnp.stack(rights), preferred...  22.7 us
    slice x2, local copies, waits for them, and re-layouts, unpack_halves(): w_out = second[:, at:at + ff]  19.6 us
  transfers between devices with their start and end apart: 6, of which 6 were waited for; matrix products, arithmetic and copies ran while one was open for 1% of the time, Pallas kernels for 0%

profile of v2, /device:TPU:1, one launch (start us, length us, event | category | flops | bytes accessed | tf_op | source)
XLA Modules:
  0.0 851.5 jit_solution(18093616565759650036)
XLA Ops:
  7.2 0.8 slice.289
  8.1 0.9 slice.288
  9.5 1.3 reduce.42
  16.2 1.1 reshape_squeeze.6
  17.4 0.9 concatenate.28
  18.3 1.8 maximum_select_fusion
  20.2 164.5 %all-gather.5.cloned.1.call-done = bf16[1024,6156]{1,0:T(8,128)(2,1)} async-done(((bf16[32,6156]{1,0:T(8,128)(2,1)}), bf16[1024,6156]{1,0:T(8,128)(2,1)}) %all-gather.5.cloned.1.call-update) | async-done | bytes 12607504 | tf_op jit(solution)/shard_map/all_gather | solution.py:270
  187.9 58.9 %all-gather.9.cloned.1.call-done = bf16[2048,6156]{1,0:T(8,128)(2,1)} async-done(((bf16[1024,6156]{1,0:T(8,128)(2,1)}), bf16[2048,6156]{1,0:T(8,128)(2,1)}) %all-gather.9.cloned.1.call-update) | async-done | bytes 25214992 | tf_op jit(solution)/shard_map/all_gather | solution.py:271
  246.8 7.7 slice.304
  254.5 13.9 %dot_general.63 = bf16[4096,1024]{1,0:T(8,128)(2,1)} reshape(bf16[1024,4096]{1,0:T(8,128)(2,1)} %slice.304) | data formatting | bytes 16777216 | tf_op jit(solution)/shard_map/td,kjd->tkj/dot_general | solution.py:156
  268.4 11.9 %copy.138 = bf16[1024,4096]{0,1:T(8,128)(2,1)} copy(bf16[1024,4096]{1,0:T(8,128)(2,1)} %slice.304) | data formatting | bytes 16777216 | tf_op jit(solution)/shard_map/slice | solution.py:226
  280.4 1.1 slice_convert_fusion.1
  281.7 1.0 convert_bitcast_fusion.1
  283.2 4.6 fusion.8
  289.3 2.9 convert_reduce_fusion.2
  292.3 2.1 fusion.105
  294.6 0.9 bitcast_dynamic-update-slice_fusion.7
  295.5 1.8 slice.302
  297.3 4.0 slice.301
  301.3 5.3 multiply_convert_fusion
  306.6 1.3 copy.137
  307.9 1.8 copy.139
  309.8 6.5 fusion.106
  316.8 1.0 fusion.97
  317.8 6.9 fusion.101
  324.7 3.1 multiply_reduce_fusion.1
  328.0 0.8 copy-done.9
  328.8 2.4 fusion.39
  331.4 1.2 fusion.103
  332.6 2.3 fusion.109
  334.9 2.8 convolution_convert_fusion
  337.7 2.8 fusion.102
  348.5 1.1 copy.151
  349.7 1.0 fusion.78
  350.6 1.0 fusion.77
  351.6 1.0 fusion.76
  352.7 1.0 fusion.75
  354.7 22.7 %fusion.110 = f32[14,1024,1024]{2,1,0:T(8,128)} fusion(bf16[14,128,1024]{2,1,0:T(8,128)(2,1)} %pad_dynamic-update-slice_fusion, bf16[14,128,1024]{2,1,0:T(8,128)(2,1)S(1)} %fusion.73), kind=kOutput, calls=%fused_computation.196 | convolution fusion | flops 3758096384 | bytes 66060288 | tf_op jit(solution)/shard_map/btk,btn->bkn/dot_general | solution.py:328
  377.5 77.0 %reduce-scatter.3.cloned.1.call-done = f32[1,7,1024,1024]{3,2,1,0:T(8,128)} async-done(((f32[2,7,1024,1024]{3,2,1,0:T(8,128)}), f32[1,7,1024,1024]{3,2,1,0:T(8,128)}) %reduce-scatter.3.cloned.1.call-update) | async-done | bytes 29360144 | tf_op jit(solution)/shard_map/reduce_scatter | solution.py:334
  454.6 324.2 %reduce-scatter.5.cloned.1.call-done = f32[7,32,1024]{2,1,0:T(8,128)} async-done(((f32[7,1024,1024]{2,1,0:T(8,128)}), f32[7,32,1024]{2,1,0:T(8,128)}) %reduce-scatter.5.cloned.1.call-update) | async-done | bytes 917520 | tf_op jit(solution)/shard_map/reduce_scatter | solution.py:335
  778.9 43.9 %all-reduce.3.cloned.1.call-done = f32[1,7,32,1024]{3,2,1,0:T(8,128)} async-done(((f32[1,7,32,1024]{3,2,1,0:T(8,128)}), f32[1,7,32,1024]{3,2,1,0:T(8,128)}) %all-reduce.3.cloned.1.call-update) | async-done | bytes 917520 | tf_op jit(solution)/shard_map/psum | solution.py:336
  822.9 5.8 fusion.34
  828.7 8.6 %all-gather.7.cloned.1.call-done = f32[2,7,32,1024]{3,2,1,0:T(8,128)} async-done(((f32[1,7,32,1024]{3,2,1,0:T(8,128)}), f32[2,7,32,1024]{3,2,1,0:T(8,128)}) %all-gather.7.cloned.1.call-update) | async-done | bytes 1835024 | tf_op jit(solution)/shard_map/all_gather | solution.py:337
  837.3 2.3 slice_bitcast_fusion.11
  839.6 0.8 slice_reduce_fusion.2
  840.8 1.0 broadcast_in_dim_reshape.7
  843.0 0.8 maximum_bitcast_fusion.1
  843.8 0.8 maximum_bitcast_fusion
  (127 shorter events, 22.7 us)
Async XLA Ops:
  7.2 177.6 %all-gather.5.cloned.1.call-start = ((), (), s32[]{:S(2)}) async-start(), calls=%async_computation.2 | async-start | bytes 13246464 | tf_op jit(solution)/shard_map/all_gather | solution.py:270
  20.2 226.7 %all-gather.9.cloned.1.call-start = ((), (), s32[]{:S(2)}) async-start(), calls=%async_computation.7 | async-start | bytes 38535168 | tf_op jit(solution)/shard_map/all_gather | solution.py:271
  184.8 0.9 copy-start.1
  184.8 3.1 copy-start.2
  184.8 269.7 %reduce-scatter.3.cloned.1.call-start = ((), (), s32[]{:S(2)}) async-start(), calls=%async_computation.3 | async-start | bytes 88080384 | tf_op jit(solution)/shard_map/reduce_scatter | solution.py:334
  287.9 0.9 copy-start.13
  288.2 0.7 copy-start.4
  288.3 0.8 copy-start.14
  289.3 8.0 copy-start.5
  297.3 4.0 copy-start.7
  301.3 5.3 copy-start
  309.7 7.1 copy-start.3
  309.8 8.0 copy-start.17
  316.8 7.9 slice-start
  317.8 6.9 slice-start.1
  317.8 6.9 copy-start.8
  324.6 3.1 copy-start.12
  328.0 0.8 copy-start.9
  331.4 9.1 %copy-start.6 = (bf16[16,64,128]{2,1,0:T(8,128)(2,1)S(1)}, bf16[16,64,128]{2,1,0:T(8,128)(2,1)}, u32[]{:S(2)}) copy-start(bf16[16,64,128]{2,1,0:T(8,128)(2,1)} %copy-done.5) | copy-start | bytes 786436
  337.7 9.6 %copy-start.11 = (bf16[1,128,16,64]{1,3,2,0:T(8,128)(2,1)S(1)}, bf16[1,128,16,64]{1,3,2,0:T(8,128)(2,1)}, u32[]{:S(2)}) copy-start(bf16[1,128,16,64]{1,3,2,0:T(8,128)(2,1)} %get-tuple-element.74) | copy-start | bytes 786436
  340.6 7.6 copy-start.15
  345.7 6.9 copy-start.10
  377.5 401.4 %reduce-scatter.5.cloned.1.call-start = ((), (), s32[]{:S(2)}) async-start(), calls=%async_computation.4 | async-start | bytes 30277632 | tf_op jit(solution)/shard_map/reduce_scatter | solution.py:335
  454.5 368.3 %copy-start.16 = (bf16[1,128,16,64]{1,3,2,0:T(8,128)(2,1)S(1)}, bf16[1,128,16,64]{1,3,2,0:T(8,128)(2,1)}, u32[]{:S(2)}) copy-start(bf16[1,128,16,64]{1,3,2,0:T(8,128)(2,1)} %get-tuple-element.72) | copy-start | bytes 786436
  454.6 368.3 %all-reduce.3.cloned.1.call-start = ((), (), s32[]{:S(2)}) async-start(), calls=%async_computation.5 | async-start | bytes 1835008 | tf_op jit(solution)/shard_map/psum | solution.py:336
  778.9 58.4 %all-gather.7.cloned.1.call-start = ((), (), s32[]{:S(2)}) async-start(), calls=%async_computation.6 | async-start | bytes 2752512 | tf_op jit(solution)/shard_map/all_gather | solution.py:337
Sparse Core Ops, SparseCore 0:
  20.3 164.4 all-gather.4
  186.4 60.3 all-gather.8
  377.6 76.8 reduce-scatter.2
  456.8 321.9 reduce-scatter.4
  781.1 41.6 all-reduce.2
  824.5 12.7 all-gather.6

commit v3 on v2

--- a/solution.py
+++ b/solution.py
@@ -332,8 +332,10 @@
         preferred_element_type=jnp.float32,
     ).reshape(2, len(lefts) // 2, model_width, model_width)
     half = lax.psum_scatter(wgrads, "core", scatter_dimension=0, tiled=False)
-    part = lax.psum_scatter(half, SHARD_AXES, scatter_dimension=1, tiled=True)
-    part = lax.psum(part, "xh")
+    part = lax.psum_scatter(
+        half.astype(jnp.bfloat16), SHARD_AXES, scatter_dimension=1, tiled=True
+    )
+    part = lax.psum(part.astype(jnp.float32), "xh")
     res = lax.all_gather(part, "core", axis=0, tiled=False)
     r0, r1 = res[0], res[1]
     r_qkv = jnp.concatenate([r0[0], r0[1], r0[2]], axis=1)

time: 853 us -> 745 us (0.87)
  waiting for transfers between devices: 677 us -> 549 us
  other arithmetic: 13.5 us -> 32.1 us
    reduce_scatter x1, waiting for transfers between devices: 324 us -> 178 us  [body(): lax.psum_scatter(half.astype(jnp.bfloat16), SHARD_AXES, scatter_dimension...]
    psum x1, waiting for transfers between devices: 43.9 us -> 62.2 us  [body(): part = lax.psum(part.astype(jnp.float32), 'xh')]
    convert_element_type x0 -> x1, other arithmetic: none -> 16.5 us  [body(): half.astype(jnp.bfloat16)]
where the time goes in v3:
time: 745 us; the launch traced here: 743 us
  waiting for transfers between devices  549 us (74%)
  local copies, waits for them, and re-layouts  76.8 us (10%)
  matrix products  69.2 us (9%)
  other arithmetic  32.1 us (4%)
  between operations  15.4 us (2%)
    reduce_scatter x1, waiting for transfers between devices, body(): lax.psum_scatter(half.astype(jnp.bfloat16), SHARD_AXES, scatter_dimension...  178 us
    all_gather x1, waiting for transfers between devices, body(): gathered = lax.all_gather(mine, SHARD_AXES, axis=0, tiled=True)  165 us
    reduce_scatter x1, waiting for transfers between devices, body(): half = lax.psum_scatter(wgrads, 'core', scatter_dimension=0, tiled=False)  77 us
    psum x1, waiting for transfers between devices, body(): part = lax.psum(part.astype(jnp.float32), 'xh')  62.2 us
    all_gather x1, waiting for transfers between devices, body(): both = lax.all_gather(gathered, 'core', axis=0, tiled=False)  58.9 us
    dot_general x1, matrix products, body(): jnp.einsum('btk,btn->bkn', jnp.stack(lefts), jnp.stack(rights), preferred...  22.7 us
    slice x2, local copies, waits for them, and re-layouts, unpack_halves(): w_out = second[:, at:at + ff]  19.6 us
    convert_element_type x1, other arithmetic, body(): half.astype(jnp.bfloat16)  16.5 us
  transfers between devices with their start and end apart: 6, of which 6 were waited for; matrix products, arithmetic and copies ran while one was open for 1% of the time, Pallas kernels for 0%

profile of v3, /device:TPU:1, one launch (start us, length us, event | category | flops | bytes accessed | tf_op | source)
XLA Modules:
  0.0 743.1 jit_solution(15871336206072775465)
XLA Ops:
  7.2 0.8 slice.289
  8.1 0.9 slice.288
  9.5 1.3 reduce.42
  16.2 1.1 reshape_squeeze.6
  17.4 0.9 concatenate.28
  18.3 1.8 maximum_select_fusion
  20.2 164.5 %all-gather.5.cloned.1.call-done = bf16[1024,6156]{1,0:T(8,128)(2,1)} async-done(((bf16[32,6156]{1,0:T(8,128)(2,1)}), bf16[1024,6156]{1,0:T(8,128)(2,1)}) %all-gather.5.cloned.1.call-update) | async-done | bytes 12607504 | tf_op jit(solution)/shard_map/all_gather | solution.py:270
  187.9 58.9 %all-gather.9.cloned.1.call-done = bf16[2048,6156]{1,0:T(8,128)(2,1)} async-done(((bf16[1024,6156]{1,0:T(8,128)(2,1)}), bf16[2048,6156]{1,0:T(8,128)(2,1)}) %all-gather.9.cloned.1.call-update) | async-done | bytes 25214992 | tf_op jit(solution)/shard_map/all_gather | solution.py:271
  246.8 7.7 %slice.304 = bf16[1024,4096]{1,0:T(8,128)(2,1)} slice(bf16[2048,6156]{1,0:T(8,128)(2,1)} %all-gather.9.cloned.1.call-done), slice={[1024:2048], [2048:6144]} | slice | bytes 16777216 | tf_op jit(solution)/shard_map/slice | solution.py:226
  254.5 13.9 %dot_general.63 = bf16[4096,1024]{1,0:T(8,128)(2,1)} reshape(bf16[1024,4096]{1,0:T(8,128)(2,1)} %slice.304) | data formatting | bytes 16777216 | tf_op jit(solution)/shard_map/td,kjd->tkj/dot_general | solution.py:156
  268.4 11.9 %copy.138 = bf16[1024,4096]{0,1:T(8,128)(2,1)} copy(bf16[1024,4096]{1,0:T(8,128)(2,1)} %slice.304) | data formatting | bytes 16777216 | tf_op jit(solution)/shard_map/slice | solution.py:226
  280.4 1.1 slice_convert_fusion.1
  281.7 1.0 convert_bitcast_fusion.2
  283.2 4.6 fusion.8
  289.3 2.9 convert_reduce_fusion.2
  292.3 2.2 fusion.105
  294.6 0.9 bitcast_dynamic-update-slice_fusion.7
  295.5 1.8 slice.302
  297.3 4.0 slice.301
  301.3 5.3 multiply_convert_fusion
  306.6 1.3 copy.137
  307.9 1.8 copy.139
  309.8 6.5 fusion.106
  316.8 1.0 fusion.97
  317.8 6.9 fusion.101
  324.7 3.1 multiply_reduce_fusion.1
  328.8 2.4 fusion.39
  331.4 1.2 fusion.103
  332.6 2.3 fusion.109
  334.9 2.8 convolution_convert_fusion
  337.7 2.8 fusion.102
  348.2 1.1 copy.152
  349.4 1.1 copy.151
  350.6 1.0 fusion.78
  351.5 1.0 fusion.77
  352.5 1.0 fusion.76
  353.6 1.0 fusion.75
  355.6 22.7 %fusion.110 = f32[14,1024,1024]{2,1,0:T(8,128)} fusion(bf16[14,128,1024]{2,1,0:T(8,128)(2,1)} %pad_dynamic-update-slice_fusion, bf16[14,128,1024]{2,1,0:T(8,128)(2,1)S(1)} %fusion.73), kind=kOutput, calls=%fused_computation.198 | convolution fusion | flops 3758096384 | bytes 66060288 | tf_op jit(solution)/shard_map/btk,btn->bkn/dot_general | solution.py:328
  378.4 77.0 %reduce-scatter.3.cloned.1.call-done = f32[1,7,1024,1024]{3,2,1,0:T(8,128)} async-done(((f32[2,7,1024,1024]{3,2,1,0:T(8,128)}), f32[1,7,1024,1024]{3,2,1,0:T(8,128)}) %reduce-scatter.3.cloned.1.call-update) | async-done | bytes 29360144 | tf_op jit(solution)/shard_map/reduce_scatter | solution.py:334
  455.4 16.5 %convert_bitcast_fusion = bf16[7,1024,1024]{2,1,0:T(8,128)(2,1)} fusion(f32[1,7,1024,1024]{3,2,1,0:T(8,128)} %reduce-scatter.3.cloned.1.call-done), kind=kLoop, calls=%fused_computation.1 | loop fusion | flops 7340032 | bytes 44040192 | tf_op jit(solution)/shard_map/convert_element_type | solution.py:336
  472.0 178.1 %reduce-scatter.5.cloned.1.call-done = bf16[7,32,1024]{2,1,0:T(8,128)(2,1)} async-done(((bf16[7,1024,1024]{2,1,0:T(8,128)(2,1)}), bf16[7,32,1024]{2,1,0:T(8,128)(2,1)}) %reduce-scatter.5.cloned.1.call-update) | async-done | bytes 458768 | tf_op jit(solution)/shard_map/reduce_scatter | solution.py:335
  650.2 2.0 bitcast_convert_fusion
  652.3 62.2 %all-reduce.3.cloned.1.call-done = f32[1,7,32,1024]{3,2,1,0:T(8,128)} async-done(((f32[1,7,32,1024]{3,2,1,0:T(8,128)}), f32[1,7,32,1024]{3,2,1,0:T(8,128)}) %all-reduce.3.cloned.1.call-update) | async-done | bytes 917520 | tf_op jit(solution)/shard_map/psum | solution.py:338
  714.5 5.8 fusion.34
  720.3 8.6 %all-gather.7.cloned.1.call-done = f32[2,7,32,1024]{3,2,1,0:T(8,128)} async-done(((f32[1,7,32,1024]{3,2,1,0:T(8,128)}), f32[2,7,32,1024]{3,2,1,0:T(8,128)}) %all-gather.7.cloned.1.call-update) | async-done | bytes 1835024 | tf_op jit(solution)/shard_map/all_gather | solution.py:339
  728.9 2.3 slice_bitcast_fusion.11
  732.4 1.0 broadcast_in_dim_reshape.7
  735.4 0.8 maximum_bitcast_fusion
  (129 shorter events, 24.9 us)
Async XLA Ops:
  7.2 177.6 %all-gather.5.cloned.1.call-start = ((), (), s32[]{:S(2)}) async-start(), calls=%async_computation.2 | async-start | bytes 13246464 | tf_op jit(solution)/shard_map/all_gather | solution.py:270
  20.2 226.7 %all-gather.9.cloned.1.call-start = ((), (), s32[]{:S(2)}) async-start(), calls=%async_computation.7 | async-start | bytes 38535168 | tf_op jit(solution)/shard_map/all_gather | solution.py:271
  184.8 0.9 copy-start.1
  184.8 3.1 copy-start.2
  184.8 270.6 %reduce-scatter.3.cloned.1.call-start = ((), (), s32[]{:S(2)}) async-start(), calls=%async_computation.3 | async-start | bytes 88080384 | tf_op jit(solution)/shard_map/reduce_scatter | solution.py:334
  287.9 0.9 copy-start.13
  288.2 0.7 copy-start.4
  288.3 0.8 copy-start.14
  289.3 5.3 copy-start.5
  297.3 4.0 copy-start.7
  301.3 5.3 copy-start
  309.7 7.1 copy-start.3
  309.8 8.0 %copy-start.17 = (f32[128,4096]{1,0:T(8,128)S(1)}, f32[128,4096]{1,0:T(8,128)}, u32[]{:S(2)}) copy-start(f32[128,4096]{1,0:T(8,128)} %get-tuple-element.83) | copy-start | bytes 6291460
  316.8 7.9 %slice-start = ((s8[6291456]{0:T(1024)(128)(4,1)}), s8[4194304]{0:T(1024)(128)(4,1)S(1)}, s32[]{:S(2)}) async-start(s8[6291456]{0:T(1024)(128)(4,1)} %bitcast.208), calls=%async_computation.8 | async-start | bytes 8388608
  317.8 6.9 slice-start.1
  317.8 6.9 copy-start.8
  324.6 3.1 copy-start.12
  328.0 0.8 copy-start.9
  331.4 9.1 %copy-start.6 = (bf16[16,64,128]{2,1,0:T(8,128)(2,1)S(1)}, bf16[16,64,128]{2,1,0:T(8,128)(2,1)}, u32[]{:S(2)}) copy-start(bf16[16,64,128]{2,1,0:T(8,128)(2,1)} %copy-done.5) | copy-start | bytes 786436
  340.5 6.8 copy-start.11
  345.7 7.8 %copy-start.10 = (f32[128,1024]{1,0:T(8,128)S(1)}, f32[128,1024]{1,0:T(8,128)}, u32[]{:S(2)}) copy-start(f32[128,1024]{1,0:T(8,128)} %copy-done.9) | copy-start | bytes 1572868
  378.4 271.8 %reduce-scatter.5.cloned.1.call-start = ((), (), s32[]{:S(2)}) async-start(), calls=%async_computation.4 | async-start | bytes 15138816 | tf_op jit(solution)/shard_map/reduce_scatter | solution.py:335
  472.0 242.5 %copy-start.15 = (bf16[16,64,128]{2,1,0:T(8,128)(2,1)S(1)}, bf16[16,64,128]{2,1,0:T(8,128)(2,1)}, u32[]{:S(2)}) copy-start(bf16[16,64,128]{2,1,0:T(8,128)(2,1)} %convolution_convert_fusion) | copy-start | bytes 786436
  472.0 242.5 %copy-start.16 = (bf16[1,128,16,64]{1,3,2,0:T(8,128)(2,1)S(1)}, bf16[1,128,16,64]{1,3,2,0:T(8,128)(2,1)}, u32[]{:S(2)}) copy-start(bf16[1,128,16,64]{1,3,2,0:T(8,128)(2,1)} %get-tuple-element.72) | copy-start | bytes 786436
  472.0 242.5 %all-reduce.3.cloned.1.call-start = ((), (), s32[]{:S(2)}) async-start(), calls=%async_computation.5 | async-start | bytes 1835008 | tf_op jit(solution)/shard_map/psum | solution.py:338
  652.3 76.6 %all-gather.7.cloned.1.call-start = ((), (), s32[]{:S(2)}) async-start(), calls=%async_computation.6 | async-start | bytes 2752512 | tf_op jit(solution)/shard_map/all_gather | solution.py:339
Sparse Core Ops, SparseCore 0:
  20.3 164.4 all-gather.4
  186.4 60.3 all-gather.8
  378.5 76.8 reduce-scatter.2
  472.1 178.0 reduce-scatter.4
  652.5 61.9 all-reduce.2
  716.1 12.7 all-gather.6

commit v4 on v2

--- a/solution.py
+++ b/solution.py
@@ -3,6 +3,8 @@
 import jax
 import jax.numpy as jnp
 from jax import lax
+from jax.experimental import pallas as pl
+from jax.experimental.pallas import tpu as pltpu
 from jax.sharding import PartitionSpec as P
 
 HEAD_DIM = 64
@@ -12,6 +14,77 @@
 EPS = 1e-12
 ROOT_HALF = 0.7071067811865476
 INV_ROOT_TWO_PI = 0.3989422804014327
+
+
+def _ffn_out_kernel(act_ref, w_ref, out_ref):
+    @pl.when(pl.program_id(0) == 0)
+    def _():
+        out_ref[...] = jnp.zeros_like(out_ref)
+
+    out_ref[...] += jnp.dot(act_ref[...], w_ref[...], preferred_element_type=jnp.float32)
+
+
+def ffn_out(act_grouped, w_out):
+    buffer, first_block = w_out
+    tokens = act_grouped.shape[0]
+    width = buffer.shape[0]
+    groups = act_grouped.shape[1] // width
+    return pl.pallas_call(
+        _ffn_out_kernel,
+        grid=(groups,),
+        in_specs=[
+            pl.BlockSpec((tokens, width), lambda j: (0, j)),
+            pl.BlockSpec((width, width), lambda j: (0, first_block + j)),
+        ],
+        out_specs=pl.BlockSpec((tokens, width), lambda j: (0, 0)),
+        out_shape=jax.ShapeDtypeStruct((tokens, width), jnp.float32),
+        cost_estimate=pl.CostEstimate(
+            flops=2 * tokens * width * width * groups,
+            bytes_accessed=2 * width * width * groups + 2 * tokens * width * groups + 4 * tokens * width,
+            transcendentals=0,
+        ),
+    )(act_grouped, buffer)
+
+
+def _ffn_out_back_kernel(grad_ref, w_ref, out_ref):
+    out_ref[...] = lax.dot_general(
+        grad_ref[...],
+        w_ref[...],
+        (((1,), (1,)), ((), ())),
+        preferred_element_type=jnp.float32,
+    )
+
+
+def ffn_out_back(grad_bf, w_out):
+    buffer, first_block = w_out
+    tokens = grad_bf.shape[0]
+    width = buffer.shape[0]
+    groups = 4
+    return pl.pallas_call(
+        _ffn_out_back_kernel,
+        grid=(groups,),
+        in_specs=[
+            pl.BlockSpec((tokens, width), lambda j: (0, 0)),
+            pl.BlockSpec((width, width), lambda j: (0, first_block + j)),
+        ],
+        out_specs=pl.BlockSpec((tokens, width), lambda j: (0, j)),
+        out_shape=jax.ShapeDtypeStruct((tokens, width * groups), jnp.float32),
+        cost_estimate=pl.CostEstimate(
+            flops=2 * tokens * width * width * groups,
+            bytes_accessed=2 * width * width * groups + 2 * tokens * width + 4 * tokens * width * groups,
+            transcendentals=0,
+        ),
+    )(grad_bf, buffer)
+
+
+def group_columns(x, groups):
+    tokens = x.shape[0]
+    return x.reshape(tokens, -1, groups).transpose(0, 2, 1).reshape(tokens, -1)
+
+
+def ungroup_columns(x, groups):
+    tokens = x.shape[0]
+    return x.reshape(tokens, groups, -1).transpose(0, 2, 1).reshape(tokens, -1)
 
 
 def batched(form, left, right):
@@ -89,12 +162,7 @@
     )
     second = (
         middle
-        + jnp.einsum(
-            "tkj,kjd->td",
-            act_bf.reshape(act_bf.shape[0], -1, w_out.shape[1]),
-            w_out,
-            preferred_element_type=jnp.float32,
-        )
+        + ffn_out(group_columns(act_bf, 4), w_out)
         + b_out.astype(jnp.float32)
     )
     result, normed_two, inv_two = layer_norm(second, gain_two, shift_two)
@@ -153,9 +221,7 @@
     )
     grad_b_out = jnp.sum(grad_second, axis=0)
     second_bf = grad_second.astype(jnp.bfloat16)
-    back_act = jnp.einsum(
-        "td,kjd->tkj", second_bf, w_out, preferred_element_type=jnp.float32
-    ).reshape(second_bf.shape[0], -1)
+    back_act = ungroup_columns(ffn_out_back(second_bf, w_out), 4)
     cumulative = 0.5 * (1.0 + jax.scipy.special.erf(pre_act * ROOT_HALF))
     density = jnp.exp(-0.5 * pre_act * pre_act) * INV_ROOT_TWO_PI
     grad_pre = back_act * (cumulative + pre_act * density)
@@ -270,7 +336,7 @@
     gathered = lax.all_gather(mine, SHARD_AXES, axis=0, tiled=True)
     both = lax.all_gather(gathered, "core", axis=0, tiled=False)
     f_qkv, f_att, f_in, f_out, f_small = unpack_halves(both[0], both[1], model_width, ff)
-    f_out = f_out.reshape(f_out.shape[0], -1, model_width)
+    f_out = (both[1], (model_width + ff - 3 * model_width) // model_width)
     f_bqv = f_small[:, 0:2].T
     f_bin = f_small[:, 8:].reshape(ff)
     params = (

time: 853 us -> 861 us (level)
  Pallas kernels: 0 us -> 12.8 us
  matrix products: 69.2 us -> 58.6 us
    dot_general x1 -> x0, local copies, waits for them, and re-layouts: 13.9 us -> none  [layer_backward(): jnp.einsum('td,kjd->tkj', second_bf, w_out, preferred_element_type=jnp.fl...]
    dot_general x2 -> x0, matrix products: 13.4 us -> none  [the longest x1 6.85 us: layer_backward(): jnp.einsum('td,kjd->tkj', second_bf, w_out, preferred_element_type=jnp.fl...]
    pallas_call x0 -> x2, Pallas kernels: none -> 12.8 us  [the longest x1 6.82 us: ffn_out_back(): pl.pallas_call(_ffn_out_back_kernel, grid=(groups,), in_specs=[pl.BlockSp...]
    reshape x1 -> x3, local copies, waits for them, and re-layouts: 1.79 us -> 10.5 us  [ungroup_columns(): return x.reshape(tokens, groups, -1).transpose(0, 2, 1).reshape(tokens, -1)]
    unnamed x61 -> x68, local copies, waits for them, and re-layouts: 14.3 us -> 20 us
where the time goes in v4:
time: 861 us; the launch traced here: 859 us
  waiting for transfers between devices  677 us (79%)
  local copies, waits for them, and re-layouts  75.5 us (9%)
  matrix products  58.6 us (7%)
  other arithmetic  19.4 us (2%)
  between operations  15.4 us (2%)
  Pallas kernels  12.8 us (1%)
    reduce_scatter x1, waiting for transfers between devices, body(): part = lax.psum_scatter(half, SHARD_AXES, scatter_dimension=1, tiled=True)  324 us
    all_gather x1, waiting for transfers between devices, body(): gathered = lax.all_gather(mine, SHARD_AXES, axis=0, tiled=True)  165 us
    reduce_scatter x1, waiting for transfers between devices, body(): half = lax.psum_scatter(wgrads, 'core', scatter_dimension=0, tiled=False)  77 us
    all_gather x1, waiting for transfers between devices, body(): both = lax.all_gather(gathered, 'core', axis=0, tiled=False)  58.9 us
    psum x1, waiting for transfers between devices, body(): part = lax.psum(part, 'xh')  43.9 us
    dot_general x1, matrix products, body(): jnp.einsum('btk,btn->bkn', jnp.stack(lefts), jnp.stack(rights), preferred...  22.5 us
    unnamed x68, local copies, waits for them, and re-layouts  20 us
  transfers between devices with their start and end apart: 6, of which 6 were waited for; matrix products, arithmetic and copies ran while one was open for 1% of the time, Pallas kernels for 0%

profile of v4, /device:TPU:1, one launch (start us, length us, event | category | flops | bytes accessed | tf_op | source)
XLA Modules:
  0.0 859.2 jit_solution(2808840562718835633)
XLA Ops:
  9.5 1.3 reduce.42
  16.2 1.1 reshape_squeeze.6
  17.4 0.9 concatenate.28
  18.3 1.8 maximum_select_fusion
  20.2 164.5 %all-gather.5.cloned.1.call-done = bf16[1024,6156]{1,0:T(8,128)(2,1)} async-done(((bf16[32,6156]{1,0:T(8,128)(2,1)}), bf16[1024,6156]{1,0:T(8,128)(2,1)}) %all-gather.5.cloned.1.call-update) | async-done | bytes 12607504 | tf_op jit(solution)/shard_map/all_gather | solution.py:336
  187.9 58.9 %all-gather.9.cloned.1.call-done = bf16[2048,6156]{1,0:T(8,128)(2,1)} async-done(((bf16[1024,6156]{1,0:T(8,128)(2,1)}), bf16[2048,6156]{1,0:T(8,128)(2,1)}) %all-gather.9.cloned.1.call-update) | async-done | bytes 25214992 | tf_op jit(solution)/shard_map/all_gather | solution.py:337
  246.8 1.1 slice_convert_fusion.1
  248.2 1.0 convert_bitcast_fusion.1
  249.7 4.6 fusion.8
  255.8 2.9 convert_reduce_fusion.2
  258.7 2.1 fusion.103
  262.0 1.8 slice.298
  263.8 4.0 slice.297
  267.8 5.7 multiply_convert_fusion
  273.5 1.6 copy.118
  275.1 2.4 copy.119
  277.5 2.6 copy.147
  280.0 12.2 %slice.300.w_ref = bf16[1024,6156]{1,0:T(8,128)(2,1)} slice(bf16[2048,6156]{1,0:T(8,128)(2,1)} %all-gather.9.cloned.1.call-done), slice={[1024:2048], [0:6156]} | slice | bytes 25214976 | tf_op jit(solution)/shard_map/slice | solution.py:338
  292.3 6.0 shard_map.254
  298.2 1.3 fusion.98
  300.1 1.9 fusion.94
  302.7 6.8 shard_map.255
  309.5 3.7 reshape.415
  313.2 3.9 copy.120
  317.2 2.9 copy.121
  320.1 2.8 fusion.92
  323.0 5.7 multiply_reduce_fusion.1
  329.7 2.4 fusion.38
  332.3 1.2 fusion.101
  333.5 2.3 fusion.106
  335.8 2.8 convolution_convert_fusion
  338.6 2.8 fusion.100
  345.1 2.3 fusion.99
  347.5 1.0 copy.146
  348.5 2.0 copy.145
  350.4 1.9 copy.144
  352.3 1.0 copy.143
  355.0 1.1 copy.133
  356.3 1.1 copy.132
  357.4 1.0 constant_dynamic-update-slice_fusion.4
  362.6 22.5 %fusion.107 = f32[14,1024,1024]{2,1,0:T(8,128)} fusion(bf16[14,128,1024]{2,1,0:T(8,128)(2,1)} %pad_dynamic-update-slice_fusion, bf16[14,128,1024]{2,1,0:T(8,128)(2,1)S(1)} %fusion.72), kind=kOutput, calls=%fused_computation.192 | convolution fusion | flops 3758096384 | bytes 66060288 | tf_op jit(solution)/shard_map/btk,btn->bkn/dot_general | solution.py:394
  385.2 77.0 %reduce-scatter.3.cloned.1.call-done = f32[1,7,1024,1024]{3,2,1,0:T(8,128)} async-done(((f32[2,7,1024,1024]{3,2,1,0:T(8,128)}), f32[1,7,1024,1024]{3,2,1,0:T(8,128)}) %reduce-scatter.3.cloned.1.call-update) | async-done | bytes 29360144 | tf_op jit(solution)/shard_map/reduce_scatter | solution.py:400
  462.3 324.2 %reduce-scatter.5.cloned.1.call-done = f32[7,32,1024]{2,1,0:T(8,128)} async-done(((f32[7,1024,1024]{2,1,0:T(8,128)}), f32[7,32,1024]{2,1,0:T(8,128)}) %reduce-scatter.5.cloned.1.call-update) | async-done | bytes 917520 | tf_op jit(solution)/shard_map/reduce_scatter | solution.py:401
  786.6 43.9 %all-reduce.3.cloned.1.call-done = f32[1,7,32,1024]{3,2,1,0:T(8,128)} async-done(((f32[1,7,32,1024]{3,2,1,0:T(8,128)}), f32[1,7,32,1024]{3,2,1,0:T(8,128)}) %all-reduce.3.cloned.1.call-update) | async-done | bytes 917520 | tf_op jit(solution)/shard_map/psum | solution.py:402
  830.6 5.8 fusion.35
  836.4 8.6 all-gather.7.cloned.1.call-done
  845.0 2.3 slice_bitcast_fusion.7
  848.5 1.0 broadcast_in_dim_reshape.7
  (138 shorter events, 29.9 us)
Async XLA Ops:
  7.2 177.6 %all-gather.5.cloned.1.call-start = ((), (), s32[]{:S(2)}) async-start(), calls=%async_computation.2 | async-start | bytes 13246464 | tf_op jit(solution)/shard_map/all_gather | solution.py:336
  20.2 226.7 %all-gather.9.cloned.1.call-start = ((), (), s32[]{:S(2)}) async-start(), calls=%async_computation.7 | async-start | bytes 38535168 | tf_op jit(solution)/shard_map/all_gather | solution.py:337
  184.8 0.9 copy-start.3
  184.8 3.1 copy-start.4
  184.8 277.5 %reduce-scatter.3.cloned.1.call-start = ((), (), s32[]{:S(2)}) async-start(), calls=%async_computation.3 | async-start | bytes 88080384 | tf_op jit(solution)/shard_map/reduce_scatter | solution.py:400
  254.4 0.9 copy-start.17
  254.7 0.7 copy-start.5
  254.7 0.8 copy-start.18
  255.8 8.0 copy-start.6
  263.8 4.0 copy-start.8
  267.8 5.7 copy-start
  320.1 2.9 copy-start.9
  322.9 5.7 copy-start.1
  328.9 0.8 copy-start.10
  332.3 9.1 %copy-start.7 = (bf16[16,64,128]{2,1,0:T(8,128)(2,1)S(1)}, bf16[16,64,128]{2,1,0:T(8,128)(2,1)}, u32[]{:S(2)}) copy-start(bf16[16,64,128]{2,1,0:T(8,128)(2,1)} %copy-done.6) | copy-start | bytes 786436
  345.1 8.2 copy-start.12
  348.5 10.0 %copy-start.2 = (bf16[128,4096]{1,0:T(8,128)(2,1)S(1)}, bf16[128,4096]{1,0:T(8,128)(2,1)}, u32[]{:S(2)}) copy-start(bf16[128,4096]{1,0:T(8,128)(2,1)} %copy-done.1) | copy-start | bytes 3145732
  352.3 6.3 copy-start.11
  357.4 1.4 copy-start.16
  357.4 2.1 copy-start.15
  358.5 1.8 copy-start.14
  358.5 2.5 copy-start.13
  385.2 401.4 %reduce-scatter.5.cloned.1.call-start = ((), (), s32[]{:S(2)}) async-start(), calls=%async_computation.4 | async-start | bytes 30277632 | tf_op jit(solution)/shard_map/reduce_scatter | solution.py:401
  462.2 368.3 %copy-start.19 = (bf16[16,64,128]{2,1,0:T(8,128)(2,1)S(1)}, bf16[16,64,128]{2,1,0:T(8,128)(2,1)}, u32[]{:S(2)}) copy-start(bf16[16,64,128]{2,1,0:T(8,128)(2,1)} %convolution_convert_fusion) | copy-start | bytes 786436
  462.2 368.3 %copy-start.20 = (bf16[1,128,16,64]{1,3,2,0:T(8,128)(2,1)S(1)}, bf16[1,128,16,64]{1,3,2,0:T(8,128)(2,1)}, u32[]{:S(2)}) copy-start(bf16[1,128,16,64]{1,3,2,0:T(8,128)(2,1)} %get-tuple-element.78) | copy-start | bytes 786436
  462.3 368.3 %all-reduce.3.cloned.1.call-start = ((), (), s32[]{:S(2)}) async-start(), calls=%async_computation.5 | async-start | bytes 1835008 | tf_op jit(solution)/shard_map/psum | solution.py:402
  786.6 58.4 %all-gather.7.cloned.1.call-start = ((), (), s32[]{:S(2)}) async-start(), calls=%async_computation.6 | async-start | bytes 2752512 | tf_op jit(solution)/shard_map/all_gather | solution.py:403
Sparse Core Ops, SparseCore 0:
  20.3 164.4 all-gather.4
  186.4 60.3 all-gather.8
  385.3 76.8 reduce-scatter.2
  464.5 321.9 reduce-scatter.4
  788.8 41.6 all-reduce.2
  832.2 12.7 all-gather.6

commit v5 on v4

--- a/solution.py
+++ b/solution.py
@@ -25,16 +25,16 @@
 
 
 def ffn_out(act_grouped, w_out):
-    buffer, first_block = w_out
+    buffer, which, first_block = w_out
     tokens = act_grouped.shape[0]
-    width = buffer.shape[0]
+    width = buffer.shape[1]
     groups = act_grouped.shape[1] // width
     return pl.pallas_call(
         _ffn_out_kernel,
         grid=(groups,),
         in_specs=[
             pl.BlockSpec((tokens, width), lambda j: (0, j)),
-            pl.BlockSpec((width, width), lambda j: (0, first_block + j)),
+            pl.BlockSpec((None, width, width), lambda j: (which, 0, first_block + j)),
         ],
         out_specs=pl.BlockSpec((tokens, width), lambda j: (0, 0)),
         out_shape=jax.ShapeDtypeStruct((tokens, width), jnp.float32),
@@ -56,16 +56,16 @@
 
 
 def ffn_out_back(grad_bf, w_out):
-    buffer, first_block = w_out
+    buffer, which, first_block = w_out
     tokens = grad_bf.shape[0]
-    width = buffer.shape[0]
+    width = buffer.shape[1]
     groups = 4
     return pl.pallas_call(
         _ffn_out_back_kernel,
         grid=(groups,),
         in_specs=[
             pl.BlockSpec((tokens, width), lambda j: (0, 0)),
-            pl.BlockSpec((width, width), lambda j: (0, first_block + j)),
+            pl.BlockSpec((None, width, width), lambda j: (which, 0, first_block + j)),
         ],
         out_specs=pl.BlockSpec((tokens, width), lambda j: (0, j)),
         out_shape=jax.ShapeDtypeStruct((tokens, width * groups), jnp.float32),
@@ -162,7 +162,7 @@
     )
     second = (
         middle
-        + ffn_out(group_columns(act_bf, 4), w_out)
+        + ffn_out(act_bf, w_out)
         + b_out.astype(jnp.float32)
     )
     result, normed_two, inv_two = layer_norm(second, gain_two, shift_two)
@@ -221,7 +221,7 @@
     )
     grad_b_out = jnp.sum(grad_second, axis=0)
     second_bf = grad_second.astype(jnp.bfloat16)
-    back_act = ungroup_columns(ffn_out_back(second_bf, w_out), 4)
+    back_act = ffn_out_back(second_bf, w_out)
     cumulative = 0.5 * (1.0 + jax.scipy.special.erf(pre_act * ROOT_HALF))
     density = jnp.exp(-0.5 * pre_act * pre_act) * INV_ROOT_TWO_PI
     grad_pre = back_act * (cumulative + pre_act * density)
@@ -331,14 +331,14 @@
         ],
         axis=1,
     )
-    first, second = pack_halves(w_qkv[0], w_att[0], w_in[0], w_out[0], small)
+    first, second = pack_halves(w_qkv[0], w_att[0], group_columns(w_in[0], 4), w_out[0], small)
     mine = jnp.where(core == 0, first, second)
     gathered = lax.all_gather(mine, SHARD_AXES, axis=0, tiled=True)
     both = lax.all_gather(gathered, "core", axis=0, tiled=False)
     f_qkv, f_att, f_in, f_out, f_small = unpack_halves(both[0], both[1], model_width, ff)
-    f_out = (both[1], (model_width + ff - 3 * model_width) // model_width)
+    f_out = (both, 1, (model_width + ff - 3 * model_width) // model_width)
     f_bqv = f_small[:, 0:2].T
-    f_bin = f_small[:, 8:].reshape(ff)
+    f_bin = group_columns(f_small[:, 8:].reshape(1, ff), 4)[0]
     params = (
         f_qkv,
         f_bqv,
@@ -367,13 +367,12 @@
             g_bout[:, None],
             g_n2g[:, None],
             g_n2b[:, None],
-            g_bin.reshape(model_width, -1),
+            ungroup_columns(g_bin[None], 4)[0].reshape(model_width, -1),
         ],
         axis=1,
     )
     tokens = g_qkv[0].shape[0]
     col = lambda b, c: b[:, c * model_width : (c + 1) * model_width]
-    act_split = g_out[0].reshape(tokens, model_width, -1)
     hi = g_small.astype(jnp.bfloat16)
     rest = g_small - hi.astype(jnp.float32)
     mid_part = rest.astype(jnp.bfloat16)
@@ -388,7 +387,7 @@
     enc_right = (picks & rows_used).astype(jnp.bfloat16)
     zero = jnp.zeros((tokens, model_width), jnp.bfloat16)
     lefts = [g_qkv[0]] * 3 + [g_in[0]] * 3 + [zero]
-    lefts += [g_att[0], g_in[0]] + [act_split[:, :, j] for j in range(4)] + [enc_left]
+    lefts += [g_att[0], g_in[0]] + [col(g_out[0], j) for j in range(4)] + [enc_left]
     rights = [col(g_qkv[1], c) for c in range(3)] + [col(g_in[1], c) for c in range(3)] + [zero]
     rights += [g_att[1], col(g_in[1], 3)] + [g_out[1]] * 4 + [enc_right]
     wgrads = jnp.einsum(
@@ -403,7 +402,7 @@
     res = lax.all_gather(part, "core", axis=0, tiled=False)
     r0, r1 = res[0], res[1]
     r_qkv = jnp.concatenate([r0[0], r0[1], r0[2]], axis=1)
-    r_in = jnp.concatenate([r0[3], r0[4], r0[5], r1[1]], axis=1)
+    r_in = ungroup_columns(jnp.concatenate([r0[3], r0[4], r0[5], r1[1]], axis=1), 4)
     r_att = r1[0]
     r_out = jnp.stack([r1[2], r1[3], r1[4], r1[5]], axis=1)
     r_small = r1[6][:, :n_small]

time: 861 us -> 815 us (0.947)
  local copies, waits for them, and re-layouts: 75.5 us -> 33.9 us
    slice x2 -> x0, local copies, waits for them, and re-layouts: 14.5 us -> none  [the longest x1 12.2 us: body(): both[1]]
    reshape x5 -> x0, local copies, waits for them, and re-layouts: 11.3 us -> none  [the longest x3 10.5 us: ungroup_columns(): return x.reshape(tokens, groups, -1).transpose(0, 2, 1).reshape(tokens, -1)]
    unnamed x68 -> x79, local copies, waits for them, and re-layouts: 20 us -> 15.5 us
where the time goes in v5:
time: 815 us; the launch traced here: 814 us
  waiting for transfers between devices  677 us (83%)
  matrix products  58.2 us (7%)
  local copies, waits for them, and re-layouts  33.9 us (4%)
  other arithmetic  16 us (2%)
  between operations  15.5 us (2%)
  Pallas kernels  12.8 us (2%)
    reduce_scatter x1, waiting for transfers between devices, body(): part = lax.psum_scatter(half, SHARD_AXES, scatter_dimension=1, tiled=True)  324 us
    all_gather x1, waiting for transfers between devices, body(): gathered = lax.all_gather(mine, SHARD_AXES, axis=0, tiled=True)  165 us
    reduce_scatter x1, waiting for transfers between devices, body(): half = lax.psum_scatter(wgrads, 'core', scatter_dimension=0, tiled=False)  77 us
    all_gather x1, waiting for transfers between devices, body(): both = lax.all_gather(gathered, 'core', axis=0, tiled=False)  58.9 us
    psum x1, waiting for transfers between devices, body(): part = lax.psum(part, 'xh')  43.8 us
    dot_general x1, matrix products, body(): jnp.einsum('btk,btn->bkn', jnp.stack(lefts), jnp.stack(rights), preferred...  22.5 us
  transfers between devices with their start and end apart: 6, of which 6 were waited for; matrix products, arithmetic and copies ran while one was open for 1% of the time, Pallas kernels for 0%

profile of v5, /device:TPU:1, one launch (start us, length us, event | category | flops | bytes accessed | tf_op | source)
XLA Modules:
  0.0 814.0 jit_solution(11043035866831026028)
XLA Ops:
  7.3 1.5 copy.121
  12.1 0.9 maximum_select_fusion
  13.0 164.5 %all-gather.5.cloned.1.call-done = bf16[1024,6156]{1,0:T(8,128)(2,1)} async-done(((bf16[32,6156]{1,0:T(8,128)(2,1)}), bf16[1024,6156]{1,0:T(8,128)(2,1)}) %all-gather.5.cloned.1.call-update) | async-done | bytes 12607504 | tf_op jit(solution)/shard_map/all_gather | solution.py:336
  178.5 0.7 constant_dynamic-update-slice_fusion.3
  180.0 0.7 constant_dynamic-update-slice_fusion.1
  180.7 58.9 %all-gather.9.cloned.1.call-done = bf16[2048,6156]{1,0:T(8,128)(2,1)} async-done(((bf16[1024,6156]{1,0:T(8,128)(2,1)}), bf16[2048,6156]{1,0:T(8,128)(2,1)}) %all-gather.9.cloned.1.call-update) | async-done | bytes 25214992 | tf_op jit(solution)/shard_map/all_gather | solution.py:337
  239.6 1.1 convert_bitcast_fusion.1
  240.9 1.0 convert_bitcast_fusion.2
  242.4 4.6 fusion.8
  248.5 2.9 convert_reduce_fusion.2
  251.4 2.1 fusion.106
  253.8 0.9 bitcast_dynamic-update-slice_fusion.7
  254.7 1.8 slice.297
  256.5 4.0 slice.296
  260.5 5.7 multiply_convert_fusion
  266.2 6.0 shard_map.254
  272.1 1.3 fusion.102
  274.0 1.0 fusion.98
  274.9 0.7 convert_element_type.188.grad_ref
  275.7 6.8 shard_map.255
  282.5 2.8 fusion.96
  285.4 5.3 multiply_reduce_fusion.1
  290.9 0.8 copy-done.9
  291.7 2.4 fusion.38
  294.3 1.2 fusion.104
  295.5 2.3 fusion.109
  297.7 2.8 convolution_convert_fusion
  300.5 2.8 fusion.103
  304.9 0.7 broadcast_dynamic-update-slice_fusion.1
  305.6 0.7 constant_dynamic-update-slice_fusion
  306.4 0.7 bitcast_dynamic-update-slice_fusion.8
  307.1 1.7 fusion.81
  308.8 1.7 fusion.80
  310.5 0.7 fusion.79
  312.1 1.1 copy.139
  313.5 1.1 copy.137
  315.9 22.5 %fusion.110 = f32[14,1024,1024]{2,1,0:T(8,128)} fusion(bf16[14,128,1024]{2,1,0:T(8,128)(2,1)} %pad_dynamic-update-slice_fusion, bf16[14,128,1024]{2,1,0:T(8,128)(2,1)S(1)} %fusion.72), kind=kOutput, calls=%fused_computation.197 | convolution fusion | flops 3758096384 | bytes 66060288 | tf_op jit(solution)/shard_map/btk,btn->bkn/dot_general | solution.py:393
  338.5 77.0 %reduce-scatter.3.cloned.1.call-done = f32[1,7,1024,1024]{3,2,1,0:T(8,128)} async-done(((f32[2,7,1024,1024]{3,2,1,0:T(8,128)}), f32[1,7,1024,1024]{3,2,1,0:T(8,128)}) %reduce-scatter.3.cloned.1.call-update) | async-done | bytes 29360144 | tf_op jit(solution)/shard_map/reduce_scatter | solution.py:399
  415.6 324.2 %reduce-scatter.5.cloned.1.call-done = f32[7,32,1024]{2,1,0:T(8,128)} async-done(((f32[7,1024,1024]{2,1,0:T(8,128)}), f32[7,32,1024]{2,1,0:T(8,128)}) %reduce-scatter.5.cloned.1.call-update) | async-done | bytes 917520 | tf_op jit(solution)/shard_map/reduce_scatter | solution.py:400
  740.1 43.8 %all-reduce.3.cloned.1.call-done = f32[1,7,32,1024]{3,2,1,0:T(8,128)} async-done(((f32[1,7,32,1024]{3,2,1,0:T(8,128)}), f32[1,7,32,1024]{3,2,1,0:T(8,128)}) %all-reduce.3.cloned.1.call-update) | async-done | bytes 917520 | tf_op jit(solution)/shard_map/psum | solution.py:401
  783.9 5.8 fusion.35
  789.7 8.6 %all-gather.7.cloned.1.call-done = f32[2,7,32,1024]{3,2,1,0:T(8,128)} async-done(((f32[1,7,32,1024]{3,2,1,0:T(8,128)}), f32[2,7,32,1024]{3,2,1,0:T(8,128)}) %all-gather.7.cloned.1.call-update) | async-done | bytes 1835024 | tf_op jit(solution)/shard_map/all_gather | solution.py:402
  798.3 2.3 slice_bitcast_fusion.12
  800.6 0.8 slice_reduce_fusion.2
  801.8 1.0 broadcast_in_dim_reshape.11
  804.1 0.9 copy.142
  805.0 1.4 copy.144
  806.3 0.8 maximum_bitcast_fusion.1
  (143 shorter events, 13.4 us)
Async XLA Ops:
  7.2 3.0 copy-start.26
  7.2 3.8 copy-start.19
  7.2 3.9 copy-start.20
  7.2 4.0 copy-start.21
  7.2 4.1 copy-start.22
  7.2 4.2 copy-start.23
  7.2 4.3 copy-start.24
  7.3 4.4 copy-start.25
  7.3 4.5 copy-start.14
  7.3 4.7 copy-start.18
  7.3 4.8 copy-start.17
  7.3 170.3 %all-gather.5.cloned.1.call-start = ((), (), s32[]{:S(2)}) async-start(), calls=%async_computation.2 | async-start | bytes 13246464 | tf_op jit(solution)/shard_map/all_gather | solution.py:336
  13.0 226.7 %all-gather.9.cloned.1.call-start = ((), (), s32[]{:S(2)}) async-start(), calls=%async_computation.7 | async-start | bytes 38535168 | tf_op jit(solution)/shard_map/all_gather | solution.py:337
  177.6 0.9 copy-start.1
  177.6 3.1 copy-start.3
  177.6 237.9 %reduce-scatter.3.cloned.1.call-start = ((), (), s32[]{:S(2)}) async-start(), calls=%async_computation.3 | async-start | bytes 88080384 | tf_op jit(solution)/shard_map/reduce_scatter | solution.py:399
  247.1 0.9 copy-start.12
  247.5 0.7 copy-start.13
  247.5 6.1 copy-start.4
  248.5 5.3 copy-start.5
  256.4 4.0 copy-start.7
  260.4 5.7 copy-start
  282.5 2.9 copy-start.8
  290.9 0.8 copy-start.9
  294.3 9.0 %copy-start.6 = (bf16[16,64,128]{2,1,0:T(8,128)(2,1)S(1)}, bf16[16,64,128]{2,1,0:T(8,128)(2,1)}, u32[]{:S(2)}) copy-start(bf16[16,64,128]{2,1,0:T(8,128)(2,1)} %copy-done.5) | copy-start | bytes 786436
  303.3 7.2 copy-start.2
  303.5 9.8 %copy-start.15 = (bf16[16,64,128]{2,1,0:T(8,128)(2,1)S(1)}, bf16[16,64,128]{2,1,0:T(8,128)(2,1)}, u32[]{:S(2)}) copy-start(bf16[16,64,128]{2,1,0:T(8,128)(2,1)} %convolution_convert_fusion) | copy-start | bytes 786436
  307.1 7.7 copy-start.10
  338.5 401.4 %reduce-scatter.5.cloned.1.call-start = ((), (), s32[]{:S(2)}) async-start(), calls=%async_computation.4 | async-start | bytes 30277632 | tf_op jit(solution)/shard_map/reduce_scatter | solution.py:400
  415.5 368.4 %copy-start.11 = (bf16[1,128,16,64]{1,3,2,0:T(8,128)(2,1)S(1)}, bf16[1,128,16,64]{1,3,2,0:T(8,128)(2,1)}, u32[]{:S(2)}) copy-start(bf16[1,128,16,64]{1,3,2,0:T(8,128)(2,1)} %get-tuple-element.132) | copy-start | bytes 786436
  415.5 368.4 %copy-start.16 = (bf16[1,128,16,64]{1,3,2,0:T(8,128)(2,1)S(1)}, bf16[1,128,16,64]{1,3,2,0:T(8,128)(2,1)}, u32[]{:S(2)}) copy-start(bf16[1,128,16,64]{1,3,2,0:T(8,128)(2,1)} %get-tuple-element.130) | copy-start | bytes 786436
  415.5 368.3 %all-reduce.3.cloned.1.call-start = ((), (), s32[]{:S(2)}) async-start(), calls=%async_computation.5 | async-start | bytes 1835008 | tf_op jit(solution)/shard_map/psum | solution.py:401
  739.8 58.4 %all-gather.7.cloned.1.call-start = ((), (), s32[]{:S(2)}) async-start(), calls=%async_computation.6 | async-start | bytes 2752512 | tf_op jit(solution)/shard_map/all_gather | solution.py:402
Sparse Core Ops, SparseCore 0:
  13.1 164.4 all-gather.4
  179.2 60.3 all-gather.8
  338.6 76.8 reduce-scatter.2
  417.8 321.9 reduce-scatter.4
  742.1 41.7 all-reduce.2
  785.5 12.7 all-gather.6

commit v6 on v5

--- a/solution.py
+++ b/solution.py
@@ -396,8 +396,10 @@
         jnp.stack(rights),
         preferred_element_type=jnp.float32,
     ).reshape(2, len(lefts) // 2, model_width, model_width)
-    half = lax.psum_scatter(wgrads, "core", scatter_dimension=0, tiled=False)
-    part = lax.psum_scatter(half, SHARD_AXES, scatter_dimension=1, tiled=True)
+    half = lax.psum_scatter(wgrads.astype(jnp.bfloat16), "core", scatter_dimension=0, tiled=False)
+    part = lax.psum_scatter(
+        half.astype(jnp.float32), SHARD_AXES, scatter_dimension=1, tiled=True
+    )
     part = lax.psum(part, "xh")
     res = lax.all_gather(part, "core", axis=0, tiled=False)
     r0, r1 = res[0], res[1]

time: 815 us -> 789 us (0.968)
  waiting for transfers between devices: 677 us -> 642 us
  other arithmetic: 16 us -> 32.5 us
    reduce_scatter x2, waiting for transfers between devices: 401 us -> 367 us  [the longest x1 322 us: body(): lax.psum_scatter(half.astype(jnp.float32), SHARD_AXES, scatter_dimension=...]
    convert_element_type x0 -> x1, other arithmetic: none -> 16.4 us  [body(): half.astype(jnp.float32)]
where the time goes in v6:
time: 789 us; the launch traced here: 788 us
  waiting for transfers between devices  642 us (81%)
  matrix products  50.4 us (6%)
  local copies, waits for them, and re-layouts  33.9 us (4%)
  other arithmetic  32.5 us (4%)
  between operations  15.5 us (2%)
  Pallas kernels  12.8 us (2%)
    reduce_scatter x1, waiting for transfers between devices, body(): lax.psum_scatter(half.astype(jnp.float32), SHARD_AXES, scatter_dimension=...  322 us
    all_gather x1, waiting for transfers between devices, body(): gathered = lax.all_gather(mine, SHARD_AXES, axis=0, tiled=True)  165 us
    all_gather x1, waiting for transfers between devices, body(): both = lax.all_gather(gathered, 'core', axis=0, tiled=False)  58.9 us
    reduce_scatter x1, waiting for transfers between devices, body(): lax.psum_scatter(wgrads.astype(jnp.bfloat16), 'core', scatter_dimension=0...  44.5 us
    psum x1, waiting for transfers between devices, body(): part = lax.psum(part, 'xh')  43.7 us
    convert_element_type x1, other arithmetic, body(): half.astype(jnp.float32)  16.4 us
  transfers between devices with their start and end apart: 6, of which 6 were waited for; matrix products, arithmetic and copies ran while one was open for 1% of the time, Pallas kernels for 0%

profile of v6, /device:TPU:1, one launch (start us, length us, event | category | flops | bytes accessed | tf_op | source)
XLA Modules:
  0.0 787.9 jit_solution(16434990544687238010)
XLA Ops:
  7.3 1.5 copy.121
  12.1 0.9 maximum_select_fusion
  13.0 164.5 %all-gather.5.cloned.1.call-done = bf16[1024,6156]{1,0:T(8,128)(2,1)} async-done(((bf16[32,6156]{1,0:T(8,128)(2,1)}), bf16[1024,6156]{1,0:T(8,128)(2,1)}) %all-gather.5.cloned.1.call-update) | async-done | bytes 12607504 | tf_op jit(solution)/shard_map/all_gather | solution.py:336
  179.2 0.7 constant_dynamic-update-slice_fusion.2
  180.8 58.9 %all-gather.9.cloned.1.call-done = bf16[2048,6156]{1,0:T(8,128)(2,1)} async-done(((bf16[1024,6156]{1,0:T(8,128)(2,1)}), bf16[2048,6156]{1,0:T(8,128)(2,1)}) %all-gather.9.cloned.1.call-update) | async-done | bytes 25214992 | tf_op jit(solution)/shard_map/all_gather | solution.py:337
  239.6 1.1 convert_bitcast_fusion.1
  240.9 1.0 convert_bitcast_fusion.2
  242.4 4.6 fusion.8
  248.4 3.0 convert_reduce_fusion.2
  251.5 2.1 fusion.106
  253.8 0.9 bitcast_dynamic-update-slice_fusion.7
  254.7 1.8 slice.297
  256.5 4.0 slice.296
  260.5 5.7 multiply_convert_fusion
  266.2 6.0 shard_map.254
  272.2 1.3 fusion.102
  274.1 1.0 fusion.98
  275.0 0.7 convert_element_type.200.grad_ref
  275.8 6.8 shard_map.255
  282.6 2.8 fusion.96
  285.4 5.3 multiply_reduce_fusion.1
  290.9 0.8 copy-done.9
  291.7 2.4 fusion.38
  294.3 1.2 fusion.104
  295.5 2.3 fusion.109
  297.8 2.8 convolution_convert_fusion.1
  300.6 2.8 fusion.103
  304.3 0.7 bitcast_dynamic-update-slice_fusion.5
  305.0 0.7 broadcast_dynamic-update-slice_fusion.1
  305.7 0.7 constant_dynamic-update-slice_fusion
  306.5 0.7 bitcast_dynamic-update-slice_fusion.8
  307.2 1.8 fusion.81
  308.9 1.7 fusion.80
  312.1 1.1 copy.139
  313.3 1.1 copy.138
  316.0 14.7 %convolution_convert_fusion = bf16[14,1024,1024]{2,1,0:T(8,128)(2,1)} fusion(bf16[14,128,1024]{2,1,0:T(8,128)(2,1)} %pad_dynamic-update-slice_fusion, bf16[14,128,1024]{2,1,0:T(8,128)(2,1)S(1)} %fusion.72), kind=kOutput, calls=%fused_computation.1 | convolution fusion | flops 3772776448 | bytes 36700160 | tf_op jit(solution)/shard_map/btk,btn->bkn/dot_general | solution.py:393
  330.8 44.5 %reduce-scatter.3.cloned.1.call-done = bf16[1,7,1024,1024]{3,2,1,0:T(8,128)(2,1)} async-done(((bf16[2,7,1024,1024]{3,2,1,0:T(8,128)(2,1)}), bf16[1,7,1024,1024]{3,2,1,0:T(8,128)(2,1)}) %reduce-scatter.3.cloned.1.call-update) | async-done | bytes 14680080 | tf_op jit(solution)/shard_map/reduce_scatter | solution.py:399
  375.2 16.4 %bitcast_convert_fusion = f32[7,1024,1024]{2,1,0:T(8,128)} fusion(bf16[1,7,1024,1024]{3,2,1,0:T(8,128)(2,1)} %reduce-scatter.3.cloned.1.call-done), kind=kLoop, calls=%fused_computation.2 | loop fusion | flops 7340032 | bytes 44040192 | tf_op jit(solution)/shard_map/convert_element_type | solution.py:401
  391.7 322.1 %reduce-scatter.5.cloned.1.call-done = f32[7,32,1024]{2,1,0:T(8,128)} async-done(((f32[7,1024,1024]{2,1,0:T(8,128)}), f32[7,32,1024]{2,1,0:T(8,128)}) %reduce-scatter.5.cloned.1.call-update) | async-done | bytes 917520 | tf_op jit(solution)/shard_map/reduce_scatter | solution.py:400
  714.1 43.7 %all-reduce.3.cloned.1.call-done = f32[1,7,32,1024]{3,2,1,0:T(8,128)} async-done(((f32[1,7,32,1024]{3,2,1,0:T(8,128)}), f32[1,7,32,1024]{3,2,1,0:T(8,128)}) %all-reduce.3.cloned.1.call-update) | async-done | bytes 917520 | tf_op jit(solution)/shard_map/psum | solution.py:403
  757.9 5.8 fusion.35
  763.7 8.6 %all-gather.7.cloned.1.call-done = f32[2,7,32,1024]{3,2,1,0:T(8,128)} async-done(((f32[1,7,32,1024]{3,2,1,0:T(8,128)}), f32[2,7,32,1024]{3,2,1,0:T(8,128)}) %all-gather.7.cloned.1.call-update) | async-done | bytes 1835024 | tf_op jit(solution)/shard_map/all_gather | solution.py:404
  772.3 2.3 slice_bitcast_fusion.12
  774.5 0.8 slice_reduce_fusion.2
  775.8 1.0 broadcast_in_dim_reshape.11
  778.1 0.9 copy.142
  778.9 1.4 copy.144
  780.3 0.8 maximum_bitcast_fusion.1
  (144 shorter events, 14.1 us)
Async XLA Ops:
  7.2 3.0 copy-start.26
  7.2 3.8 copy-start.19
  7.2 3.9 copy-start.20
  7.2 4.0 copy-start.21
  7.2 4.1 copy-start.22
  7.2 4.2 copy-start.23
  7.2 4.3 copy-start.24
  7.3 4.4 copy-start.25
  7.3 4.5 copy-start.14
  7.3 4.7 copy-start.18
  7.3 4.8 copy-start.17
  7.3 170.3 %all-gather.5.cloned.1.call-start = ((), (), s32[]{:S(2)}) async-start(), calls=%async_computation.2 | async-start | bytes 13246464 | tf_op jit(solution)/shard_map/all_gather | solution.py:336
  13.0 226.7 %all-gather.9.cloned.1.call-start = ((), (), s32[]{:S(2)}) async-start(), calls=%async_computation.7 | async-start | bytes 38535168 | tf_op jit(solution)/shard_map/all_gather | solution.py:337
  177.6 0.9 copy-start.1
  177.6 3.1 copy-start.3
  177.6 197.6 %reduce-scatter.3.cloned.1.call-start = ((), (), s32[]{:S(2)}) async-start(), calls=%async_computation.3 | async-start | bytes 44040192 | tf_op jit(solution)/shard_map/reduce_scatter | solution.py:399
  247.1 0.9 copy-start.12
  247.4 0.7 copy-start.13
  247.5 6.2 copy-start.4
  248.4 5.4 copy-start.5
  256.5 4.0 copy-start.7
  260.5 5.8 copy-start
  282.6 2.9 copy-start.8
  290.9 0.8 copy-start.9
  294.3 9.1 %copy-start.6 = (bf16[16,64,128]{2,1,0:T(8,128)(2,1)S(1)}, bf16[16,64,128]{2,1,0:T(8,128)(2,1)}, u32[]{:S(2)}) copy-start(bf16[16,64,128]{2,1,0:T(8,128)(2,1)} %copy-done.5) | copy-start | bytes 786436
  303.4 7.2 copy-start.2
  307.2 7.3 copy-start.16
  307.2 7.7 copy-start.10
  330.7 383.1 %reduce-scatter.5.cloned.1.call-start = ((), (), s32[]{:S(2)}) async-start(), calls=%async_computation.4 | async-start | bytes 30277632 | tf_op jit(solution)/shard_map/reduce_scatter | solution.py:400
  391.6 366.2 %copy-start.11 = (bf16[1,128,16,64]{1,3,2,0:T(8,128)(2,1)S(1)}, bf16[1,128,16,64]{1,3,2,0:T(8,128)(2,1)}, u32[]{:S(2)}) copy-start(bf16[1,128,16,64]{1,3,2,0:T(8,128)(2,1)} %get-tuple-element.132) | copy-start | bytes 786436
  391.6 366.2 %copy-start.15 = (bf16[16,64,128]{2,1,0:T(8,128)(2,1)S(1)}, bf16[16,64,128]{2,1,0:T(8,128)(2,1)}, u32[]{:S(2)}) copy-start(bf16[16,64,128]{2,1,0:T(8,128)(2,1)} %convolution_convert_fusion.1) | copy-start | bytes 786436
  391.7 366.2 %all-reduce.3.cloned.1.call-start = ((), (), s32[]{:S(2)}) async-start(), calls=%async_computation.5 | async-start | bytes 1835008 | tf_op jit(solution)/shard_map/psum | solution.py:403
  713.9 58.4 %all-gather.7.cloned.1.call-start = ((), (), s32[]{:S(2)}) async-start(), calls=%async_computation.6 | async-start | bytes 2752512 | tf_op jit(solution)/shard_map/all_gather | solution.py:404
Sparse Core Ops, SparseCore 0:
  13.1 164.4 all-gather.4
  179.2 60.3 all-gather.8
  330.8 44.3 reduce-scatter.2
  391.8 321.9 reduce-scatter.4
  716.1 41.6 all-reduce.2
  759.5 12.7 all-gather.6

commit v7 on v6

--- a/solution.py
+++ b/solution.py
@@ -400,8 +400,8 @@
     part = lax.psum_scatter(
         half.astype(jnp.float32), SHARD_AXES, scatter_dimension=1, tiled=True
     )
-    part = lax.psum(part, "xh")
-    res = lax.all_gather(part, "core", axis=0, tiled=False)
+    slots = jnp.zeros((2,) + part.shape, part.dtype)
+    res = lax.psum(lax.dynamic_update_index_in_dim(slots, part, core, 0), ("xh", "core"))
     r0, r1 = res[0], res[1]
     r_qkv = jnp.concatenate([r0[0], r0[1], r0[2]], axis=1)
     r_in = ungroup_columns(jnp.concatenate([r0[3], r0[4], r0[5], r1[1]], axis=1), 4)

time: 789 us -> 795 us (level)
  local copies, waits for them, and re-layouts: 33.9 us -> 42.3 us
    all_gather x1 -> x0, waiting for transfers between devices: 8.58 us -> none  [body(): res = lax.all_gather(part, 'core', axis=0, tiled=False)]
    unnamed x79 -> x83, local copies, waits for them, and re-layouts: 15.4 us -> 22.4 us
  transfers between devices with their start and end apart: 6 -> 5, of which waited for: 6 -> 5; matrix products, arithmetic and copies ran while one was open for 1% -> 1% of each run, Pallas kernels for 0% -> 0%
where the time goes in v7:
time: 795 us; the launch traced here: 794 us
  waiting for transfers between devices  636 us (80%)
  matrix products  50.6 us (6%)
  local copies, waits for them, and re-layouts  42.3 us (5%)
  other arithmetic  36.8 us (5%)
  between operations  15.1 us (2%)
  Pallas kernels  12.8 us (2%)
    reduce_scatter x1, waiting for transfers between devices, body(): lax.psum_scatter(half.astype(jnp.float32), SHARD_AXES, scatter_dimension=...  322 us
    all_gather x1, waiting for transfers between devices, body(): gathered = lax.all_gather(mine, SHARD_AXES, axis=0, tiled=True)  165 us
    all_gather x1, waiting for transfers between devices, body(): both = lax.all_gather(gathered, 'core', axis=0, tiled=False)  58.9 us
    psum x1, waiting for transfers between devices, body(): lax.psum(lax.dynamic_update_index_in_dim(slots, part, core, 0), ('xh', 'c...  46 us
    reduce_scatter x1, waiting for transfers between devices, body(): lax.psum_scatter(wgrads.astype(jnp.bfloat16), 'core', scatter_dimension=0...  44.5 us
    unnamed x83, local copies, waits for them, and re-layouts  22.4 us
    convert_element_type x1, other arithmetic, body(): half.astype(jnp.float32)  16.4 us
  transfers between devices with their start and end apart: 5, of which 5 were waited for; matrix products, arithmetic and copies ran while one was open for 1% of the time, Pallas kernels for 0%

profile of v7, /device:TPU:1, one launch (start us, length us, event | category | flops | bytes accessed | tf_op | source)
XLA Modules:
  0.0 793.8 jit_solution(6395155367134391830)
XLA Ops:
  7.3 1.6 copy.74
  12.2 0.9 maximum_select_fusion
  13.1 164.5 %all-gather.4.cloned.1.call-done = bf16[1024,6156]{1,0:T(8,128)(2,1)} async-done(((bf16[32,6156]{1,0:T(8,128)(2,1)}), bf16[1024,6156]{1,0:T(8,128)(2,1)}) %all-gather.4.cloned.1.call-update) | async-done | bytes 12607504 | tf_op jit(solution)/shard_map/all_gather | solution.py:336
  179.3 0.7 constant_dynamic-update-slice_fusion.2
  180.8 58.9 %all-gather.6.cloned.1.call-done = bf16[2048,6156]{1,0:T(8,128)(2,1)} async-done(((bf16[1024,6156]{1,0:T(8,128)(2,1)}), bf16[2048,6156]{1,0:T(8,128)(2,1)}) %all-gather.6.cloned.1.call-update) | async-done | bytes 25214992 | tf_op jit(solution)/shard_map/all_gather | solution.py:337
  239.7 1.1 convert_bitcast_fusion.1
  241.0 1.0 convert_bitcast_fusion.2
  242.5 4.6 fusion.8
  248.5 3.0 convert_reduce_fusion.2
  251.5 2.1 fusion.106
  253.9 0.9 bitcast_dynamic-update-slice_fusion.8
  254.8 1.8 slice.297
  256.6 4.0 slice.296
  260.6 5.7 multiply_convert_fusion
  266.3 6.0 shard_map.254
  272.3 1.3 fusion.102
  274.1 1.0 fusion.98
  275.8 6.8 shard_map.255
  282.6 2.8 fusion.96
  285.5 5.3 multiply_reduce_fusion.1
  291.0 0.8 copy-done.10
  291.8 2.4 fusion.38
  294.4 1.2 fusion.104
  295.6 2.3 fusion.109
  297.9 2.8 convolution_convert_fusion.1
  300.7 2.8 fusion.103
  307.3 1.8 fusion.81
  309.1 1.7 fusion.80
  312.4 1.1 copy.90
  314.4 1.1 copy.92
  319.8 0.8 bitcast_dynamic-update-slice_fusion.5
  322.1 0.7 bitcast_dynamic-update-slice_fusion.2
  322.8 0.8 bitcast_dynamic-update-slice_fusion.1
  325.0 0.9 fusion.72
  325.9 14.9 %convolution_convert_fusion = bf16[14,1024,1024]{2,1,0:T(8,128)(2,1)} fusion(bf16[14,128,1024]{2,1,0:T(8,128)(2,1)} %pad_dynamic-update-slice_fusion, bf16[14,128,1024]{2,1,0:T(8,128)(2,1)} %fusion.72), kind=kOutput, calls=%fused_computation.1 | convolution fusion | flops 3772776448 | bytes 36700160 | tf_op jit(solution)/shard_map/btk,btn->bkn/dot_general | solution.py:393
  340.8 44.5 %reduce-scatter.3.cloned.1.call-done = bf16[1,7,1024,1024]{3,2,1,0:T(8,128)(2,1)} async-done(((bf16[2,7,1024,1024]{3,2,1,0:T(8,128)(2,1)}), bf16[1,7,1024,1024]{3,2,1,0:T(8,128)(2,1)}) %reduce-scatter.3.cloned.1.call-update) | async-done | bytes 14680080 | tf_op jit(solution)/shard_map/reduce_scatter | solution.py:399
  385.3 16.4 %bitcast_convert_fusion = f32[7,1024,1024]{2,1,0:T(8,128)} fusion(bf16[1,7,1024,1024]{3,2,1,0:T(8,128)(2,1)} %reduce-scatter.3.cloned.1.call-done), kind=kLoop, calls=%fused_computation.2 | loop fusion | flops 7340032 | bytes 44040192 | tf_op jit(solution)/shard_map/convert_element_type | solution.py:401
  402.0 321.9 %reduce-scatter.5.cloned.1.call-done = f32[7,32,1024]{2,1,0:T(8,128)} async-done(((f32[7,1024,1024]{2,1,0:T(8,128)}), f32[7,32,1024]{2,1,0:T(8,128)}) %reduce-scatter.5.cloned.1.call-update) | async-done | bytes 917520 | tf_op jit(solution)/shard_map/reduce_scatter | solution.py:400
  724.1 1.2 bitcast_dynamic-update-slice_fusion
  725.3 1.2 copy-done
  726.6 5.8 fusion.35
  732.4 46.0 %all-reduce.3.cloned.1.call-done = f32[2,7,32,1024]{3,2,1,0:T(8,128)} async-done(((f32[2,7,32,1024]{3,2,1,0:T(8,128)}), f32[2,7,32,1024]{3,2,1,0:T(8,128)}) %all-reduce.3.cloned.1.call-update) | async-done | bytes 1835024 | tf_op jit(solution)/shard_map/psum | solution.py:404
  778.4 2.3 slice_bitcast_fusion.12
  780.7 0.8 slice_reduce_fusion.2
  782.3 0.9 copy.95
  783.1 1.4 copy.97
  785.5 1.0 broadcast_in_dim_reshape.11
  786.5 0.8 maximum_bitcast_fusion.1
  (147 shorter events, 24.7 us)
Async XLA Ops:
  7.2 2.6 copy-start.16
  7.2 2.8 copy-start.21
  7.2 2.9 copy-start.22
  7.2 3.0 copy-start.23
  7.2 3.0 copy-start.24
  7.2 3.1 copy-start.25
  7.2 3.2 copy-start.26
  7.3 3.3 copy-start.27
  7.3 4.0 copy-start.28
  7.3 4.8 copy-start.20
  7.3 4.9 copy-start.19
  7.3 170.4 %all-gather.4.cloned.1.call-start = ((), (), s32[]{:S(2)}) async-start(), calls=%async_computation.2 | async-start | bytes 13246464 | tf_op jit(solution)/shard_map/all_gather | solution.py:336
  13.1 226.7 %all-gather.6.cloned.1.call-start = ((), (), s32[]{:S(2)}) async-start(), calls=%async_computation.6 | async-start | bytes 38535168 | tf_op jit(solution)/shard_map/all_gather | solution.py:337
  177.7 0.9 copy-start.2
  177.7 3.1 copy-start.4
  177.7 207.6 %reduce-scatter.3.cloned.1.call-start = ((), (), s32[]{:S(2)}) async-start(), calls=%async_computation.3 | async-start | bytes 44040192 | tf_op jit(solution)/shard_map/reduce_scatter | solution.py:399
  247.2 0.9 copy-start.14
  247.5 0.7 copy-start.15
  247.5 6.2 copy-start.5
  248.5 5.4 copy-start.6
  256.6 4.0 copy-start.8
  260.6 5.7 copy-start.1
  282.6 2.9 copy-start.9
  291.0 0.8 copy-start.10
  295.6 10.1 %copy-start.7 = (bf16[16,64,128]{2,1,0:T(8,128)(2,1)S(1)}, bf16[16,64,128]{2,1,0:T(8,128)(2,1)}, u32[]{:S(2)}) copy-start(bf16[16,64,128]{2,1,0:T(8,128)(2,1)} %copy-done.6) | copy-start | bytes 786436
  303.5 7.2 copy-start.3
  307.3 6.9 copy-start.17
  307.3 12.5 %copy-start.11 = (f32[128,1024]{1,0:T(8,128)S(1)}, f32[128,1024]{1,0:T(8,128)}, u32[]{:S(2)}) copy-start(f32[128,1024]{1,0:T(8,128)} %copy-done.10) | copy-start | bytes 1572868
  340.8 383.1 %reduce-scatter.5.cloned.1.call-start = ((), (), s32[]{:S(2)}) async-start(), calls=%async_computation.4 | async-start | bytes 30277632 | tf_op jit(solution)/shard_map/reduce_scatter | solution.py:400
  401.7 324.9 %copy-start.12 = (f32[128,1024]{1,0:T(8,128)S(1)}, f32[128,1024]{1,0:T(8,128)}, u32[]{:S(2)}) copy-start(f32[128,1024]{1,0:T(8,128)} %copy-done.10) | copy-start | bytes 1572868
  401.7 324.9 %copy-start.13 = (bf16[1,128,16,64]{1,3,2,0:T(8,128)(2,1)S(1)}, bf16[1,128,16,64]{1,3,2,0:T(8,128)(2,1)}, u32[]{:S(2)}) copy-start(bf16[1,128,16,64]{1,3,2,0:T(8,128)(2,1)} %get-tuple-element.104) | copy-start | bytes 786436
  401.7 324.9 %copy-start.18 = (bf16[1,128,16,64]{1,3,2,0:T(8,128)(2,1)S(1)}, bf16[1,128,16,64]{1,3,2,0:T(8,128)(2,1)}, u32[]{:S(2)}) copy-start(bf16[1,128,16,64]{1,3,2,0:T(8,128)(2,1)} %get-tuple-element.102) | copy-start | bytes 786436
  401.7 376.7 %all-reduce.3.cloned.1.call-start = ((), (), s32[]{:S(2)}) async-start(), calls=%async_computation.5 | async-start | bytes 3670016 | tf_op jit(solution)/shard_map/psum | solution.py:404
  725.3 1.2 copy-start
Sparse Core Ops, SparseCore 0:
  13.2 164.4 all-gather.3
  179.3 60.3 all-gather.5
  340.9 44.3 reduce-scatter.2
  401.8 321.9 reduce-scatter.4
  726.7 51.6 all-reduce.2

commit v8 on v6

--- a/solution.py
+++ b/solution.py
@@ -386,16 +386,22 @@
     rows_used = lax.broadcasted_iota(jnp.int32, (tokens, model_width), 0) < 3 * n_small
     enc_right = (picks & rows_used).astype(jnp.bfloat16)
     zero = jnp.zeros((tokens, model_width), jnp.bfloat16)
-    lefts = [g_qkv[0]] * 3 + [g_in[0]] * 3 + [zero]
-    lefts += [g_att[0], g_in[0]] + [col(g_out[0], j) for j in range(4)] + [enc_left]
-    rights = [col(g_qkv[1], c) for c in range(3)] + [col(g_in[1], c) for c in range(3)] + [zero]
-    rights += [g_att[1], col(g_in[1], 3)] + [g_out[1]] * 4 + [enc_right]
+    lefts = [g_qkv[0]] * 3 + [g_in[0]] * 3
+    lefts += [g_att[0], g_in[0]] + [col(g_out[0], j) for j in range(4)]
+    rights = [col(g_qkv[1], c) for c in range(3)] + [col(g_in[1], c) for c in range(3)]
+    rights += [g_att[1], col(g_in[1], 3)] + [g_out[1]] * 4
+    narrow = model_width // 4
+    split_left = [a for a in lefts for _ in range(4)]
+    split_right = [b[:, q * narrow : (q + 1) * narrow] for b in rights for q in range(4)]
+    at = len(split_left) // 2
+    split_left = split_left[:at] + [zero] + split_left[at:] + [enc_left]
+    split_right = split_right[:at] + [zero[:, :narrow]] + split_right[at:] + [enc_right[:, :narrow]]
     wgrads = jnp.einsum(
         "btk,btn->bkn",
-        jnp.stack(lefts),
-        jnp.stack(rights),
+        jnp.stack(split_left),
+        jnp.stack(split_right),
         preferred_element_type=jnp.float32,
-    ).reshape(2, len(lefts) // 2, model_width, model_width)
+    ).reshape(2, len(split_left) // 2, model_width, narrow)
     half = lax.psum_scatter(wgrads.astype(jnp.bfloat16), "core", scatter_dimension=0, tiled=False)
     part = lax.psum_scatter(
         half.astype(jnp.float32), SHARD_AXES, scatter_dimension=1, tiled=True
@@ -403,11 +409,12 @@
     part = lax.psum(part, "xh")
     res = lax.all_gather(part, "core", axis=0, tiled=False)
     r0, r1 = res[0], res[1]
-    r_qkv = jnp.concatenate([r0[0], r0[1], r0[2]], axis=1)
-    r_in = ungroup_columns(jnp.concatenate([r0[3], r0[4], r0[5], r1[1]], axis=1), 4)
-    r_att = r1[0]
-    r_out = jnp.stack([r1[2], r1[3], r1[4], r1[5]], axis=1)
-    r_small = r1[6][:, :n_small]
+    joined = lambda r: r.transpose(1, 0, 2).reshape(r.shape[1], -1)
+    r_qkv = joined(r0[0:12])
+    r_in = ungroup_columns(jnp.concatenate([joined(r0[12:24]), joined(r1[4:8])], axis=1), 4)
+    r_att = joined(r1[0:4])
+    r_out = jnp.stack([joined(r1[8 + 4 * j : 12 + 4 * j]) for j in range(4)], axis=1)
+    r_small = r1[24][:, :n_small]
     grad_inputs = upstream.reshape(inputs.shape)
     return (
         outputs,

time: 789 us -> 938 us (1.19)
  local copies, waits for them, and re-layouts: 33.9 us -> 133 us
  waiting for transfers between devices: 642 us -> 686 us
    unnamed x79 -> x179, local copies, waits for them, and re-layouts: 15.4 us -> 82.8 us
    reduce_scatter x1, waiting for transfers between devices: 322 us -> 366 us  [body(): lax.psum_scatter(half.astype(jnp.float32), SHARD_AXES, scatter_dimension=...]
    convert_element_type x0 -> x1, local copies, waits for them, and re-layouts: none -> 25 us  [body(): wgrads.astype(jnp.bfloat16)]
  transfers between devices with their start and end apart: 6 -> 6, of which waited for: 6 -> 6; matrix products, arithmetic and copies ran while one was open for 1% -> 2% of each run, Pallas kernels for 0% -> 0%
where the time goes in v8:
time: 938 us; the launch traced here: 935 us
  waiting for transfers between devices  686 us (73%)
  local copies, waits for them, and re-layouts  133 us (14%)
  matrix products  53.2 us (6%)
  other arithmetic  34.6 us (4%)
  between operations  15.8 us (2%)
  Pallas kernels  12.8 us (1%)
    reduce_scatter x1, waiting for transfers between devices, body(): lax.psum_scatter(half.astype(jnp.float32), SHARD_AXES, scatter_dimension=...  366 us
    all_gather x1, waiting for transfers between devices, body(): gathered = lax.all_gather(mine, SHARD_AXES, axis=0, tiled=True)  165 us
    unnamed x179, local copies, waits for them, and re-layouts  82.8 us
    all_gather x1, waiting for transfers between devices, body(): both = lax.all_gather(gathered, 'core', axis=0, tiled=False)  52.3 us
    reduce_scatter x1, waiting for transfers between devices, body(): lax.psum_scatter(wgrads.astype(jnp.bfloat16), 'core', scatter_dimension=0...  49.2 us
    psum x1, waiting for transfers between devices, body(): part = lax.psum(part, 'xh')  46.8 us
    convert_element_type x1, local copies, waits for them, and re-layouts, body(): wgrads.astype(jnp.bfloat16)  25 us
    dot_general x1, matrix products, body(): jnp.einsum('btk,btn->bkn', jnp.stack(split_left), jnp.stack(split_right),...  18.9 us
  transfers between devices with their start and end apart: 6, of which 6 were waited for; matrix products, arithmetic and copies ran while one was open for 2% of the time, Pallas kernels for 0%

profile of v8, /device:TPU:1, one launch (start us, length us, event | category | flops | bytes accessed | tf_op | source)
XLA Modules:
  0.0 935.3 jit_solution(15586754231309302393)
XLA Ops:
  7.3 1.6 copy.226
  13.1 164.5 %all-gather.5.cloned.1.call-done = bf16[1024,6156]{1,0:T(8,128)(2,1)} async-done(((bf16[32,6156]{1,0:T(8,128)(2,1)}), bf16[1024,6156]{1,0:T(8,128)(2,1)}) %all-gather.5.cloned.1.call-update) | async-done | bytes 12607504 | tf_op jit(solution)/shard_map/all_gather | solution.py:336
  187.4 52.3 %all-gather.9.cloned.1.call-done = bf16[2048,6156]{1,0:T(8,128)(2,1)} async-done(((bf16[1024,6156]{1,0:T(8,128)(2,1)}), bf16[2048,6156]{1,0:T(8,128)(2,1)}) %all-gather.9.cloned.1.call-update) | async-done | bytes 25214992 | tf_op jit(solution)/shard_map/all_gather | solution.py:337
  239.7 1.1 convert_bitcast_fusion.1
  241.0 1.0 convert_bitcast_fusion.2
  242.5 4.6 fusion.8
  248.5 3.1 convert_reduce_fusion.2
  251.6 2.1 fusion.100
  253.9 0.9 bitcast_dynamic-update-slice_fusion.14
  254.8 1.8 slice.483
  256.6 4.0 slice.482
  260.6 5.7 multiply_convert_fusion
  266.3 6.0 shard_map.254
  272.3 1.3 fusion.93
  274.1 1.0 fusion.89
  275.8 6.8 shard_map.255
  282.7 2.8 fusion.87
  285.5 5.7 multiply_reduce_fusion.1
  293.0 2.5 fusion.38
  295.6 1.2 fusion.95
  296.8 1.3 fusion.103
  298.2 2.7 convolution_convert_fusion.1
  300.9 2.1 fusion.94
  331.9 1.6 copy.279
  333.5 1.6 copy.280
  335.0 1.6 fusion.97
  336.6 1.6 copy.281
  338.2 1.6 copy.282
  339.8 1.6 copy.283
  341.3 1.6 copy.284
  342.9 1.6 fusion.96
  344.5 1.6 copy.285
  346.1 1.6 copy.286
  347.6 1.6 copy.287
  349.2 1.6 copy.288
  376.6 18.9 %convolution_convert_fusion = bf16[50,1024,256]{2,1,0:T(8,128)(2,1)} fusion(bf16[50,128,1024]{2,1,0:T(8,128)(2,1)} %pad_dynamic-update-slice_fusion, bf16[50,128,256]{2,1,0:T(8,128)(2,1)S(1)} %constant_dynamic-update-slice_fusion.33), kind=kOutput, calls=%fused_computation.1 | convolution fusion | flops 3368550400 | bytes 42598400 | tf_op jit(solution)/shard_map/btk,btn->bkn/dot_general | solution.py:399
  395.5 25.0 %copy.258 = bf16[2,25,1024,256]{3,1,2,0:T(8,128)(2,1)} copy(bf16[2,25,1024,256]{3,2,1,0:T(8,128)(2,1)} %bitcast.382) | data formatting | bytes 52428800 | tf_op jit(solution)/shard_map/convert_element_type | solution.py:405
  420.6 49.2 %reduce-scatter.3.cloned.1.call-done = bf16[1,25,1024,256]{3,1,2,0:T(8,128)(2,1)} async-done(((bf16[2,25,1024,256]{3,1,2,0:T(8,128)(2,1)}), bf16[1,25,1024,256]{3,1,2,0:T(8,128)(2,1)}) %reduce-scatter.3.cloned.1.call-update) | async-done | bytes 13107216 | tf_op jit(solution)/shard_map/reduce_scatter | solution.py:405
  469.9 18.6 %bitcast_convert_fusion = f32[25,1024,256]{2,0,1:T(8,128)} fusion(bf16[1,25,1024,256]{3,1,2,0:T(8,128)(2,1)} %reduce-scatter.3.cloned.1.call-done), kind=kLoop, calls=%fused_computation.2 | loop fusion | flops 6553600 | bytes 39321600 | tf_op jit(solution)/shard_map/convert_element_type | solution.py:407
  488.6 365.8 %reduce-scatter.5.cloned.1.call-done = f32[25,32,256]{2,0,1:T(8,128)} async-done(((f32[25,1024,256]{2,0,1:T(8,128)}), f32[25,32,256]{2,0,1:T(8,128)}) %reduce-scatter.5.cloned.1.call-update) | async-done | bytes 819216 | tf_op jit(solution)/shard_map/reduce_scatter | solution.py:406
  854.5 46.8 %all-reduce.3.cloned.1.call-done = f32[1,25,32,256]{3,1,2,0:T(8,128)} async-done(((f32[1,25,32,256]{3,1,2,0:T(8,128)}), f32[1,25,32,256]{3,1,2,0:T(8,128)}) %all-reduce.3.cloned.1.call-update) | async-done | bytes 819216 | tf_op jit(solution)/shard_map/psum | solution.py:409
  901.3 2.6 copy.259
  903.9 5.8 fusion.35
  909.7 6.8 all-gather.7.cloned.1.call-done
  918.2 1.2 slice_bitcast_fusion
  921.0 1.3 slice_bitcast_fusion.10
  924.5 1.4 copy.271
  927.5 1.0 broadcast_in_dim_reshape.19
  (257 shorter events, 80.2 us)
Async XLA Ops:
  7.2 2.6 copy-start.15
  7.2 2.8 copy-start.24
  7.2 2.9 copy-start.25
  7.2 3.0 copy-start.26
  7.2 3.0 copy-start.27
  7.2 3.1 copy-start.28
  7.2 3.2 copy-start.29
  7.3 3.3 copy-start.30
  7.3 4.0 copy-start.31
  7.3 4.8 copy-start.23
  7.3 4.9 copy-start.19
  7.3 170.4 %all-gather.5.cloned.1.call-start = ((), (), s32[]{:S(2)}) async-start(), calls=%async_computation.2 | async-start | bytes 13246464 | tf_op jit(solution)/shard_map/all_gather | solution.py:336
  13.1 226.7 %all-gather.9.cloned.1.call-start = ((), (), s32[]{:S(2)}) async-start(), calls=%async_computation.7 | async-start | bytes 38535168 | tf_op jit(solution)/shard_map/all_gather | solution.py:337
  177.7 0.9 copy-start
  177.7 9.6 %copy-start.5 = (bf16[1,128,1024]{2,1,0:T(8,128)(2,1)S(1)}, bf16[1,128,1024]{2,1,0:T(8,128)(2,1)}, u32[]{:S(2)}) copy-start(bf16[1,128,1024]{2,1,0:T(8,128)(2,1)} %param.19) | copy-start | bytes 786436
  177.7 292.2 %reduce-scatter.3.cloned.1.call-start = ((), (), s32[]{:S(2)}) async-start(), calls=%async_computation.3 | async-start | bytes 50331648 | tf_op jit(solution)/shard_map/reduce_scatter | solution.py:405
  247.5 0.7 copy-start.13
  256.6 4.0 copy-start.6
  260.6 5.7 copy-start.3
  282.7 2.9 copy-start.7
  285.5 5.7 copy-start.4
  291.5 0.8 copy-start.8
  292.3 0.7 copy-start.10
  293.0 5.2 copy-start.14
  303.0 27.4 %copy-start.17 = (bf16[1,128,16,64]{1,3,2,0:T(8,128)(2,1)}, bf16[1,128,16,64]{1,3,2,0:T(8,128)(2,1)S(1)}, u32[]{:S(2)}) copy-start(bf16[1,128,16,64]{1,3,2,0:T(8,128)(2,1)S(1)} %get-tuple-element.139) | copy-start | bytes 786436
  308.9 8.9 copy-start.1
  331.9 43.5 %copy-start.2 = (bf16[128,1024]{1,0:T(8,128)(2,1)S(1)}, bf16[128,1024]{1,0:T(8,128)(2,1)}, u32[]{:S(2)}) copy-start(bf16[128,1024]{1,0:T(8,128)(2,1)} %convert_element_type.191.grad_ref) | copy-start | bytes 786436
  350.8 21.2 %copy-start.11 = (bf16[128,1024]{1,0:T(8,128)(2,1)S(1)}, bf16[128,1024]{1,0:T(8,128)(2,1)}, u32[]{:S(2)}) copy-start(bf16[128,1024]{1,0:T(8,128)(2,1)} %copy-done.10) | copy-start | bytes 786436
  350.8 24.9 %copy-start.20 = (bf16[12,1024]{1,0:T(8,128)(2,1)S(1)}, bf16[12,1024]{1,0:T(8,128)(2,1)}, u32[]{:S(2)}) copy-start(bf16[12,1024]{1,0:T(8,128)(2,1)} %get-tuple-element.154) | copy-start | bytes 73732
  350.8 24.9 %copy-start.21 = (bf16[12,1024]{1,0:T(8,128)(2,1)S(1)}, bf16[12,1024]{1,0:T(8,128)(2,1)}, u32[]{:S(2)}) copy-start(bf16[12,1024]{1,0:T(8,128)(2,1)} %get-tuple-element.155) | copy-start | bytes 73732
  350.8 24.9 %copy-start.22 = (bf16[12,1024]{1,0:T(8,128)(2,1)S(1)}, bf16[12,1024]{1,0:T(8,128)(2,1)}, u32[]{:S(2)}) copy-start(bf16[12,1024]{1,0:T(8,128)(2,1)} %get-tuple-element.156) | copy-start | bytes 73732
  420.6 433.8 %reduce-scatter.5.cloned.1.call-start = ((), (), s32[]{:S(2)}) async-start(), calls=%async_computation.4 | async-start | bytes 34603008 | tf_op jit(solution)/shard_map/reduce_scatter | solution.py:406
  488.5 415.4 %copy-start.9 = (f32[128,1024]{1,0:T(8,128)S(1)}, f32[128,1024]{1,0:T(8,128)}, u32[]{:S(2)}) copy-start(f32[128,1024]{1,0:T(8,128)} %copy-done.8) | copy-start | bytes 1572868
  488.5 415.4 %copy-start.12 = (bf16[1,128,16,64]{1,3,2,0:T(8,128)(2,1)S(1)}, bf16[1,128,16,64]{1,3,2,0:T(8,128)(2,1)}, u32[]{:S(2)}) copy-start(bf16[1,128,16,64]{1,3,2,0:T(8,128)(2,1)} %get-tuple-element.141) | copy-start | bytes 786436
  488.5 415.4 %copy-start.16 = (bf16[16,64,128]{2,1,0:T(8,128)(2,1)S(1)}, bf16[16,64,128]{2,1,0:T(8,128)(2,1)}, u32[]{:S(2)}) copy-start(bf16[16,64,128]{2,1,0:T(8,128)(2,1)} %convolution_convert_fusion.1) | copy-start | bytes 786436
  488.5 415.4 %copy-start.18 = (bf16[1,128,16,64]{1,3,2,0:T(8,128)(2,1)S(1)}, bf16[1,128,16,64]{1,3,2,0:T(8,128)(2,1)}, u32[]{:S(2)}) copy-start(bf16[1,128,16,64]{1,3,2,0:T(8,128)(2,1)} %copy-done.17) | copy-start | bytes 786436
  488.6 412.7 %all-reduce.3.cloned.1.call-start = ((), (), s32[]{:S(2)}) async-start(), calls=%async_computation.5 | async-start | bytes 2097152 | tf_op jit(solution)/shard_map/psum | solution.py:409
  854.4 62.1 %all-gather.7.cloned.1.call-start = ((), (), s32[]{:S(2)}) async-start(), calls=%async_computation.6 | async-start | bytes 2457600 | tf_op jit(solution)/shard_map/all_gather | solution.py:410
Sparse Core Ops, SparseCore 0:
  13.2 164.4 all-gather.4
  179.3 60.3 all-gather.8
  420.7 49.1 reduce-scatter.2
  488.6 365.7 reduce-scatter.4
  856.7 44.5 all-reduce.2
  904.0 12.4 all-gather.6

commit v9 on v6

--- a/solution.py
+++ b/solution.py
@@ -76,6 +76,34 @@
         ),
     )(grad_bf, buffer)
 
+
+def _wgrad_kernel(left_ref, right_ref, out_ref):
+    out_ref[...] = lax.dot_general(
+        left_ref[...],
+        right_ref[...],
+        (((0,), (0,)), ((), ())),
+        preferred_element_type=jnp.float32,
+    ).astype(out_ref.dtype)
+
+
+def weight_grads(lefts, rights):
+    blocks, tokens, rows = lefts.shape
+    cols = rights.shape[2]
+    return pl.pallas_call(
+        _wgrad_kernel,
+        grid=(blocks,),
+        in_specs=[
+            pl.BlockSpec((None, tokens, rows), lambda b: (b, 0, 0)),
+            pl.BlockSpec((None, tokens, cols), lambda b: (b, 0, 0)),
+        ],
+        out_specs=pl.BlockSpec((None, rows, cols), lambda b: (b, 0, 0)),
+        out_shape=jax.ShapeDtypeStruct((blocks, rows, cols), jnp.bfloat16),
+        cost_estimate=pl.CostEstimate(
+            flops=2 * blocks * tokens * rows * cols,
+            bytes_accessed=2 * blocks * (tokens * rows + tokens * cols + rows * cols),
+            transcendentals=0,
+        ),
+    )(lefts, rights)
 
 def group_columns(x, groups):
     tokens = x.shape[0]
@@ -390,13 +418,10 @@
     lefts += [g_att[0], g_in[0]] + [col(g_out[0], j) for j in range(4)] + [enc_left]
     rights = [col(g_qkv[1], c) for c in range(3)] + [col(g_in[1], c) for c in range(3)] + [zero]
     rights += [g_att[1], col(g_in[1], 3)] + [g_out[1]] * 4 + [enc_right]
-    wgrads = jnp.einsum(
-        "btk,btn->bkn",
-        jnp.stack(lefts),
-        jnp.stack(rights),
-        preferred_element_type=jnp.float32,
-    ).reshape(2, len(lefts) // 2, model_width, model_width)
-    half = lax.psum_scatter(wgrads.astype(jnp.bfloat16), "core", scatter_dimension=0, tiled=False)
+    wgrads = weight_grads(jnp.stack(lefts), jnp.stack(rights)).reshape(
+        2, len(lefts) // 2, model_width, model_width
+    )
+    half = lax.psum_scatter(wgrads, "core", scatter_dimension=0, tiled=False)
     part = lax.psum_scatter(
         half.astype(jnp.float32), SHARD_AXES, scatter_dimension=1, tiled=True
     )

time: 789 us -> 802 us (1.016)
  Pallas kernels: 12.8 us -> 30.7 us
  matrix products: 50.4 us -> 35.7 us
    pallas_call x0 -> x1, Pallas kernels: none -> 17.9 us  [weight_grads(): pl.pallas_call(_wgrad_kernel, grid=(blocks,), in_specs=[pl.BlockSpec((Non...]
    dot_general x1 -> x0, matrix products: 14.7 us -> none  [body(): jnp.einsum('btk,btn->bkn', jnp.stack(lefts), jnp.stack(rights), preferred...]
where the time goes in v9:
time: 802 us; the launch traced here: 801 us
  waiting for transfers between devices  642 us (80%)
  local copies, waits for them, and re-layouts  39.5 us (5%)
  other arithmetic  36.8 us (5%)
  matrix products  35.7 us (4%)
  Pallas kernels  30.7 us (4%)
  between operations  15.4 us (2%)
    reduce_scatter x1, waiting for transfers between devices, body(): lax.psum_scatter(half.astype(jnp.float32), SHARD_AXES, scatter_dimension=...  322 us
    all_gather x1, waiting for transfers between devices, body(): gathered = lax.all_gather(mine, SHARD_AXES, axis=0, tiled=True)  165 us
    all_gather x1, waiting for transfers between devices, body(): both = lax.all_gather(gathered, 'core', axis=0, tiled=False)  58.9 us
    reduce_scatter x1, waiting for transfers between devices, body(): half = lax.psum_scatter(wgrads, 'core', scatter_dimension=0, tiled=False)  44.5 us
    psum x1, waiting for transfers between devices, body(): part = lax.psum(part, 'xh')  43.7 us
    unnamed x79, local copies, waits for them, and re-layouts  21.1 us
    pallas_call x1, Pallas kernels, weight_grads(): pl.pallas_call(_wgrad_kernel, grid=(blocks,), in_specs=[pl.BlockSpec((Non...  17.9 us
    convert_element_type x1, other arithmetic, body(): half.astype(jnp.float32)  16.4 us
  transfers between devices with their start and end apart: 6, of which 6 were waited for; matrix products, arithmetic and copies ran while one was open for 1% of the time, Pallas kernels for 0%

profile of v9, /device:TPU:1, one launch (start us, length us, event | category | flops | bytes accessed | tf_op | source)
XLA Modules:
  0.0 800.9 jit_solution(12716118611087180290)
XLA Ops:
  7.3 1.5 copy.117
  12.1 0.9 maximum_select_fusion
  13.0 164.5 %all-gather.5.cloned.1.call-done = bf16[1024,6156]{1,0:T(8,128)(2,1)} async-done(((bf16[32,6156]{1,0:T(8,128)(2,1)}), bf16[1024,6156]{1,0:T(8,128)(2,1)}) %all-gather.5.cloned.1.call-update) | async-done | bytes 12607504 | tf_op jit(solution)/shard_map/all_gather | solution.py:364
  179.2 0.7 constant_dynamic-update-slice_fusion.2
  180.8 58.9 %all-gather.9.cloned.1.call-done = bf16[2048,6156]{1,0:T(8,128)(2,1)} async-done(((bf16[1024,6156]{1,0:T(8,128)(2,1)}), bf16[2048,6156]{1,0:T(8,128)(2,1)}) %all-gather.9.cloned.1.call-update) | async-done | bytes 25214992 | tf_op jit(solution)/shard_map/all_gather | solution.py:365
  239.6 1.1 convert_bitcast_fusion.1
  240.9 1.0 convert_bitcast_fusion.2
  242.4 4.6 fusion.8
  248.4 3.0 convert_reduce_fusion.2
  251.5 2.1 fusion.106
  253.8 0.9 bitcast_dynamic-update-slice_fusion.7
  254.7 1.8 slice.297
  256.5 4.0 slice.296
  260.5 5.7 multiply_convert_fusion
  266.2 6.0 shard_map.254
  272.2 1.3 fusion.102
  274.1 1.0 fusion.98
  275.8 6.8 shard_map.255
  282.6 2.8 fusion.96
  285.4 5.3 multiply_reduce_fusion.1
  290.9 0.8 copy-done.9
  291.7 2.4 fusion.38
  294.3 1.2 fusion.104
  295.5 2.3 fusion.109
  297.8 2.8 convolution_convert_fusion
  300.6 2.8 fusion.103
  305.7 0.7 constant_dynamic-update-slice_fusion
  307.2 1.8 fusion.81
  308.9 1.7 fusion.80
  312.1 1.1 copy.135
  313.3 1.1 copy.134
  319.7 0.8 bitcast_dynamic-update-slice_fusion.4
  322.0 0.7 bitcast_dynamic-update-slice_fusion.1
  322.7 0.8 bitcast_dynamic-update-slice_fusion
  324.9 0.9 fusion.72.right_ref
  325.8 17.9 %shard_map.256 = bf16[14,1024,1024]{2,1,0:T(8,128)(2,1)} custom-call(bf16[14,128,1024]{2,1,0:T(8,128)(2,1)} %pad_dynamic-update-slice_fusion.left_ref, bf16[14,128,1024]{2,1,0:T(8,128)(2,1)} %fusion.72.right_ref), custom_call_target="tpu_custom_call" | custom-call | flops 3758096384 | bytes 36700160 | tf_op jit(solution)/shard_map/pallas_call | solution.py:92
  343.8 44.5 %reduce-scatter.3.cloned.1.call-done = bf16[1,7,1024,1024]{3,2,1,0:T(8,128)(2,1)} async-done(((bf16[2,7,1024,1024]{3,2,1,0:T(8,128)(2,1)}), bf16[1,7,1024,1024]{3,2,1,0:T(8,128)(2,1)}) %reduce-scatter.3.cloned.1.call-update) | async-done | bytes 14680080 | tf_op jit(solution)/shard_map/reduce_scatter | solution.py:424
  388.2 16.4 %bitcast_convert_fusion = f32[7,1024,1024]{2,1,0:T(8,128)} fusion(bf16[1,7,1024,1024]{3,2,1,0:T(8,128)(2,1)} %reduce-scatter.3.cloned.1.call-done), kind=kLoop, calls=%fused_computation.1 | loop fusion | flops 7340032 | bytes 44040192 | tf_op jit(solution)/shard_map/convert_element_type | solution.py:426
  404.7 322.1 %reduce-scatter.5.cloned.1.call-done = f32[7,32,1024]{2,1,0:T(8,128)} async-done(((f32[7,1024,1024]{2,1,0:T(8,128)}), f32[7,32,1024]{2,1,0:T(8,128)}) %reduce-scatter.5.cloned.1.call-update) | async-done | bytes 917520 | tf_op jit(solution)/shard_map/reduce_scatter | solution.py:425
  727.1 43.7 %all-reduce.3.cloned.1.call-done = f32[1,7,32,1024]{3,2,1,0:T(8,128)} async-done(((f32[1,7,32,1024]{3,2,1,0:T(8,128)}), f32[1,7,32,1024]{3,2,1,0:T(8,128)}) %all-reduce.3.cloned.1.call-update) | async-done | bytes 917520 | tf_op jit(solution)/shard_map/psum | solution.py:428
  770.9 5.8 fusion.35
  776.7 8.6 %all-gather.7.cloned.1.call-done = f32[2,7,32,1024]{3,2,1,0:T(8,128)} async-done(((f32[1,7,32,1024]{3,2,1,0:T(8,128)}), f32[2,7,32,1024]{3,2,1,0:T(8,128)}) %all-gather.7.cloned.1.call-update) | async-done | bytes 1835024 | tf_op jit(solution)/shard_map/all_gather | solution.py:429
  785.3 2.3 slice_bitcast_fusion.12
  787.5 0.8 slice_reduce_fusion.2
  788.8 1.0 broadcast_in_dim_reshape.11
  791.1 0.9 copy.137
  791.9 1.4 copy.139
  793.3 0.8 maximum_bitcast_fusion.1
  (144 shorter events, 23.8 us)
Async XLA Ops:
  7.2 3.0 copy-start.26
  7.2 3.8 copy-start.19
  7.2 3.9 copy-start.20
  7.2 4.0 copy-start.21
  7.2 4.1 copy-start.22
  7.2 4.2 copy-start.23
  7.2 4.3 copy-start.24
  7.3 4.4 copy-start.25
  7.3 4.5 copy-start.14
  7.3 4.7 copy-start.18
  7.3 4.8 copy-start.17
  7.3 170.3 %all-gather.5.cloned.1.call-start = ((), (), s32[]{:S(2)}) async-start(), calls=%async_computation.2 | async-start | bytes 13246464 | tf_op jit(solution)/shard_map/all_gather | solution.py:364
  13.0 226.7 %all-gather.9.cloned.1.call-start = ((), (), s32[]{:S(2)}) async-start(), calls=%async_computation.7 | async-start | bytes 38535168 | tf_op jit(solution)/shard_map/all_gather | solution.py:365
  177.6 0.9 copy-start.1
  177.6 3.1 copy-start.3
  177.6 210.6 %reduce-scatter.3.cloned.1.call-start = ((), (), s32[]{:S(2)}) async-start(), calls=%async_computation.3 | async-start | bytes 44040192 | tf_op jit(solution)/shard_map/reduce_scatter | solution.py:424
  247.1 0.9 copy-start.12
  247.4 0.7 copy-start.13
  247.5 6.2 copy-start.4
  248.4 5.4 copy-start.5
  256.5 4.0 copy-start.7
  260.5 5.8 copy-start
  282.6 2.9 copy-start.8
  290.9 0.8 copy-start.9
  294.3 9.1 %copy-start.6 = (bf16[16,64,128]{2,1,0:T(8,128)(2,1)S(1)}, bf16[16,64,128]{2,1,0:T(8,128)(2,1)}, u32[]{:S(2)}) copy-start(bf16[16,64,128]{2,1,0:T(8,128)(2,1)} %copy-done.5) | copy-start | bytes 786436
  303.4 7.2 copy-start.2
  307.2 7.3 copy-start.16
  307.2 12.5 %copy-start.10 = (f32[128,1024]{1,0:T(8,128)S(1)}, f32[128,1024]{1,0:T(8,128)}, u32[]{:S(2)}) copy-start(f32[128,1024]{1,0:T(8,128)} %copy-done.9) | copy-start | bytes 1572868
  343.7 383.1 %reduce-scatter.5.cloned.1.call-start = ((), (), s32[]{:S(2)}) async-start(), calls=%async_computation.4 | async-start | bytes 30277632 | tf_op jit(solution)/shard_map/reduce_scatter | solution.py:425
  404.6 366.2 %copy-start.11 = (bf16[1,128,16,64]{1,3,2,0:T(8,128)(2,1)S(1)}, bf16[1,128,16,64]{1,3,2,0:T(8,128)(2,1)}, u32[]{:S(2)}) copy-start(bf16[1,128,16,64]{1,3,2,0:T(8,128)(2,1)} %get-tuple-element.132) | copy-start | bytes 786436
  404.6 366.2 %copy-start.15 = (bf16[16,64,128]{2,1,0:T(8,128)(2,1)S(1)}, bf16[16,64,128]{2,1,0:T(8,128)(2,1)}, u32[]{:S(2)}) copy-start(bf16[16,64,128]{2,1,0:T(8,128)(2,1)} %convolution_convert_fusion) | copy-start | bytes 786436
  404.7 366.2 %all-reduce.3.cloned.1.call-start = ((), (), s32[]{:S(2)}) async-start(), calls=%async_computation.5 | async-start | bytes 1835008 | tf_op jit(solution)/shard_map/psum | solution.py:428
  726.8 58.4 %all-gather.7.cloned.1.call-start = ((), (), s32[]{:S(2)}) async-start(), calls=%async_computation.6 | async-start | bytes 2752512 | tf_op jit(solution)/shard_map/all_gather | solution.py:429
Sparse Core Ops, SparseCore 0:
  13.1 164.4 all-gather.4
  179.2 60.3 all-gather.8
  343.8 44.3 reduce-scatter.2
  404.8 321.9 reduce-scatter.4
  729.1 41.6 all-reduce.2
  772.5 12.7 all-gather.6

commit v10 on v5

--- a/solution.py
+++ b/solution.py
@@ -390,13 +390,19 @@
     lefts += [g_att[0], g_in[0]] + [col(g_out[0], j) for j in range(4)] + [enc_left]
     rights = [col(g_qkv[1], c) for c in range(3)] + [col(g_in[1], c) for c in range(3)] + [zero]
     rights += [g_att[1], col(g_in[1], 3)] + [g_out[1]] * 4 + [enc_right]
-    wgrads = jnp.einsum(
-        "btk,btn->bkn",
-        jnp.stack(lefts),
-        jnp.stack(rights),
-        preferred_element_type=jnp.float32,
-    ).reshape(2, len(lefts) // 2, model_width, model_width)
-    half = lax.psum_scatter(wgrads, "core", scatter_dimension=0, tiled=False)
+    per_half = len(lefts) // 2
+    stacked_left = jnp.stack(lefts).reshape(2, per_half, tokens, model_width)
+    stacked_right = jnp.stack(rights).reshape(2, per_half, tokens, model_width)
+    mine_first = core == 0
+
+    def products(pick_first):
+        left = jnp.where(pick_first, stacked_left[0], stacked_left[1])
+        right = jnp.where(pick_first, stacked_right[0], stacked_right[1])
+        return jnp.einsum("btk,btn->bkn", left, right, preferred_element_type=jnp.float32)
+
+    kept = products(mine_first)
+    sent = products(jnp.logical_not(mine_first)).astype(jnp.bfloat16)
+    half = kept + lax.ppermute(sent, "core", perm=[(0, 1), (1, 0)]).astype(jnp.float32)
     part = lax.psum_scatter(half, SHARD_AXES, scatter_dimension=1, tiled=True)
     part = lax.psum(part, "xh")
     res = lax.all_gather(part, "core", axis=0, tiled=False)

time: 815 us -> 773 us (0.948)
  waiting for transfers between devices: 677 us -> 621 us
    reduce_scatter x1 -> x0, waiting for transfers between devices: 77 us -> none  [body(): half = lax.psum_scatter(wgrads, 'core', scatter_dimension=0, tiled=False)]
    ppermute x0 -> x1, waiting for transfers between devices: none -> 22.5 us  [body(): lax.ppermute(sent, 'core', perm=[(0, 1), (1, 0)]).astype(jnp.float32)]
    dot_general x1 -> x2, matrix products: 22.5 us -> 30.7 us  [products(): jnp.einsum('btk,btn->bkn', left, right, preferred_element_type=jnp.float32)]
    unnamed x79 -> x83, local copies, waits for them, and re-layouts: 15.5 us -> 17.4 us
where the time goes in v10:
time: 773 us; the launch traced here: 772 us
  waiting for transfers between devices  621 us (80%)
  matrix products  65.4 us (8%)
  local copies, waits for them, and re-layouts  39.8 us (5%)
  other arithmetic  17.9 us (2%)
  between operations  15.2 us (2%)
  Pallas kernels  12.8 us (2%)
    reduce_scatter x1, waiting for transfers between devices, body(): part = lax.psum_scatter(half, SHARD_AXES, scatter_dimension=1, tiled=True)  323 us
    all_gather x1, waiting for transfers between devices, body(): gathered = lax.all_gather(mine, SHARD_AXES, axis=0, tiled=True)  165 us
    all_gather x1, waiting for transfers between devices, body(): both = lax.all_gather(gathered, 'core', axis=0, tiled=False)  58.9 us
    psum x1, waiting for transfers between devices, body(): part = lax.psum(part, 'xh')  43.9 us
    dot_general x2, matrix products, products(): jnp.einsum('btk,btn->bkn', left, right, preferred_element_type=jnp.float32)  30.7 us
    ppermute x1, waiting for transfers between devices, body(): lax.ppermute(sent, 'core', perm=[(0, 1), (1, 0)]).astype(jnp.float32)  22.5 us
    unnamed x83, local copies, waits for them, and re-layouts  17.4 us
  transfers between devices with their start and end apart: 6, of which 6 were waited for; matrix products, arithmetic and copies ran while one was open for 1% of the time, Pallas kernels for 0%

profile of v10, /device:TPU:1, one launch (start us, length us, event | category | flops | bytes accessed | tf_op | source)
XLA Modules:
  0.0 772.3 jit_solution(16142988622222139529)
XLA Ops:
  7.3 1.5 copy.99
  12.0 0.9 maximum_select_fusion
  13.0 164.5 %all-gather.5.cloned.1.call-done = bf16[1024,6156]{1,0:T(8,128)(2,1)} async-done(((bf16[32,6156]{1,0:T(8,128)(2,1)}), bf16[1024,6156]{1,0:T(8,128)(2,1)}) %all-gather.5.cloned.1.call-update) | async-done | bytes 12607504 | tf_op jit(solution)/shard_map/all_gather | solution.py:336
  180.7 58.9 %all-gather.9.cloned.1.call-done = bf16[2048,6156]{1,0:T(8,128)(2,1)} async-done(((bf16[1024,6156]{1,0:T(8,128)(2,1)}), bf16[2048,6156]{1,0:T(8,128)(2,1)}) %all-gather.9.cloned.1.call-update) | async-done | bytes 25214992 | tf_op jit(solution)/shard_map/all_gather | solution.py:337
  239.6 1.1 convert_bitcast_fusion.1
  240.9 1.0 convert_bitcast_fusion.2
  242.4 4.6 fusion.8
  248.4 3.0 convert_reduce_fusion.2
  251.5 2.1 fusion.115
  254.6 0.9 bitcast_dynamic-update-slice_fusion.7
  255.4 1.9 slice.313
  257.3 4.0 slice.312
  261.3 5.5 multiply_convert_fusion
  266.9 6.0 shard_map.254
  272.8 1.3 fusion.111
  274.7 1.0 fusion.107
  276.4 6.8 shard_map.255
  283.2 2.8 fusion.105
  286.1 5.4 multiply_reduce_fusion.1
  291.8 0.8 copy-done.11
  292.5 2.5 fusion.47
  295.2 1.2 fusion.113
  296.4 1.3 fusion.118
  297.7 2.8 convolution_convert_fusion.1
  300.5 2.7 fusion.112
  303.2 1.2 bitcast_dynamic-update-slice_fusion.4
  304.4 1.7 bitcast_dynamic-update-slice_fusion.6
  306.1 1.9 fusion.90
  311.7 1.8 copy.117
  313.6 1.8 copy.116
  316.1 1.8 copy.115
  317.9 1.0 constant_dynamic-update-slice_fusion.6
  318.8 1.0 constant_dynamic-update-slice_fusion.5
  319.8 1.0 constant_dynamic-update-slice_fusion.4
  321.7 0.7 pad_dynamic-update-slice_fusion
  322.6 11.3 %convolution_convert_fusion = bf16[7,1024,1024]{2,1,0:T(8,128)(2,1)} fusion(bf16[7,128,1024]{2,1,0:T(8,128)(2,1)} %copy-done, bf16[7,128,1024]{2,1,0:T(8,128)(2,1)S(1)} %fusion.81, bf16[7,128,1024]{2,1,0:T(8,128)(2,1)} %broadcast_dynamic-update-slice_fusion.1, bf16[7,128,1024]{2,1,0:T(8,128)(2,1)} %pad_dynamic-update-slice_fusion, pred[]{:T(512)S(6)} %not.3), kind=kOutput, calls=%fused_computation.2 | convolution fusion | flops 1888223232 | bytes 22020096 | tf_op jit(solution)/shard_map/btk,btn->bkn/dot_general | solution.py:401
  333.9 22.5 %collective-permute-done = bf16[7,1024,1024]{2,1,0:T(8,128)(2,1)} collective-permute-done((bf16[7,1024,1024]{2,1,0:T(8,128)(2,1)}, bf16[7,1024,1024]{2,1,0:T(8,128)(2,1)}, u32[]{:S(2)}, u32[]{:S(2)}) %collective-permute-start) | collective-permute-done | bytes 14680096 | tf_op jit(solution)/shard_map/ppermute | solution.py:405
  356.4 19.4 %convert_add_fusion = f32[7,1024,1024]{2,1,0:T(8,128)} fusion(bf16[7,1024,1024]{2,1,0:T(8,128)(2,1)} %collective-permute-done, bf16[7,128,1024]{2,1,0:T(8,128)(2,1)} %copy-done, bf16[7,128,1024]{2,1,0:T(8,128)(2,1)S(1)} %fusion.81, bf16[7,128,1024]{2,1,0:T(8,128)(2,1)} %broadcast_dynamic-update-slice_fusion.1, ...), kind=kOutput, calls=%fused_computation.1 | convolution fusion | flops 1895563264 | bytes 51380224 | tf_op jit(solution)/shard_map/btk,btn->bkn/dot_general | solution.py:401
  375.9 322.6 %reduce-scatter.2.cloned.1.call-done = f32[7,32,1024]{2,1,0:T(8,128)} async-done(((f32[7,1024,1024]{2,1,0:T(8,128)}), f32[7,32,1024]{2,1,0:T(8,128)}) %reduce-scatter.2.cloned.1.call-update) | async-done | bytes 917520 | tf_op jit(solution)/shard_map/reduce_scatter | solution.py:406
  698.6 43.9 %all-reduce.3.cloned.1.call-done = f32[1,7,32,1024]{3,2,1,0:T(8,128)} async-done(((f32[1,7,32,1024]{3,2,1,0:T(8,128)}), f32[1,7,32,1024]{3,2,1,0:T(8,128)}) %all-reduce.3.cloned.1.call-update) | async-done | bytes 917520 | tf_op jit(solution)/shard_map/psum | solution.py:407
  742.6 5.8 fusion.44
  748.4 8.6 %all-gather.7.cloned.1.call-done = f32[2,7,32,1024]{3,2,1,0:T(8,128)} async-done(((f32[1,7,32,1024]{3,2,1,0:T(8,128)}), f32[2,7,32,1024]{3,2,1,0:T(8,128)}) %all-gather.7.cloned.1.call-update) | async-done | bytes 1835024 | tf_op jit(solution)/shard_map/all_gather | solution.py:408
  757.0 2.3 slice_bitcast_fusion.12
  759.2 0.8 slice_reduce_fusion.2
  760.5 1.0 broadcast_in_dim_reshape.11
  762.8 0.9 copy.121
  763.6 1.4 copy.123
  765.0 0.8 maximum_bitcast_fusion.1
  (149 shorter events, 17.7 us)
Async XLA Ops:
  7.2 170.3 %all-gather.5.cloned.1.call-start = ((), (), s32[]{:S(2)}) async-start(), calls=%async_computation.1 | async-start | bytes 13246464 | tf_op jit(solution)/shard_map/all_gather | solution.py:336
  7.2 2.9 copy-start.30
  7.2 3.7 copy-start.23
  7.3 3.8 copy-start.24
  7.3 3.9 copy-start.25
  7.3 4.0 copy-start.26
  7.3 4.1 copy-start.27
  7.3 4.2 copy-start.28
  7.3 4.3 copy-start.29
  7.3 4.4 copy-start.17
  7.3 4.6 copy-start.22
  8.8 3.2 copy-start.20
  12.9 226.7 %all-gather.9.cloned.1.call-start = ((), (), s32[]{:S(2)}) async-start(), calls=%async_computation.5 | async-start | bytes 38535168 | tf_op jit(solution)/shard_map/all_gather | solution.py:337
  177.5 0.9 copy-start.4
  177.5 3.1 copy-start.6
  177.6 521.0 %reduce-scatter.2.cloned.1.call-start = ((), (), s32[]{:S(2)}) async-start(), calls=%async_computation.2 | async-start | bytes 30277632 | tf_op jit(solution)/shard_map/reduce_scatter | solution.py:406
  247.0 0.9 copy-start.14
  247.4 0.9 copy-start.7
  247.4 0.9 copy-start.16
  255.4 5.9 copy-start.2
  257.3 4.0 copy-start.9
  261.3 5.6 copy-start.1
  283.2 2.9 copy-start.10
  291.7 0.8 copy-start.11
  292.5 3.8 copy-start.8
  296.4 4.1 copy-start.15
  303.2 4.7 copy-start.5
  303.2 6.9 copy-start.3
  320.9 0.8 copy-start.21
  321.1 1.3 copy-start
  333.9 22.5 %collective-permute-start = (bf16[7,1024,1024]{2,1,0:T(8,128)(2,1)}, bf16[7,1024,1024]{2,1,0:T(8,128)(2,1)}, u32[]{:S(2)}, u32[]{:S(2)}) collective-permute-start(bf16[7,1024,1024]{2,1,0:T(8,128)(2,1)} %convolution_convert_fusion), channel_id=1, source_target_pairs={{0,32},{32,0},{1,33},{33,1},{2,34},{34,2},{3,35},{35,3},{4,36},{36... | collective-permute-start | bytes 44040200 | tf_op jit(solution)/shard_map/ppermute | solution.py:405
  375.8 366.7 %copy-start.12 = (f32[128,1024]{1,0:T(8,128)S(1)}, f32[128,1024]{1,0:T(8,128)}, u32[]{:S(2)}) copy-start(f32[128,1024]{1,0:T(8,128)} %copy-done.11) | copy-start | bytes 1572868
  375.8 366.7 %copy-start.13 = (bf16[1,128,16,64]{1,3,2,0:T(8,128)(2,1)S(1)}, bf16[1,128,16,64]{1,3,2,0:T(8,128)(2,1)}, u32[]{:S(2)}) copy-start(bf16[1,128,16,64]{1,3,2,0:T(8,128)(2,1)} %get-tuple-element.120) | copy-start | bytes 786436
  375.9 366.7 %copy-start.18 = (bf16[16,64,128]{2,1,0:T(8,128)(2,1)S(1)}, bf16[16,64,128]{2,1,0:T(8,128)(2,1)}, u32[]{:S(2)}) copy-start(bf16[16,64,128]{2,1,0:T(8,128)(2,1)} %convolution_convert_fusion.1) | copy-start | bytes 786436
  375.9 366.7 %copy-start.19 = (bf16[1,128,16,64]{1,3,2,0:T(8,128)(2,1)S(1)}, bf16[1,128,16,64]{1,3,2,0:T(8,128)(2,1)}, u32[]{:S(2)}) copy-start(bf16[1,128,16,64]{1,3,2,0:T(8,128)(2,1)} %get-tuple-element.118) | copy-start | bytes 786436
  375.9 366.7 %all-reduce.3.cloned.1.call-start = ((), (), s32[]{:S(2)}) async-start(), calls=%async_computation.3 | async-start | bytes 1835008 | tf_op jit(solution)/shard_map/psum | solution.py:407
  698.6 58.4 %all-gather.7.cloned.1.call-start = ((), (), s32[]{:S(2)}) async-start(), calls=%async_computation.4 | async-start | bytes 2752512 | tf_op jit(solution)/shard_map/all_gather | solution.py:408
Sparse Core Ops, SparseCore 0:
  13.1 164.4 all-gather.4
  179.2 60.3 all-gather.8
  376.0 322.5 reduce-scatter.1
  700.8 41.6 all-reduce.2
  744.1 12.7 all-gather.6

commit v11 on v10

--- a/solution.py
+++ b/solution.py
@@ -334,9 +334,11 @@
     first, second = pack_halves(w_qkv[0], w_att[0], group_columns(w_in[0], 4), w_out[0], small)
     mine = jnp.where(core == 0, first, second)
     gathered = lax.all_gather(mine, SHARD_AXES, axis=0, tiled=True)
-    both = lax.all_gather(gathered, "core", axis=0, tiled=False)
-    f_qkv, f_att, f_in, f_out, f_small = unpack_halves(both[0], both[1], model_width, ff)
-    f_out = (both, 1, (model_width + ff - 3 * model_width) // model_width)
+    other = lax.ppermute(gathered, "core", perm=[(0, 1), (1, 0)])
+    first_all = jnp.where(core == 0, gathered, other)
+    second_all = jnp.where(core == 0, other, gathered)
+    f_qkv, f_att, f_in, f_out, f_small = unpack_halves(first_all, second_all, model_width, ff)
+    f_out = (second_all[None], 0, (model_width + ff - 3 * model_width) // model_width)
     f_bqv = f_small[:, 0:2].T
     f_bin = group_columns(f_small[:, 8:].reshape(1, ff), 4)[0]
     params = (

time: 773 us -> 789 us (1.021)
  waiting for transfers between devices: 621 us -> 576 us
  local copies, waits for them, and re-layouts: 39.8 us -> 77.7 us
  starting transfers between devices: 0.2 us -> 16.5 us
    all_gather x1 -> x0, waiting for transfers between devices: 58.9 us -> none  [body(): both = lax.all_gather(gathered, 'core', axis=0, tiled=False)]
    all_gather x0 -> x1, local copies, waits for them, and re-layouts: none -> 17.4 us  [body(): gathered = lax.all_gather(mine, SHARD_AXES, axis=0, tiled=True)]
    ppermute x0 -> x1, starting transfers between devices: none -> 16.3 us  [body(): other = lax.ppermute(gathered, 'core', perm=[(0, 1), (1, 0)])]
    ppermute x0 -> x1, waiting for transfers between devices: none -> 16.2 us  [body(): other = lax.ppermute(gathered, 'core', perm=[(0, 1), (1, 0)])]
    ppermute x0 -> x1, local copies, waits for them, and re-layouts: none -> 16.1 us  [body(): other = lax.ppermute(gathered, 'core', perm=[(0, 1), (1, 0)])]
    select_n x0 -> x1, other arithmetic: none -> 10.2 us  [body(): first_all = jnp.where(core == 0, gathered, other)]
    unnamed x83 -> x87, local copies, waits for them, and re-layouts: 17.4 us -> 20.7 us
where the time goes in v11:
time: 789 us; the launch traced here: 788 us
  waiting for transfers between devices  576 us (73%)
  local copies, waits for them, and re-layouts  77.7 us (10%)
  matrix products  65.7 us (8%)
  other arithmetic  24.1 us (3%)
  starting transfers between devices  16.5 us (2%)
  between operations  15.1 us (2%)
  Pallas kernels  12.8 us (2%)
    reduce_scatter x1, waiting for transfers between devices, body(): part = lax.psum_scatter(half, SHARD_AXES, scatter_dimension=1, tiled=True)  320 us
    all_gather x1, waiting for transfers between devices, body(): gathered = lax.all_gather(mine, SHARD_AXES, axis=0, tiled=True)  165 us
    psum x1, waiting for transfers between devices, body(): part = lax.psum(part, 'xh')  44.1 us
    dot_general x2, matrix products, products(): jnp.einsum('btk,btn->bkn', left, right, preferred_element_type=jnp.float32)  30.7 us
    ppermute x1, waiting for transfers between devices, body(): lax.ppermute(sent, 'core', perm=[(0, 1), (1, 0)]).astype(jnp.float32)  22.5 us
    unnamed x87, local copies, waits for them, and re-layouts  20.7 us
    all_gather x1, local copies, waits for them, and re-layouts, body(): gathered = lax.all_gather(mine, SHARD_AXES, axis=0, tiled=True)  17.4 us
    ppermute x1, starting transfers between devices, body(): other = lax.ppermute(gathered, 'core', perm=[(0, 1), (1, 0)])  16.3 us
  transfers between devices with their start and end apart: 6, of which 6 were waited for; matrix products, arithmetic and copies ran while one was open for 1% of the time, Pallas kernels for 0%

profile of v11, /device:TPU:1, one launch (start us, length us, event | category | flops | bytes accessed | tf_op | source)
XLA Modules:
  0.0 787.5 jit_solution(13905469935223151647)
XLA Ops:
  7.3 1.5 copy.75
  12.0 0.9 maximum_select_fusion
  13.0 164.5 %all-gather.3.cloned.1.call-done = bf16[1024,6156]{1,0:T(8,128)(2,1)} async-done(((bf16[32,6156]{1,0:T(8,128)(2,1)}), bf16[1024,6156]{1,0:T(8,128)(2,1)}) %all-gather.3.cloned.1.call-update) | async-done | bytes 12607504 | tf_op jit(solution)/shard_map/all_gather | solution.py:336
  177.5 17.4 %copy.84 = bf16[1024,6156]{0,1:T(8,128)(2,1)} copy(bf16[1024,6156]{1,0:T(8,128)(2,1)} %all-gather.3.cloned.1.call-done) | data formatting | bytes 25214976 | tf_op jit(solution)/shard_map/all_gather | solution.py:336
  195.0 16.3 %collective-permute-start = (bf16[1024,6156]{0,1:T(8,128)(2,1)}, bf16[1024,6156]{0,1:T(8,128)(2,1)}, u32[]{:S(2)}, u32[]{:S(2)}) collective-permute-start(bf16[1024,6156]{0,1:T(8,128)(2,1)} %copy.84), channel_id=1, source_target_pairs={{0,32},{32,0},{1,33},{33,1},{2,34},{34,2},{3,35},{35,3},{4,36},{36... | collective-permute-start | bytes 37822472 | tf_op jit(solution)/shard_map/ppermute | solution.py:337
  214.3 16.2 %collective-permute-done = bf16[1024,6156]{0,1:T(8,128)(2,1)} collective-permute-done((bf16[1024,6156]{0,1:T(8,128)(2,1)}, bf16[1024,6156]{0,1:T(8,128)(2,1)}, u32[]{:S(2)}, u32[]{:S(2)}) %collective-permute-start) | collective-permute-done | bytes 12607520 | tf_op jit(solution)/shard_map/ppermute | solution.py:337
  230.5 16.1 %copy.85 = bf16[1024,6156]{1,0:T(8,128)(2,1)} copy(bf16[1024,6156]{0,1:T(8,128)(2,1)} %collective-permute-done) | data formatting | bytes 25214976 | tf_op jit(solution)/shard_map/ppermute | solution.py:337
  246.6 10.2 %broadcast_select_fusion.1 = (bf16[1024,6156]{1,0:T(8,128)(2,1)S(1)}, bf16[1024,6156]{1,0:T(8,128)(2,1)S(1)}) fusion(bf16[1024,6156]{1,0:T(8,128)(2,1)} %all-gather.3.cloned.1.call-done, bf16[1024,6156]{1,0:T(8,128)(2,1)} %copy.85, pred[]{:T(512)S(6)} %eq.18), kind=kLoop, calls=%fused_computation.3 | loop fusion | flops 12607488 | bytes 50429952 | tf_op jit(solution)/shard_map/jit(_where)/select_n | solution.py:338
  256.8 1.0 convert_reduce_fusion.2
  258.1 3.4 copy-done
  261.4 2.4 slice.291
  263.9 3.0 fusion.8
  266.9 3.5 slice.290
  271.0 1.1 slice.408
  273.5 2.1 fusion.115
  276.6 0.9 bitcast_dynamic-update-slice_fusion.7
  277.5 7.4 multiply_convert_fusion
  284.9 6.0 shard_map.254
  290.9 1.3 fusion.111
  292.7 1.0 fusion.107
  294.4 6.8 shard_map.255
  301.2 2.8 fusion.105
  304.1 5.5 multiply_reduce_fusion.1
  310.6 2.5 fusion.47
  313.3 1.2 fusion.113
  314.5 1.3 fusion.118
  315.8 2.8 convolution_convert_fusion.1
  318.6 2.7 fusion.112
  321.3 1.2 bitcast_dynamic-update-slice_fusion.4
  322.5 1.7 bitcast_dynamic-update-slice_fusion.6
  324.2 1.9 fusion.90
  329.8 1.8 copy.96
  331.6 1.8 copy.95
  334.2 1.8 copy.94
  336.0 1.0 constant_dynamic-update-slice_fusion.6
  336.9 1.0 constant_dynamic-update-slice_fusion.5
  337.9 1.0 constant_dynamic-update-slice_fusion.4
  340.7 11.3 %convolution_convert_fusion = bf16[7,1024,1024]{2,1,0:T(8,128)(2,1)} fusion(bf16[7,128,1024]{2,1,0:T(8,128)(2,1)} %copy-done.2, bf16[7,128,1024]{2,1,0:T(8,128)(2,1)S(1)} %fusion.81, bf16[7,128,1024]{2,1,0:T(8,128)(2,1)} %broadcast_dynamic-update-slice_fusion.1, bf16[7,128,1024]{2,1,0:T(8,128)(2,1)} %pad_dynamic-update-slice_fusion, pred[]{:T(512)S(6)} %not.3), kind=kOutput, calls=%fused_computation.4 | convolution fusion | flops 1888223232 | bytes 22020096 | tf_op jit(solution)/shard_map/btk,btn->bkn/dot_general | solution.py:403
  351.9 22.5 %collective-permute-done.1 = bf16[7,1024,1024]{2,1,0:T(8,128)(2,1)} collective-permute-done((bf16[7,1024,1024]{2,1,0:T(8,128)(2,1)}, bf16[7,1024,1024]{2,1,0:T(8,128)(2,1)}, u32[]{:S(2)}, u32[]{:S(2)}) %collective-permute-start.1) | collective-permute-done | bytes 14680096 | tf_op jit(solution)/shard_map/ppermute | solution.py:407
  374.4 19.4 %convert_add_fusion = f32[7,1024,1024]{2,1,0:T(8,128)} fusion(bf16[7,1024,1024]{2,1,0:T(8,128)(2,1)} %collective-permute-done.1, bf16[7,128,1024]{2,1,0:T(8,128)(2,1)} %copy-done.2, bf16[7,128,1024]{2,1,0:T(8,128)(2,1)S(1)} %fusion.81, bf16[7,128,1024]{2,1,0:T(8,128)(2,1)} %broadcast_dynamic-update-slice_fusion.1, ...), kind=kOutput, calls=%fused_computation.1 | convolution fusion | flops 1895563264 | bytes 51380224 | tf_op jit(solution)/shard_map/btk,btn->bkn/dot_general | solution.py:403
  394.0 319.6 %reduce-scatter.2.cloned.1.call-done = f32[7,32,1024]{2,1,0:T(8,128)} async-done(((f32[7,1024,1024]{2,1,0:T(8,128)}), f32[7,32,1024]{2,1,0:T(8,128)}) %reduce-scatter.2.cloned.1.call-update) | async-done | bytes 917520 | tf_op jit(solution)/shard_map/reduce_scatter | solution.py:408
  713.7 44.1 %all-reduce.3.cloned.1.call-done = f32[1,7,32,1024]{3,2,1,0:T(8,128)} async-done(((f32[1,7,32,1024]{3,2,1,0:T(8,128)}), f32[1,7,32,1024]{3,2,1,0:T(8,128)}) %all-reduce.3.cloned.1.call-update) | async-done | bytes 917520 | tf_op jit(solution)/shard_map/psum | solution.py:409
  757.8 5.8 fusion.44
  763.6 8.6 %all-gather.5.cloned.1.call-done = f32[2,7,32,1024]{3,2,1,0:T(8,128)} async-done(((f32[1,7,32,1024]{3,2,1,0:T(8,128)}), f32[2,7,32,1024]{3,2,1,0:T(8,128)}) %all-gather.5.cloned.1.call-update) | async-done | bytes 1835024 | tf_op jit(solution)/shard_map/all_gather | solution.py:410
  772.2 2.3 slice_bitcast_fusion.12
  775.7 1.0 broadcast_in_dim_reshape.11
  778.0 0.9 copy.100
  778.9 1.4 copy.102
  (155 shorter events, 20.7 us)
Async XLA Ops:
  7.2 170.3 %all-gather.3.cloned.1.call-start = ((), (), s32[]{:S(2)}) async-start(), calls=%async_computation.1 | async-start | bytes 13246464 | tf_op jit(solution)/shard_map/all_gather | solution.py:336
  7.2 2.9 copy-start.32
  7.2 3.7 copy-start.25
  7.3 3.8 copy-start.26
  7.3 3.9 copy-start.27
  7.3 4.0 copy-start.28
  7.3 4.1 copy-start.29
  7.3 4.2 copy-start.30
  7.3 4.3 copy-start.31
  7.3 4.4 copy-start.19
  7.3 4.6 copy-start.24
  8.8 3.2 copy-start.22
  12.9 199.1 %copy-start.6 = (bf16[1,128,1024]{2,1,0:T(8,128)(2,1)S(1)}, bf16[1,128,1024]{2,1,0:T(8,128)(2,1)}, u32[]{:S(2)}) copy-start(bf16[1,128,1024]{2,1,0:T(8,128)(2,1)} %param.17) | copy-start | bytes 786436
  12.9 201.3 %copy-start.7 = (bf16[1,128,1024]{2,1,0:T(8,128)(2,1)S(1)}, bf16[1,128,1024]{2,1,0:T(8,128)(2,1)}, u32[]{:S(2)}) copy-start(bf16[1,128,1024]{2,1,0:T(8,128)(2,1)} %param.19) | copy-start | bytes 786436
  13.0 700.6 %reduce-scatter.2.cloned.1.call-start = ((), (), s32[]{:S(2)}) async-start(), calls=%async_computation.2 | async-start | bytes 30277632 | tf_op jit(solution)/shard_map/reduce_scatter | solution.py:408
  195.0 35.5 %collective-permute-start = (bf16[1024,6156]{0,1:T(8,128)(2,1)}, bf16[1024,6156]{0,1:T(8,128)(2,1)}, u32[]{:S(2)}, u32[]{:S(2)}) collective-permute-start(bf16[1024,6156]{0,1:T(8,128)(2,1)} %copy.84), channel_id=1, source_target_pairs={{0,32},{32,0},{1,33},{33,1},{2,34},{34,2},{3,35},{35,3},{4,36},{36... | collective-permute-start | bytes 37822472 | tf_op jit(solution)/shard_map/ppermute | solution.py:337
  256.8 4.6 copy-start
  256.8 10.0 %copy-start.1 = (bf16[1024,6156]{1,0:T(8,128)(2,1)}, bf16[1024,6156]{1,0:T(8,128)(2,1)S(1)}, u32[]{:S(2)}) copy-start(bf16[1024,6156]{1,0:T(8,128)(2,1)S(1)} %get-tuple-element.83) | copy-start | bytes 37822468
  270.5 1.6 copy-start.14
  272.1 0.9 copy-start.16
  272.5 0.9 copy-start.8
  272.5 0.9 copy-start.18
  275.7 1.8 copy-start.10
  277.5 7.4 copy-start.4
  301.2 2.9 copy-start.11
  309.8 0.8 copy-start.12
  310.6 3.8 copy-start.9
  314.5 4.1 copy-start.17
  321.3 4.8 copy-start.3
  321.3 6.9 copy-start.5
  339.0 0.8 copy-start.23
  339.2 1.3 copy-start.2
  351.9 22.5 %collective-permute-start.1 = (bf16[7,1024,1024]{2,1,0:T(8,128)(2,1)}, bf16[7,1024,1024]{2,1,0:T(8,128)(2,1)}, u32[]{:S(2)}, u32[]{:S(2)}) collective-permute-start(bf16[7,1024,1024]{2,1,0:T(8,128)(2,1)} %convolution_convert_fusion), channel_id=1, source_target_pairs={{0,32},{32,0},{1,33},{33,1},{2,34},{34,2},{3,35},{35,3},{4,36},{36... | collective-permute-start | bytes 44040200 | tf_op jit(solution)/shard_map/ppermute | solution.py:407
  393.9 363.9 %copy-start.13 = (f32[128,1024]{1,0:T(8,128)S(1)}, f32[128,1024]{1,0:T(8,128)}, u32[]{:S(2)}) copy-start(f32[128,1024]{1,0:T(8,128)} %copy-done.12) | copy-start | bytes 1572868
  393.9 363.9 %copy-start.15 = (bf16[1,128,16,64]{1,3,2,0:T(8,128)(2,1)S(1)}, bf16[1,128,16,64]{1,3,2,0:T(8,128)(2,1)}, u32[]{:S(2)}) copy-start(bf16[1,128,16,64]{1,3,2,0:T(8,128)(2,1)} %get-tuple-element.108) | copy-start | bytes 786436
  393.9 363.9 %copy-start.20 = (bf16[16,64,128]{2,1,0:T(8,128)(2,1)S(1)}, bf16[16,64,128]{2,1,0:T(8,128)(2,1)}, u32[]{:S(2)}) copy-start(bf16[16,64,128]{2,1,0:T(8,128)(2,1)} %convolution_convert_fusion.1) | copy-start | bytes 786436
  393.9 363.9 %copy-start.21 = (bf16[1,128,16,64]{1,3,2,0:T(8,128)(2,1)S(1)}, bf16[1,128,16,64]{1,3,2,0:T(8,128)(2,1)}, u32[]{:S(2)}) copy-start(bf16[1,128,16,64]{1,3,2,0:T(8,128)(2,1)} %get-tuple-element.106) | copy-start | bytes 786436
  393.9 363.8 %all-reduce.3.cloned.1.call-start = ((), (), s32[]{:S(2)}) async-start(), calls=%async_computation.3 | async-start | bytes 1835008 | tf_op jit(solution)/shard_map/psum | solution.py:409
  713.6 58.6 %all-gather.5.cloned.1.call-start = ((), (), s32[]{:S(2)}) async-start(), calls=%async_computation.4 | async-start | bytes 2752512 | tf_op jit(solution)/shard_map/all_gather | solution.py:410
Sparse Core Ops, SparseCore 0:
  13.1 164.4 all-gather.2
  394.0 319.5 reduce-scatter.1
  716.0 41.6 all-reduce.2
  759.4 12.7 all-gather.4

commit v12 on v5

--- a/solution.py
+++ b/solution.py
@@ -386,26 +386,39 @@
     rows_used = lax.broadcasted_iota(jnp.int32, (tokens, model_width), 0) < 3 * n_small
     enc_right = (picks & rows_used).astype(jnp.bfloat16)
     zero = jnp.zeros((tokens, model_width), jnp.bfloat16)
-    lefts = [g_qkv[0]] * 3 + [g_in[0]] * 3 + [zero]
-    lefts += [g_att[0], g_in[0]] + [col(g_out[0], j) for j in range(4)] + [enc_left]
-    rights = [col(g_qkv[1], c) for c in range(3)] + [col(g_in[1], c) for c in range(3)] + [zero]
-    rights += [g_att[1], col(g_in[1], 3)] + [g_out[1]] * 4 + [enc_right]
-    wgrads = jnp.einsum(
-        "btk,btn->bkn",
-        jnp.stack(lefts),
-        jnp.stack(rights),
-        preferred_element_type=jnp.float32,
-    ).reshape(2, len(lefts) // 2, model_width, model_width)
-    half = lax.psum_scatter(wgrads, "core", scatter_dimension=0, tiled=False)
+    mine_first = core == 0
+
+    def exchange(lefts, rights):
+        stacked_left = jnp.stack([jnp.stack(side) for side in lefts])
+        stacked_right = jnp.stack([jnp.stack(side) for side in rights])
+
+        def products(pick_first):
+            left = jnp.where(pick_first, stacked_left[0], stacked_left[1])
+            right = jnp.where(pick_first, stacked_right[0], stacked_right[1])
+            return jnp.einsum("btk,btn->bkn", left, right, preferred_element_type=jnp.float32)
+
+        kept = products(mine_first)
+        sent = products(jnp.logical_not(mine_first)).astype(jnp.bfloat16)
+        return kept + lax.ppermute(sent, "core", perm=[(0, 1), (1, 0)]).astype(jnp.float32)
+
+    early = exchange(
+        [[g_in[0]] * 4, [col(g_out[0], j) for j in range(4)]],
+        [[col(g_in[1], c) for c in range(4)], [g_out[1]] * 4],
+    )
+    late = exchange(
+        [[g_qkv[0]] * 3, [g_att[0], enc_left, zero]],
+        [[col(g_qkv[1], c) for c in range(3)], [g_att[1], enc_right, zero]],
+    )
+    half = jnp.concatenate([early, late], axis=0)
     part = lax.psum_scatter(half, SHARD_AXES, scatter_dimension=1, tiled=True)
     part = lax.psum(part, "xh")
     res = lax.all_gather(part, "core", axis=0, tiled=False)
     r0, r1 = res[0], res[1]
-    r_qkv = jnp.concatenate([r0[0], r0[1], r0[2]], axis=1)
-    r_in = ungroup_columns(jnp.concatenate([r0[3], r0[4], r0[5], r1[1]], axis=1), 4)
-    r_att = r1[0]
-    r_out = jnp.stack([r1[2], r1[3], r1[4], r1[5]], axis=1)
-    r_small = r1[6][:, :n_small]
+    r_in = ungroup_columns(jnp.concatenate([r0[0], r0[1], r0[2], r0[3]], axis=1), 4)
+    r_qkv = jnp.concatenate([r0[4], r0[5], r0[6]], axis=1)
+    r_out = jnp.stack([r1[0], r1[1], r1[2], r1[3]], axis=1)
+    r_att = r1[4]
+    r_small = r1[5][:, :n_small]
     grad_inputs = upstream.reshape(inputs.shape)
     return (
         outputs,

time: 815 us -> 754 us (0.925)
  waiting for transfers between devices: 677 us -> 611 us
  other arithmetic: 16 us -> 34.7 us
  local copies, waits for them, and re-layouts: 33.9 us -> 23.6 us
    reduce_scatter x1 -> x0, waiting for transfers between devices: 77 us -> none  [body(): half = lax.psum_scatter(wgrads, 'core', scatter_dimension=0, tiled=False)]
    concatenate x0 -> x1, other arithmetic: none -> 18.6 us  [body(): half = jnp.concatenate([early, late], axis=0)]
    ppermute x0 -> x2, waiting for transfers between devices: none -> 11.7 us  [exchange(): lax.ppermute(sent, 'core', perm=[(0, 1), (1, 0)]).astype(jnp.float32)]
    unnamed x79 -> x107, local copies, waits for them, and re-layouts: 15.5 us -> 5.59 us
    dot_general x1 -> x4, matrix products: 22.5 us -> 19.8 us  [products(): jnp.einsum('btk,btn->bkn', left, right, preferred_element_type=jnp.float32)]
  transfers between devices with their start and end apart: 6 -> 7, of which waited for: 6 -> 6; matrix products, arithmetic and copies ran while one was open for 1% -> 3% of each run, Pallas kernels for 0% -> 0%
where the time goes in v12:
time: 754 us; the launch traced here: 753 us
  waiting for transfers between devices  611 us (81%)
  matrix products  54.6 us (7%)
  other arithmetic  34.7 us (5%)
  local copies, waits for them, and re-layouts  23.6 us (3%)
  between operations  15.4 us (2%)
  Pallas kernels  12.8 us (2%)
    reduce_scatter x1, waiting for transfers between devices, body(): part = lax.psum_scatter(half, SHARD_AXES, scatter_dimension=1, tiled=True)  322 us
    all_gather x1, waiting for transfers between devices, body(): gathered = lax.all_gather(mine, SHARD_AXES, axis=0, tiled=True)  165 us
    all_gather x1, waiting for transfers between devices, body(): both = lax.all_gather(gathered, 'core', axis=0, tiled=False)  60.2 us
    psum x1, waiting for transfers between devices, body(): part = lax.psum(part, 'xh')  44 us
    dot_general x4, matrix products, products(): jnp.einsum('btk,btn->bkn', left, right, preferred_element_type=jnp.float32)  19.8 us
    concatenate x1, other arithmetic, body(): half = jnp.concatenate([early, late], axis=0)  18.6 us
  transfers between devices with their start and end apart: 7, of which 6 were waited for; matrix products, arithmetic and copies ran while one was open for 3% of the time, Pallas kernels for 0%

profile of v12, /device:TPU:1, one launch (start us, length us, event | category | flops | bytes accessed | tf_op | source)
XLA Modules:
  0.0 753.3 jit_solution(1413006591095261981)
XLA Ops:
  7.3 1.5 copy.105
  8.9 0.7 copy.106
  10.2 0.7 reduce.42
  12.1 0.9 maximum_select_fusion
  13.0 164.5 %all-gather.5.cloned.1.call-done = bf16[1024,6156]{1,0:T(8,128)(2,1)} async-done(((bf16[32,6156]{1,0:T(8,128)(2,1)}), bf16[1024,6156]{1,0:T(8,128)(2,1)}) %all-gather.5.cloned.1.call-update) | async-done | bytes 12607504 | tf_op jit(solution)/shard_map/all_gather | solution.py:336
  178.6 0.9 fusion.96
  179.4 60.2 %all-gather.9.cloned.1.call-done = bf16[2048,6156]{1,0:T(8,128)(2,1)} async-done(((bf16[1024,6156]{1,0:T(8,128)(2,1)}), bf16[2048,6156]{1,0:T(8,128)(2,1)}) %all-gather.9.cloned.1.call-update) | async-done | bytes 25214992 | tf_op jit(solution)/shard_map/all_gather | solution.py:337
  239.6 1.1 convert_bitcast_fusion.1
  240.9 1.0 convert_bitcast_fusion.2
  242.4 4.6 fusion.8
  248.5 3.0 convert_reduce_fusion.2
  251.5 2.1 fusion.132
  254.0 1.8 slice.297
  255.8 4.0 slice.296
  259.8 5.6 multiply_convert_fusion
  265.4 1.1 slice_bitcast_fusion.7
  266.7 6.0 shard_map.254
  272.7 1.3 fusion.128
  274.6 1.0 fusion.125
  275.5 0.8 convert_element_type.200.grad_ref
  276.3 6.8 shard_map.255
  283.1 2.8 fusion.123
  286.1 5.2 multiply_reduce_fusion.1
  291.6 0.8 copy-done.11
  292.4 2.5 fusion.40
  295.0 1.2 fusion.130
  296.2 1.4 fusion.135
  297.7 0.7 copy-done.24
  298.4 5.5 convolution_convert_fusion
  304.2 2.8 fusion.129
  307.5 2.9 convolution_convert_fusion.2
  310.4 1.1 copy.124
  311.8 1.9 convolution_convert_fusion.1
  314.4 11.7 %collective-permute-done.1 = bf16[3,1024,1024]{2,1,0:T(8,128)(2,1)S(1)} collective-permute-done((bf16[3,1024,1024]{2,1,0:T(8,128)(2,1)S(1)}, bf16[3,1024,1024]{2,1,0:T(8,128)(2,1)S(1)}, u32[]{:S(2)}, u32[]{:S(2)}) %collective-permute-start.1) | collective-permute-done | bytes 6291488 | tf_op jit(solution)/shard_map/ppermute | solution.py:402
  326.1 6.4 convert_add_fusion.1
  332.7 6.0 convert_add_fusion
  338.7 18.6 %pad_maximum_fusion = f32[7,1024,1024]{2,1,0:T(8,128)} fusion(f32[3,1024,1024]{2,1,0:T(8,128)} %convert_add_fusion.1, f32[4,1024,1024]{2,1,0:T(8,128)S(1)} %convert_add_fusion), kind=kLoop, calls=%fused_computation.1 | loop fusion | flops 7340032 | bytes 58720256 | tf_op jit(solution)/shard_map/concatenate | solution.py:412
  357.3 322.2 %reduce-scatter.2.cloned.1.call-done = f32[7,32,1024]{2,1,0:T(8,128)} async-done(((f32[7,1024,1024]{2,1,0:T(8,128)}), f32[7,32,1024]{2,1,0:T(8,128)}) %reduce-scatter.2.cloned.1.call-update) | async-done | bytes 917520 | tf_op jit(solution)/shard_map/reduce_scatter | solution.py:413
  679.6 44.0 %all-reduce.3.cloned.1.call-done = f32[1,7,32,1024]{3,2,1,0:T(8,128)} async-done(((f32[1,7,32,1024]{3,2,1,0:T(8,128)}), f32[1,7,32,1024]{3,2,1,0:T(8,128)}) %all-reduce.3.cloned.1.call-update) | async-done | bytes 917520 | tf_op jit(solution)/shard_map/psum | solution.py:414
  723.6 5.8 fusion.37
  729.4 8.6 %all-gather.7.cloned.1.call-done = f32[2,7,32,1024]{3,2,1,0:T(8,128)} async-done(((f32[1,7,32,1024]{3,2,1,0:T(8,128)}), f32[2,7,32,1024]{3,2,1,0:T(8,128)}) %all-gather.7.cloned.1.call-update) | async-done | bytes 1835024 | tf_op jit(solution)/shard_map/all_gather | solution.py:415
  737.9 2.3 slice_bitcast_fusion.12
  740.2 0.8 slice_reduce_fusion.2
  741.5 1.0 broadcast_in_dim_reshape.11
  743.1 0.6 copy.128
  743.7 0.9 copy.129
  744.6 1.4 copy.131
  746.0 0.8 maximum_bitcast_fusion.1
  (174 shorter events, 8.8 us)
Async XLA Ops:
  7.2 3.0 copy-start.50
  7.2 3.8 copy-start.43
  7.2 3.9 copy-start.44
  7.2 4.0 copy-start.45
  7.2 4.1 copy-start.46
  7.2 4.2 copy-start.47
  7.2 4.3 copy-start.48
  7.3 4.4 copy-start.49
  7.3 4.4 copy-start.37
  7.3 170.3 %all-gather.5.cloned.1.call-start = ((), (), s32[]{:S(2)}) async-start(), calls=%async_computation.1 | async-start | bytes 13246464 | tf_op jit(solution)/shard_map/all_gather | solution.py:336
  7.3 4.6 copy-start.42
  8.8 3.2 copy-start.41
  13.0 226.7 %all-gather.9.cloned.1.call-start = ((), (), s32[]{:S(2)}) async-start(), calls=%async_computation.5 | async-start | bytes 38535168 | tf_op jit(solution)/shard_map/all_gather | solution.py:337
  177.6 64.8 %copy-start.2 = (bf16[1,128,1024]{2,1,0:T(8,128)(2,1)S(1)}, bf16[1,128,1024]{2,1,0:T(8,128)(2,1)}, u32[]{:S(2)}) copy-start(bf16[1,128,1024]{2,1,0:T(8,128)(2,1)} %param.17) | copy-start | bytes 786436
  177.6 501.9 %reduce-scatter.2.cloned.1.call-start = ((), (), s32[]{:S(2)}) async-start(), calls=%async_computation.2 | async-start | bytes 30277632 | tf_op jit(solution)/shard_map/reduce_scatter | solution.py:413
  248.4 5.2 copy-start.7
  255.8 4.0 copy-start.9
  259.8 5.6 copy-start.1
  275.5 7.6 %copy-start.13 = (f32[128,1024]{1,0:T(8,128)}, f32[128,1024]{1,0:T(8,128)S(1)}, u32[]{:S(2)}) copy-start(f32[128,1024]{1,0:T(8,128)S(1)} %get-tuple-element.90) | copy-start | bytes 1572868
  283.1 2.9 copy-start.10
  283.1 2.9 copy-start.14
  292.4 3.8 copy-start.6
  296.2 2.2 copy-start.16
  296.2 2.2 copy-start.18
  297.7 6.2 copy-start.26
  297.7 6.2 copy-start.28
  297.7 6.2 copy-start.30
  298.4 5.8 copy-start.35
  303.9 3.1 copy-start.8
  303.9 3.4 copy-start.32
  303.9 28.7 %collective-permute-start = (bf16[4,1024,1024]{2,1,0:T(8,128)(2,1)}, bf16[4,1024,1024]{2,1,0:T(8,128)(2,1)}, u32[]{:S(2)}, u32[]{:S(2)}) collective-permute-start(bf16[4,1024,1024]{2,1,0:T(8,128)(2,1)} %convolution_convert_fusion), channel_id=1, source_target_pairs={{0,32},{32,0},{1,33},{33,1},{2,34},{34,2},{3,35},{35,3},{4,36},{36... | collective-permute-start | bytes 25165832 | tf_op jit(solution)/shard_map/ppermute | solution.py:402
  307.1 4.3 copy-start.38
  307.2 4.6 copy-start.12
  307.5 4.3 copy-start.15
  313.8 18.8 %copy-start.17 = (bf16[1,128,1024]{2,1,0:T(8,128)(2,1)S(1)}, bf16[1,128,1024]{2,1,0:T(8,128)(2,1)}, u32[]{:S(2)}) copy-start(bf16[1,128,1024]{2,1,0:T(8,128)(2,1)} %get-tuple-element.112) | copy-start | bytes 786436
  313.8 18.8 %copy-start.19 = (bf16[1,128,1024]{2,1,0:T(8,128)(2,1)S(1)}, bf16[1,128,1024]{2,1,0:T(8,128)(2,1)}, u32[]{:S(2)}) copy-start(bf16[1,128,1024]{2,1,0:T(8,128)(2,1)} %get-tuple-element.113) | copy-start | bytes 786436
  313.8 18.8 %copy-start.21 = (bf16[1,128,1024]{2,1,0:T(8,128)(2,1)S(1)}, bf16[1,128,1024]{2,1,0:T(8,128)(2,1)}, u32[]{:S(2)}) copy-start(bf16[1,128,1024]{2,1,0:T(8,128)(2,1)} %get-tuple-element.114) | copy-start | bytes 786436
  313.8 18.8 %copy-start.23 = (bf16[1,128,1024]{2,1,0:T(8,128)(2,1)S(1)}, bf16[1,128,1024]{2,1,0:T(8,128)(2,1)}, u32[]{:S(2)}) copy-start(bf16[1,128,1024]{2,1,0:T(8,128)(2,1)} %get-tuple-element.115) | copy-start | bytes 786436
  313.8 18.8 %copy-start.25 = (bf16[1,128,1024]{2,1,0:T(8,128)(2,1)S(1)}, bf16[1,128,1024]{2,1,0:T(8,128)(2,1)}, u32[]{:S(2)}) copy-start(bf16[1,128,1024]{2,1,0:T(8,128)(2,1)} %copy-done.24) | copy-start | bytes 786436
  313.8 18.8 %copy-start.27 = (bf16[1,128,1024]{2,1,0:T(8,128)(2,1)S(1)}, bf16[1,128,1024]{2,1,0:T(8,128)(2,1)}, u32[]{:S(2)}) copy-start(bf16[1,128,1024]{2,1,0:T(8,128)(2,1)} %copy-done.26) | copy-start | bytes 786436
  313.8 18.8 %copy-start.29 = (bf16[1,128,1024]{2,1,0:T(8,128)(2,1)S(1)}, bf16[1,128,1024]{2,1,0:T(8,128)(2,1)}, u32[]{:S(2)}) copy-start(bf16[1,128,1024]{2,1,0:T(8,128)(2,1)} %copy-done.28) | copy-start | bytes 786436
  313.8 18.8 %copy-start.31 = (bf16[1,128,1024]{2,1,0:T(8,128)(2,1)S(1)}, bf16[1,128,1024]{2,1,0:T(8,128)(2,1)}, u32[]{:S(2)}) copy-start(bf16[1,128,1024]{2,1,0:T(8,128)(2,1)} %copy-done.30) | copy-start | bytes 786436
  313.8 12.3 %collective-permute-start.1 = (bf16[3,1024,1024]{2,1,0:T(8,128)(2,1)S(1)}, bf16[3,1024,1024]{2,1,0:T(8,128)(2,1)S(1)}, u32[]{:S(2)}, u32[]{:S(2)}) collective-permute-start(bf16[3,1024,1024]{2,1,0:T(8,128)(2,1)S(1)} %convolution_convert_fusion.1), channel_id=1, source_target_pairs={{0,32},{32,0},{1,33},{33,1},{2,34},{34,2},{3,35},{35,3},{4,36},{36... | collective-permute-start | bytes 18874376 | tf_op jit(solution)/shard_map/ppermute | solution.py:402
  357.2 366.3 %copy-start.33 = (bf16[1,128,16,64]{1,3,2,0:T(8,128)(2,1)S(1)}, bf16[1,128,16,64]{1,3,2,0:T(8,128)(2,1)}, u32[]{:S(2)}) copy-start(bf16[1,128,16,64]{1,3,2,0:T(8,128)(2,1)} %get-tuple-element.124) | copy-start | bytes 786436
  357.2 366.3 %copy-start.39 = (bf16[1,128,16,64]{1,3,2,0:T(8,128)(2,1)S(1)}, bf16[1,128,16,64]{1,3,2,0:T(8,128)(2,1)}, u32[]{:S(2)}) copy-start(bf16[1,128,16,64]{1,3,2,0:T(8,128)(2,1)} %get-tuple-element.122) | copy-start | bytes 786436
  357.2 366.3 %copy-start.40 = (bf16[16,64,128]{2,1,0:T(8,128)(2,1)S(1)}, bf16[16,64,128]{2,1,0:T(8,128)(2,1)}, u32[]{:S(2)}) copy-start(bf16[16,64,128]{2,1,0:T(8,128)(2,1)} %convolution_convert_fusion.2) | copy-start | bytes 786436
  357.3 366.2 %all-reduce.3.cloned.1.call-start = ((), (), s32[]{:S(2)}) async-start(), calls=%async_computation.3 | async-start | bytes 1835008 | tf_op jit(solution)/shard_map/psum | solution.py:414
  679.5 58.4 %all-gather.7.cloned.1.call-start = ((), (), s32[]{:S(2)}) async-start(), calls=%async_computation.4 | async-start | bytes 2752512 | tf_op jit(solution)/shard_map/all_gather | solution.py:415
  (10 other events, 12.8 us)
Sparse Core Ops, SparseCore 0:
  13.1 164.4 all-gather.4
  179.2 60.3 all-gather.8
  357.4 322.0 reduce-scatter.1
  681.8 41.6 all-reduce.2
  725.1 12.7 all-gather.6

commit v13 on v12

--- a/solution.py
+++ b/solution.py
@@ -388,28 +388,33 @@
     zero = jnp.zeros((tokens, model_width), jnp.bfloat16)
     mine_first = core == 0
 
-    def exchange(lefts, rights):
-        stacked_left = jnp.stack([jnp.stack(side) for side in lefts])
-        stacked_right = jnp.stack([jnp.stack(side) for side in rights])
-
-        def products(pick_first):
-            left = jnp.where(pick_first, stacked_left[0], stacked_left[1])
-            right = jnp.where(pick_first, stacked_right[0], stacked_right[1])
-            return jnp.einsum("btk,btn->bkn", left, right, preferred_element_type=jnp.float32)
-
-        kept = products(mine_first)
-        sent = products(jnp.logical_not(mine_first)).astype(jnp.bfloat16)
-        return kept + lax.ppermute(sent, "core", perm=[(0, 1), (1, 0)]).astype(jnp.float32)
-
-    early = exchange(
+    def stacks(lefts, rights):
+        return (
+            jnp.stack([jnp.stack(side) for side in lefts]),
+            jnp.stack([jnp.stack(side) for side in rights]),
+        )
+
+    def products(stacked, pick_first):
+        stacked_left, stacked_right = stacked
+        left = jnp.where(pick_first, stacked_left[0], stacked_left[1])
+        right = jnp.where(pick_first, stacked_right[0], stacked_right[1])
+        return jnp.einsum("btk,btn->bkn", left, right, preferred_element_type=jnp.float32)
+
+    def handed_over(stacked):
+        sent = products(stacked, jnp.logical_not(mine_first)).astype(jnp.bfloat16)
+        return lax.ppermute(sent, "core", perm=[(0, 1), (1, 0)])
+
+    early = stacks(
         [[g_in[0]] * 4, [col(g_out[0], j) for j in range(4)]],
         [[col(g_in[1], c) for c in range(4)], [g_out[1]] * 4],
     )
-    late = exchange(
+    late = stacks(
         [[g_qkv[0]] * 3, [g_att[0], enc_left, zero]],
         [[col(g_qkv[1], c) for c in range(3)], [g_att[1], enc_right, zero]],
     )
-    half = jnp.concatenate([early, late], axis=0)
+    received = jnp.concatenate([handed_over(early), handed_over(late)], axis=0)
+    every = tuple(jnp.concatenate([a, b], axis=1) for a, b in zip(early, late))
+    half = products(every, mine_first) + received.astype(jnp.float32)
     part = lax.psum_scatter(half, SHARD_AXES, scatter_dimension=1, tiled=True)
     part = lax.psum(part, "xh")
     res = lax.all_gather(part, "core", axis=0, tiled=False)

time: 754 us -> 735 us (0.975)
  other arithmetic: 34.7 us -> 17.5 us
    concatenate x1 -> x2, other arithmetic: 18.6 us -> 0.75 us  [body(): jnp.concatenate([a, b], axis=1)]
    dot_general x4 -> x3, matrix products: 19.8 us -> 21 us  [products(): jnp.einsum('btk,btn->bkn', left, right, preferred_element_type=jnp.float32)]
where the time goes in v13:
time: 735 us; the launch traced here: 734 us
  waiting for transfers between devices  607 us (83%)
  matrix products  54.7 us (7%)
  local copies, waits for them, and re-layouts  25.5 us (3%)
  other arithmetic  17.5 us (2%)
  between operations  15.4 us (2%)
  Pallas kernels  12.8 us (2%)
    reduce_scatter x1, waiting for transfers between devices, body(): part = lax.psum_scatter(half, SHARD_AXES, scatter_dimension=1, tiled=True)  322 us
    all_gather x1, waiting for transfers between devices, body(): gathered = lax.all_gather(mine, SHARD_AXES, axis=0, tiled=True)  165 us
    all_gather x1, waiting for transfers between devices, body(): both = lax.all_gather(gathered, 'core', axis=0, tiled=False)  60.2 us
    psum x1, waiting for transfers between devices, body(): part = lax.psum(part, 'xh')  44 us
    dot_general x3, matrix products, products(): jnp.einsum('btk,btn->bkn', left, right, preferred_element_type=jnp.float32)  21 us
  transfers between devices with their start and end apart: 7, of which 6 were waited for; matrix products, arithmetic and copies ran while one was open for 3% of the time, Pallas kernels for 0%

profile of v13, /device:TPU:1, one launch (start us, length us, event | category | flops | bytes accessed | tf_op | source)
XLA Modules:
  0.0 734.2 jit_solution(17918627218496432992)
XLA Ops:
  7.3 1.5 copy.102
  8.9 0.7 copy.103
  10.2 0.7 reduce.42
  12.1 0.9 maximum_select_fusion
  13.0 164.5 %all-gather.5.cloned.1.call-done = bf16[1024,6156]{1,0:T(8,128)(2,1)} async-done(((bf16[32,6156]{1,0:T(8,128)(2,1)}), bf16[1024,6156]{1,0:T(8,128)(2,1)}) %all-gather.5.cloned.1.call-update) | async-done | bytes 12607504 | tf_op jit(solution)/shard_map/all_gather | solution.py:336
  178.6 0.9 fusion.93
  179.4 60.2 %all-gather.9.cloned.1.call-done = bf16[2048,6156]{1,0:T(8,128)(2,1)} async-done(((bf16[1024,6156]{1,0:T(8,128)(2,1)}), bf16[2048,6156]{1,0:T(8,128)(2,1)}) %all-gather.9.cloned.1.call-update) | async-done | bytes 25214992 | tf_op jit(solution)/shard_map/all_gather | solution.py:337
  239.6 1.1 convert_bitcast_fusion.1
  240.9 1.0 convert_bitcast_fusion.2
  242.4 4.6 fusion.8
  248.4 3.0 convert_reduce_fusion.2
  251.5 2.1 fusion.128
  254.0 1.9 slice.313
  255.9 4.0 slice.312
  259.9 5.6 multiply_convert_fusion
  265.5 1.1 slice_bitcast_fusion.7
  266.9 6.0 shard_map.254
  272.8 1.3 fusion.124
  274.7 1.0 fusion.121
  275.6 0.7 convert_element_type.197.grad_ref
  276.4 6.8 shard_map.255
  283.2 2.8 fusion.119
  286.1 5.3 multiply_reduce_fusion.1
  291.6 0.7 copy-done.2
  293.1 5.4 convolution_convert_fusion
  299.1 2.4 fusion.50
  301.5 0.9 copy.117
  302.6 0.6 fusion.126
  303.4 1.4 fusion.131
  304.8 2.9 fusion.125
  307.8 2.2 convolution_convert_fusion.2
  310.7 1.1 copy.118
  312.0 1.9 convolution_convert_fusion.1
  314.0 0.6 collective-permute-start.1
  316.8 7.7 %collective-permute-done.1 = bf16[3,1024,1024]{2,1,0:T(8,128)(2,1)S(1)} collective-permute-done((bf16[3,1024,1024]{2,1,0:T(8,128)(2,1)S(1)}, bf16[3,1024,1024]{2,1,0:T(8,128)(2,1)S(1)}, u32[]{:S(2)}, u32[]{:S(2)}) %collective-permute-start.1) | collective-permute-done | bytes 6291488 | tf_op jit(solution)/shard_map/ppermute | solution.py:405
  324.5 13.7 %convert_add_fusion = f32[7,1024,1024]{2,1,0:T(8,128)} fusion(bf16[3,1024,1024]{2,1,0:T(8,128)(2,1)S(1)} %collective-permute-done.1, bf16[4,1024,1024]{2,1,0:T(8,128)(2,1)} %collective-permute-done, bf16[2,7,128,1024]{3,2,1,0:T(8,128)(2,1)S(1)} %maximum_maximum_fusion.1, bf16[2,7,128,1024]{3,2,1,0:T(8,128)(2,1)S(1)} %maximum_maximum_fusion, pred[]{:T(512)S(6)} %eq.16), kind=kOutput, calls=%fused_computation.1 | convolution fusion | flops 1902903296 | bytes 51381248 | tf_op jit(solution)/shard_map/btk,btn->bkn/dot_general | solution.py:401
  338.2 322.3 %reduce-scatter.2.cloned.1.call-done = f32[7,32,1024]{2,1,0:T(8,128)} async-done(((f32[7,1024,1024]{2,1,0:T(8,128)}), f32[7,32,1024]{2,1,0:T(8,128)}) %reduce-scatter.2.cloned.1.call-update) | async-done | bytes 917520 | tf_op jit(solution)/shard_map/reduce_scatter | solution.py:418
  660.5 44.0 %all-reduce.3.cloned.1.call-done = f32[1,7,32,1024]{3,2,1,0:T(8,128)} async-done(((f32[1,7,32,1024]{3,2,1,0:T(8,128)}), f32[1,7,32,1024]{3,2,1,0:T(8,128)}) %all-reduce.3.cloned.1.call-update) | async-done | bytes 917520 | tf_op jit(solution)/shard_map/psum | solution.py:419
  704.5 5.8 fusion.47
  710.3 8.6 %all-gather.7.cloned.1.call-done = f32[2,7,32,1024]{3,2,1,0:T(8,128)} async-done(((f32[1,7,32,1024]{3,2,1,0:T(8,128)}), f32[2,7,32,1024]{3,2,1,0:T(8,128)}) %all-gather.7.cloned.1.call-update) | async-done | bytes 1835024 | tf_op jit(solution)/shard_map/all_gather | solution.py:420
  718.9 2.3 slice_bitcast_fusion.12
  721.2 0.8 slice_reduce_fusion.2
  722.4 1.0 broadcast_in_dim_reshape.11
  723.4 0.6 broadcast_in_dim_reshape.10
  724.0 0.6 copy.124
  724.7 0.9 copy.125
  725.6 1.4 copy.127
  726.9 0.8 maximum_bitcast_fusion.1
  (171 shorter events, 10.7 us)
Async XLA Ops:
  7.2 3.0 copy-start.45
  7.2 3.8 copy-start.38
  7.2 3.9 copy-start.39
  7.2 4.0 copy-start.40
  7.2 4.1 copy-start.41
  7.2 4.2 copy-start.42
  7.2 4.3 copy-start.43
  7.3 4.4 copy-start.44
  7.3 4.4 copy-start.32
  7.3 170.3 %all-gather.5.cloned.1.call-start = ((), (), s32[]{:S(2)}) async-start(), calls=%async_computation.1 | async-start | bytes 13246464 | tf_op jit(solution)/shard_map/all_gather | solution.py:336
  7.3 4.6 copy-start.37
  8.8 3.2 copy-start.36
  13.0 226.7 %all-gather.9.cloned.1.call-start = ((), (), s32[]{:S(2)}) async-start(), calls=%async_computation.5 | async-start | bytes 38535168 | tf_op jit(solution)/shard_map/all_gather | solution.py:337
  177.6 64.8 %copy-start.14 = (bf16[1,128,1024]{2,1,0:T(8,128)(2,1)S(1)}, bf16[1,128,1024]{2,1,0:T(8,128)(2,1)}, u32[]{:S(2)}) copy-start(bf16[1,128,1024]{2,1,0:T(8,128)(2,1)} %param.17) | copy-start | bytes 786436
  177.6 482.9 %reduce-scatter.2.cloned.1.call-start = ((), (), s32[]{:S(2)}) async-start(), calls=%async_computation.2 | async-start | bytes 30277632 | tf_op jit(solution)/shard_map/reduce_scatter | solution.py:418
  254.0 5.9 copy-start.6
  255.9 4.0 copy-start.4
  259.9 5.7 copy-start
  265.5 1.3 copy-start.1
  283.2 2.9 copy-start.5
  291.4 1.0 copy-start.2
  291.4 1.0 copy-start.7
  291.4 1.3 copy-start.16
  291.4 1.5 copy-start.18
  291.4 1.6 copy-start.20
  291.4 1.7 copy-start.22
  291.5 7.0 copy-start.24
  291.5 7.0 copy-start.26
  291.6 7.0 copy-start.28
  291.6 7.0 copy-start.30
  298.6 25.9 %collective-permute-start = (bf16[4,1024,1024]{2,1,0:T(8,128)(2,1)}, bf16[4,1024,1024]{2,1,0:T(8,128)(2,1)}, u32[]{:S(2)}, u32[]{:S(2)}) collective-permute-start(bf16[4,1024,1024]{2,1,0:T(8,128)(2,1)} %convolution_convert_fusion), channel_id=1, source_target_pairs={{0,32},{32,0},{1,33},{33,1},{2,34},{34,2},{3,35},{35,3},{4,36},{36... | collective-permute-start | bytes 25165832 | tf_op jit(solution)/shard_map/ppermute | solution.py:405
  302.4 2.4 copy-start.9
  304.8 3.0 copy-start.11
  310.0 2.0 copy-start.12
  310.0 2.0 copy-start.13
  310.0 2.0 copy-start.15
  312.0 2.7 copy-start.17
  312.0 2.7 copy-start.19
  312.0 2.7 copy-start.21
  312.0 2.7 copy-start.23
  314.0 1.0 copy-start.27
  314.0 1.1 copy-start.29
  314.0 1.2 copy-start.31
  314.0 10.5 %collective-permute-start.1 = (bf16[3,1024,1024]{2,1,0:T(8,128)(2,1)S(1)}, bf16[3,1024,1024]{2,1,0:T(8,128)(2,1)S(1)}, u32[]{:S(2)}, u32[]{:S(2)}) collective-permute-start(bf16[3,1024,1024]{2,1,0:T(8,128)(2,1)S(1)} %convolution_convert_fusion.1), channel_id=1, source_target_pairs={{0,32},{32,0},{1,33},{33,1},{2,34},{34,2},{3,35},{35,3},{4,36},{36... | collective-permute-start | bytes 18874376 | tf_op jit(solution)/shard_map/ppermute | solution.py:405
  338.1 366.4 %copy-start.33 = (bf16[1,128,16,64]{1,3,2,0:T(8,128)(2,1)S(1)}, bf16[1,128,16,64]{1,3,2,0:T(8,128)(2,1)}, u32[]{:S(2)}) copy-start(bf16[1,128,16,64]{1,3,2,0:T(8,128)(2,1)} %get-tuple-element.122) | copy-start | bytes 786436
  338.1 366.4 %copy-start.35 = (bf16[16,64,128]{2,1,0:T(8,128)(2,1)S(1)}, bf16[16,64,128]{2,1,0:T(8,128)(2,1)}, u32[]{:S(2)}) copy-start(bf16[16,64,128]{2,1,0:T(8,128)(2,1)} %copy-done.34) | copy-start | bytes 786436
  338.1 366.3 %all-reduce.3.cloned.1.call-start = ((), (), s32[]{:S(2)}) async-start(), calls=%async_computation.3 | async-start | bytes 1835008 | tf_op jit(solution)/shard_map/psum | solution.py:419
  660.5 58.4 %all-gather.7.cloned.1.call-start = ((), (), s32[]{:S(2)}) async-start(), calls=%async_computation.4 | async-start | bytes 2752512 | tf_op jit(solution)/shard_map/all_gather | solution.py:420
  (5 other events, 4.2 us)
Sparse Core Ops, SparseCore 0:
  13.1 164.4 all-gather.4
  179.2 60.3 all-gather.8
  338.3 322.1 reduce-scatter.1
  662.8 41.6 all-reduce.2
  706.1 12.7 all-gather.6

commit v14 on v13

--- a/solution.py
+++ b/solution.py
@@ -416,9 +416,11 @@
     every = tuple(jnp.concatenate([a, b], axis=1) for a, b in zip(early, late))
     half = products(every, mine_first) + received.astype(jnp.float32)
     part = lax.psum_scatter(half, SHARD_AXES, scatter_dimension=1, tiled=True)
-    part = lax.psum(part, "xh")
-    res = lax.all_gather(part, "core", axis=0, tiled=False)
-    r0, r1 = res[0], res[1]
+    swap = [(0, 1), (1, 0)]
+    part = part + lax.ppermute(part, "xh", perm=swap)
+    other = lax.ppermute(part, "core", perm=swap)
+    r0 = jnp.where(mine_first, part, other)
+    r1 = jnp.where(mine_first, other, part)
     r_in = ungroup_columns(jnp.concatenate([r0[0], r0[1], r0[2], r0[3]], axis=1), 4)
     r_qkv = jnp.concatenate([r0[4], r0[5], r0[6]], axis=1)
     r_out = jnp.stack([r1[0], r1[1], r1[2], r1[3]], axis=1)

time: 735 us -> 707 us (0.962)
  waiting for transfers between devices: 607 us -> 575 us
    psum x1 -> x0, waiting for transfers between devices: 44 us -> none  [body(): part = lax.psum(part, 'xh')]
    ppermute x0 -> x2, waiting for transfers between devices: none -> 20.6 us  [the longest x1 20.6 us: body(): part = part + lax.ppermute(part, 'xh', perm=swap)]
    all_gather x1 -> x0, waiting for transfers between devices: 8.57 us -> none  [body(): res = lax.all_gather(part, 'core', axis=0, tiled=False)]
  transfers between devices with their start and end apart: 7 -> 7, of which waited for: 6 -> 5; matrix products, arithmetic and copies ran while one was open for 3% -> 3% of each run, Pallas kernels for 0% -> 0%
where the time goes in v14:
time: 707 us; the launch traced here: 706 us
  waiting for transfers between devices  575 us (81%)
  matrix products  54.7 us (8%)
  local copies, waits for them, and re-layouts  24.1 us (3%)
  other arithmetic  18.9 us (3%)
  between operations  15.4 us (2%)
  Pallas kernels  12.8 us (2%)
    reduce_scatter x1, waiting for transfers between devices, body(): part = lax.psum_scatter(half, SHARD_AXES, scatter_dimension=1, tiled=True)  322 us
    all_gather x1, waiting for transfers between devices, body(): gathered = lax.all_gather(mine, SHARD_AXES, axis=0, tiled=True)  165 us
    all_gather x1, waiting for transfers between devices, body(): both = lax.all_gather(gathered, 'core', axis=0, tiled=False)  60.2 us
    dot_general x3, matrix products, products(): jnp.einsum('btk,btn->bkn', left, right, preferred_element_type=jnp.float32)  21 us
    ppermute x1, waiting for transfers between devices, body(): part = part + lax.ppermute(part, 'xh', perm=swap)  20.6 us
  transfers between devices with their start and end apart: 7, of which 5 were waited for; matrix products, arithmetic and copies ran while one was open for 3% of the time, Pallas kernels for 0%

profile of v14, /device:TPU:1, one launch (start us, length us, event | category | flops | bytes accessed | tf_op | source)
XLA Modules:
  0.0 706.1 jit_solution(18112356605205267562)
XLA Ops:
  7.3 1.5 copy.76
  8.9 0.7 copy.77
  10.2 0.7 reduce.42
  12.1 0.9 maximum_select_fusion
  13.0 164.5 %all-gather.4.cloned.1.call-done = bf16[1024,6156]{1,0:T(8,128)(2,1)} async-done(((bf16[32,6156]{1,0:T(8,128)(2,1)}), bf16[1024,6156]{1,0:T(8,128)(2,1)}) %all-gather.4.cloned.1.call-update) | async-done | bytes 12607504 | tf_op jit(solution)/shard_map/all_gather | solution.py:336
  178.6 0.9 fusion.93
  179.4 60.2 %all-gather.6.cloned.1.call-done = bf16[2048,6156]{1,0:T(8,128)(2,1)} async-done(((bf16[1024,6156]{1,0:T(8,128)(2,1)}), bf16[2048,6156]{1,0:T(8,128)(2,1)}) %all-gather.6.cloned.1.call-update) | async-done | bytes 25214992 | tf_op jit(solution)/shard_map/all_gather | solution.py:337
  239.6 1.1 convert_bitcast_fusion.1
  240.9 1.0 convert_bitcast_fusion.2
  242.4 4.6 fusion.8
  248.4 3.0 convert_reduce_fusion.2
  251.5 2.1 fusion.128
  254.0 1.9 slice.282
  255.9 4.0 slice.281
  259.9 5.6 multiply_convert_fusion
  265.5 1.1 slice_bitcast_fusion.7
  266.9 6.0 shard_map.254
  272.8 1.3 fusion.124
  274.7 1.0 fusion.121
  275.6 0.7 convert_element_type.197.grad_ref
  276.4 6.8 shard_map.255
  283.2 2.8 fusion.119
  286.1 5.3 multiply_reduce_fusion.1
  291.6 0.7 copy-done.2
  293.1 5.4 convolution_convert_fusion
  299.1 2.4 fusion.50
  301.5 0.9 copy.91
  303.4 1.4 fusion.131
  304.8 2.9 fusion.125
  307.8 2.2 convolution_convert_fusion.2
  310.7 1.1 copy.92
  312.0 1.9 convolution_convert_fusion.1
  316.8 7.7 %collective-permute-done.1 = bf16[3,1024,1024]{2,1,0:T(8,128)(2,1)S(1)} collective-permute-done((bf16[3,1024,1024]{2,1,0:T(8,128)(2,1)S(1)}, bf16[3,1024,1024]{2,1,0:T(8,128)(2,1)S(1)}, u32[]{:S(2)}, u32[]{:S(2)}) %collective-permute-start.1) | collective-permute-done | bytes 6291488 | tf_op jit(solution)/shard_map/ppermute | solution.py:405
  324.5 13.7 %convert_add_fusion = f32[7,1024,1024]{2,1,0:T(8,128)} fusion(bf16[3,1024,1024]{2,1,0:T(8,128)(2,1)S(1)} %collective-permute-done.1, bf16[4,1024,1024]{2,1,0:T(8,128)(2,1)} %collective-permute-done, bf16[2,7,128,1024]{3,2,1,0:T(8,128)(2,1)S(1)} %maximum_maximum_fusion.1, bf16[2,7,128,1024]{3,2,1,0:T(8,128)(2,1)S(1)} %maximum_maximum_fusion, pred[]{:T(512)S(6)} %eq.16), kind=kOutput, calls=%fused_computation.1 | convolution fusion | flops 1902903296 | bytes 51381248 | tf_op jit(solution)/shard_map/btk,btn->bkn/dot_general | solution.py:401
  338.2 322.3 %reduce-scatter.2.cloned.1.call-done = f32[7,32,1024]{2,1,0:T(8,128)} async-done(((f32[7,1024,1024]{2,1,0:T(8,128)}), f32[7,32,1024]{2,1,0:T(8,128)}) %reduce-scatter.2.cloned.1.call-update) | async-done | bytes 917520 | tf_op jit(solution)/shard_map/reduce_scatter | solution.py:418
  660.4 2.4 collective-permute-start.2
  662.8 20.6 %collective-permute-done.2 = f32[7,32,1024]{2,1,0:T(8,128)S(1)} collective-permute-done((f32[7,32,1024]{2,1,0:T(8,128)}, f32[7,32,1024]{2,1,0:T(8,128)S(1)}, u32[]{:S(2)}, u32[]{:S(2)}) %collective-permute-start.2) | collective-permute-done | bytes 917536 | tf_op jit(solution)/shard_map/ppermute | solution.py:420
  683.4 1.3 add.149
  684.7 1.6 collective-permute-start.3
  686.3 5.8 fusion.47
  692.2 0.7 slice_bitcast_fusion.12
  693.0 0.8 slice_reduce_fusion.2
  694.2 1.0 broadcast_in_dim_reshape.11
  695.2 0.6 broadcast_in_dim_reshape.10
  695.8 0.6 copy.98
  696.6 0.9 copy.99
  697.5 1.4 copy.101
  698.8 0.8 maximum_bitcast_fusion.1
  (172 shorter events, 12.0 us)
Async XLA Ops:
  7.2 3.0 copy-start.45
  7.2 3.8 copy-start.38
  7.2 3.9 copy-start.39
  7.2 4.0 copy-start.40
  7.2 4.1 copy-start.41
  7.2 4.2 copy-start.42
  7.2 4.3 copy-start.43
  7.3 4.4 copy-start.44
  7.3 4.4 copy-start.32
  7.3 170.3 %all-gather.4.cloned.1.call-start = ((), (), s32[]{:S(2)}) async-start(), calls=%async_computation.1 | async-start | bytes 13246464 | tf_op jit(solution)/shard_map/all_gather | solution.py:336
  7.3 4.6 copy-start.37
  8.8 3.2 copy-start.36
  13.0 226.7 %all-gather.6.cloned.1.call-start = ((), (), s32[]{:S(2)}) async-start(), calls=%async_computation.3 | async-start | bytes 38535168 | tf_op jit(solution)/shard_map/all_gather | solution.py:337
  177.6 64.8 %copy-start.14 = (bf16[1,128,1024]{2,1,0:T(8,128)(2,1)S(1)}, bf16[1,128,1024]{2,1,0:T(8,128)(2,1)}, u32[]{:S(2)}) copy-start(bf16[1,128,1024]{2,1,0:T(8,128)(2,1)} %param.17) | copy-start | bytes 786436
  177.6 482.9 %reduce-scatter.2.cloned.1.call-start = ((), (), s32[]{:S(2)}) async-start(), calls=%async_computation.2 | async-start | bytes 30277632 | tf_op jit(solution)/shard_map/reduce_scatter | solution.py:418
  254.0 5.9 copy-start.6
  255.9 4.0 copy-start.4
  259.9 5.7 copy-start
  265.5 1.3 copy-start.1
  283.2 2.9 copy-start.5
  291.4 1.0 copy-start.2
  291.4 1.0 copy-start.7
  291.4 1.3 copy-start.16
  291.4 1.5 copy-start.18
  291.4 1.6 copy-start.20
  291.4 1.7 copy-start.22
  291.5 7.0 copy-start.24
  291.5 7.0 copy-start.26
  291.6 7.0 copy-start.28
  291.6 7.0 copy-start.30
  298.6 25.9 %collective-permute-start = (bf16[4,1024,1024]{2,1,0:T(8,128)(2,1)}, bf16[4,1024,1024]{2,1,0:T(8,128)(2,1)}, u32[]{:S(2)}, u32[]{:S(2)}) collective-permute-start(bf16[4,1024,1024]{2,1,0:T(8,128)(2,1)} %convolution_convert_fusion), channel_id=1, source_target_pairs={{0,32},{32,0},{1,33},{33,1},{2,34},{34,2},{3,35},{35,3},{4,36},{36... | collective-permute-start | bytes 25165832 | tf_op jit(solution)/shard_map/ppermute | solution.py:405
  302.4 2.4 copy-start.9
  304.8 3.0 copy-start.11
  310.0 2.0 copy-start.12
  310.0 2.0 copy-start.13
  310.0 2.0 copy-start.15
  312.0 2.7 copy-start.17
  312.0 2.7 copy-start.19
  312.0 2.7 copy-start.21
  312.0 2.7 copy-start.23
  314.0 1.0 copy-start.27
  314.0 1.1 copy-start.29
  314.0 1.2 copy-start.31
  314.0 10.5 %collective-permute-start.1 = (bf16[3,1024,1024]{2,1,0:T(8,128)(2,1)S(1)}, bf16[3,1024,1024]{2,1,0:T(8,128)(2,1)S(1)}, u32[]{:S(2)}, u32[]{:S(2)}) collective-permute-start(bf16[3,1024,1024]{2,1,0:T(8,128)(2,1)S(1)} %convolution_convert_fusion.1), channel_id=1, source_target_pairs={{0,32},{32,0},{1,33},{33,1},{2,34},{34,2},{3,35},{35,3},{4,36},{36... | collective-permute-start | bytes 18874376 | tf_op jit(solution)/shard_map/ppermute | solution.py:405
  338.1 348.2 %copy-start.33 = (bf16[1,128,16,64]{1,3,2,0:T(8,128)(2,1)S(1)}, bf16[1,128,16,64]{1,3,2,0:T(8,128)(2,1)}, u32[]{:S(2)}) copy-start(bf16[1,128,16,64]{1,3,2,0:T(8,128)(2,1)} %get-tuple-element.110) | copy-start | bytes 786436
  338.2 348.1 %copy-start.35 = (bf16[16,64,128]{2,1,0:T(8,128)(2,1)S(1)}, bf16[16,64,128]{2,1,0:T(8,128)(2,1)}, u32[]{:S(2)}) copy-start(bf16[16,64,128]{2,1,0:T(8,128)(2,1)} %copy-done.34) | copy-start | bytes 786436
  660.4 23.0 %collective-permute-start.2 = (f32[7,32,1024]{2,1,0:T(8,128)}, f32[7,32,1024]{2,1,0:T(8,128)S(1)}, u32[]{:S(2)}, u32[]{:S(2)}) collective-permute-start(f32[7,32,1024]{2,1,0:T(8,128)} %reduce-scatter.2.cloned.1.call-done), channel_id=1, source_target_pairs={{0,64},{64,0},{1,65},{65,1},{2,66},{66,2},{3,67},{67,3},{4,68},{68... | collective-permute-start | bytes 2752520 | tf_op jit(solution)/shard_map/ppermute | solution.py:420
  684.7 7.4 %collective-permute-start.3 = (f32[7,32,1024]{2,1,0:T(8,128)S(1)}, f32[7,32,1024]{2,1,0:T(8,128)S(1)}, u32[]{:S(2)}, u32[]{:S(2)}) collective-permute-start(f32[7,32,1024]{2,1,0:T(8,128)S(1)} %add.149), channel_id=1, source_target_pairs={{0,32},{32,0},{1,33},{33,1},{2,34},{34,2},{3,35},{35,3},{4,36},{36... | collective-permute-start | bytes 2752520 | tf_op jit(solution)/shard_map/ppermute | solution.py:421
  (5 other events, 4.2 us)
Sparse Core Ops, SparseCore 0:
  13.1 164.4 all-gather.3
  179.2 60.3 all-gather.5
  338.3 322.1 reduce-scatter.1

commit v15 on v14

--- a/solution.py
+++ b/solution.py
@@ -405,12 +405,12 @@
         return lax.ppermute(sent, "core", perm=[(0, 1), (1, 0)])
 
     early = stacks(
-        [[g_in[0]] * 4, [col(g_out[0], j) for j in range(4)]],
-        [[col(g_in[1], c) for c in range(4)], [g_out[1]] * 4],
+        [[g_in[0]] * 4 + [zero], [col(g_out[0], j) for j in range(4)] + [g_att[0]]],
+        [[col(g_in[1], c) for c in range(4)] + [zero], [g_out[1]] * 4 + [g_att[1]]],
     )
     late = stacks(
-        [[g_qkv[0]] * 3, [g_att[0], enc_left, zero]],
-        [[col(g_qkv[1], c) for c in range(3)], [g_att[1], enc_right, zero]],
+        [[g_qkv[0]] * 2, [g_qkv[0], enc_left]],
+        [[col(g_qkv[1], 0), col(g_qkv[1], 1)], [col(g_qkv[1], 2), enc_right]],
     )
     received = jnp.concatenate([handed_over(early), handed_over(late)], axis=0)
     every = tuple(jnp.concatenate([a, b], axis=1) for a, b in zip(early, late))
@@ -422,10 +422,10 @@
     r0 = jnp.where(mine_first, part, other)
     r1 = jnp.where(mine_first, other, part)
     r_in = ungroup_columns(jnp.concatenate([r0[0], r0[1], r0[2], r0[3]], axis=1), 4)
-    r_qkv = jnp.concatenate([r0[4], r0[5], r0[6]], axis=1)
+    r_qkv = jnp.concatenate([r0[5], r0[6], r1[5]], axis=1)
     r_out = jnp.stack([r1[0], r1[1], r1[2], r1[3]], axis=1)
     r_att = r1[4]
-    r_small = r1[5][:, :n_small]
+    r_small = r1[6][:, :n_small]
     grad_inputs = upstream.reshape(inputs.shape)
     return (
         outputs,

time: 707 us -> 719 us (1.017)
  local copies, waits for them, and re-layouts: 24.1 us -> 31.5 us
  transfers between devices with their start and end apart: 7 -> 7, of which waited for: 5 -> 5; matrix products, arithmetic and copies ran while one was open for 3% -> 4% of each run, Pallas kernels for 0% -> 0%
where the time goes in v15:
time: 719 us; the launch traced here: 718 us
  waiting for transfers between devices  573 us (80%)
  matrix products  59.6 us (8%)
  local copies, waits for them, and re-layouts  31.5 us (4%)
  other arithmetic  20.8 us (3%)
  between operations  15.3 us (2%)
  Pallas kernels  13.3 us (2%)
    reduce_scatter x1, waiting for transfers between devices, body(): part = lax.psum_scatter(half, SHARD_AXES, scatter_dimension=1, tiled=True)  322 us
    all_gather x1, waiting for transfers between devices, body(): gathered = lax.all_gather(mine, SHARD_AXES, axis=0, tiled=True)  165 us
    all_gather x1, waiting for transfers between devices, body(): both = lax.all_gather(gathered, 'core', axis=0, tiled=False)  61.3 us
    dot_general x3, matrix products, products(): jnp.einsum('btk,btn->bkn', left, right, preferred_element_type=jnp.float32)  22 us
    ppermute x1, waiting for transfers between devices, body(): part = part + lax.ppermute(part, 'xh', perm=swap)  20.6 us
  transfers between devices with their start and end apart: 7, of which 5 were waited for; matrix products, arithmetic and copies ran while one was open for 4% of the time, Pallas kernels for 0%

profile of v15, /device:TPU:1, one launch (start us, length us, event | category | flops | bytes accessed | tf_op | source)
XLA Modules:
  0.0 717.8 jit_solution(13148378374993290792)
XLA Ops:
  7.3 1.5 copy.76
  12.1 0.9 maximum_select_fusion
  13.0 164.5 %all-gather.4.cloned.1.call-done = bf16[1024,6156]{1,0:T(8,128)(2,1)} async-done(((bf16[32,6156]{1,0:T(8,128)(2,1)}), bf16[1024,6156]{1,0:T(8,128)(2,1)}) %all-gather.4.cloned.1.call-update) | async-done | bytes 12607504 | tf_op jit(solution)/shard_map/all_gather | solution.py:336
  178.3 61.3 %all-gather.6.cloned.1.call-done = bf16[2048,6156]{1,0:T(8,128)(2,1)} async-done(((bf16[1024,6156]{1,0:T(8,128)(2,1)}), bf16[2048,6156]{1,0:T(8,128)(2,1)}) %all-gather.6.cloned.1.call-update) | async-done | bytes 25214992 | tf_op jit(solution)/shard_map/all_gather | solution.py:337
  239.6 1.1 convert_bitcast_fusion.1
  240.9 1.0 convert_bitcast_fusion.2
  242.4 4.6 fusion.8
  248.3 0.9 copy.91
  249.2 3.0 convert_reduce_fusion.2
  252.2 2.1 fusion.129
  254.9 2.2 slice.282
  257.1 4.0 slice.281
  261.1 5.6 multiply_convert_fusion
  266.8 1.0 copy-done.12
  267.8 6.0 shard_map.254
  273.8 1.4 fusion.125
  275.5 1.0 fusion.74
  276.5 1.2 bitcast_dynamic-update-slice_fusion.3
  277.7 7.3 %shard_map.255 = f32[128,4096]{1,0:T(8,128)} custom-call(bf16[128,1024]{1,0:T(8,128)(2,1)} %get-tuple-element.80.grad_ref, bf16[2,1024,6156]{2,1,0:T(8,128)(2,1)} %bitcast.224), custom_call_target="tpu_custom_call" | custom-call | flops 1073741824 | bytes 10747904 | tf_op jit(solution)/shard_map/pallas_call | solution.py:63
  287.1 2.8 fusion.121
  290.1 5.3 multiply_reduce_fusion.1
  295.6 1.6 copy-done.4
  297.3 1.0 bitcast_dynamic-update-slice_fusion
  298.3 5.5 convolution_convert_fusion
  304.4 1.1 reduce_sum.186
  305.5 1.1 reduce_sum.183
  306.6 3.3 fusion.51
  309.9 1.8 copy.87
  311.7 2.1 fusion.127
  313.9 1.8 copy.94
  315.7 2.3 fusion.132
  318.0 2.8 fusion.126
  320.9 2.8 convolution_convert_fusion.2
  323.7 1.1 copy.93
  324.8 1.1 copy.92
  326.0 2.3 convolution_convert_fusion.1
  330.4 1.0 copy-done.10
  331.7 3.9 collective-permute-done.1
  335.6 14.2 %convert_add_fusion = f32[7,1024,1024]{2,1,0:T(8,128)} fusion(bf16[2,1024,1024]{2,1,0:T(8,128)(2,1)S(1)} %collective-permute-done.1, bf16[5,1024,1024]{2,1,0:T(8,128)(2,1)} %collective-permute-done, bf16[2,7,128,1024]{3,2,1,0:T(8,128)(2,1)S(1)} %maximum_maximum_fusion.1, bf16[2,7,128,1024]{3,2,1,0:T(8,128)(2,1)S(1)} %maximum_maximum_fusion, pred[]{:T(512)S(6)} %eq.16), kind=kOutput, calls=%fused_computation.1 | convolution fusion | flops 1902903296 | bytes 51381248 | tf_op jit(solution)/shard_map/btk,btn->bkn/dot_general | solution.py:401
  349.9 322.3 %reduce-scatter.2.cloned.1.call-done = f32[7,32,1024]{2,1,0:T(8,128)} async-done(((f32[7,1024,1024]{2,1,0:T(8,128)}), f32[7,32,1024]{2,1,0:T(8,128)}) %reduce-scatter.2.cloned.1.call-update) | async-done | bytes 917520 | tf_op jit(solution)/shard_map/reduce_scatter | solution.py:418
  672.1 2.4 collective-permute-start.2
  674.6 20.6 %collective-permute-done.2 = f32[7,32,1024]{2,1,0:T(8,128)S(1)} collective-permute-done((f32[7,32,1024]{2,1,0:T(8,128)}, f32[7,32,1024]{2,1,0:T(8,128)S(1)}, u32[]{:S(2)}, u32[]{:S(2)}) %collective-permute-start.2) | collective-permute-done | bytes 917536 | tf_op jit(solution)/shard_map/ppermute | solution.py:420
  695.1 1.3 add.149
  696.4 1.6 collective-permute-start.3
  698.0 5.8 fusion.48
  706.0 1.0 broadcast_in_dim_reshape.11
  708.3 0.9 copy.99
  709.2 1.4 copy.101
  (169 shorter events, 15.8 us)
Async XLA Ops:
  7.2 3.0 copy-start.38
  7.2 3.8 copy-start.31
  7.2 3.9 copy-start.32
  7.2 4.0 copy-start.33
  7.2 4.1 copy-start.34
  7.2 4.2 copy-start.35
  7.2 4.3 copy-start.36
  7.3 4.4 copy-start.37
  7.3 4.4 copy-start.26
  7.3 170.3 %all-gather.4.cloned.1.call-start = ((), (), s32[]{:S(2)}) async-start(), calls=%async_computation.1 | async-start | bytes 13246464 | tf_op jit(solution)/shard_map/all_gather | solution.py:336
  7.3 4.6 copy-start.30
  8.8 3.2 copy-start.29
  13.0 226.7 %all-gather.6.cloned.1.call-start = ((), (), s32[]{:S(2)}) async-start(), calls=%async_computation.3 | async-start | bytes 38535168 | tf_op jit(solution)/shard_map/all_gather | solution.py:337
  177.6 64.8 %copy-start.1 = (bf16[1,128,1024]{2,1,0:T(8,128)(2,1)S(1)}, bf16[1,128,1024]{2,1,0:T(8,128)(2,1)}, u32[]{:S(2)}) copy-start(bf16[1,128,1024]{2,1,0:T(8,128)(2,1)} %param.17) | copy-start | bytes 786436
  177.6 494.5 %reduce-scatter.2.cloned.1.call-start = ((), (), s32[]{:S(2)}) async-start(), calls=%async_computation.2 | async-start | bytes 30277632 | tf_op jit(solution)/shard_map/reduce_scatter | solution.py:418
  247.1 0.9 copy-start.24
  247.5 0.9 copy-start.17
  247.5 0.9 copy-start.25
  254.8 2.3 copy-start.7
  257.1 4.0 copy-start.18
  261.1 5.7 copy-start.11
  266.8 1.0 copy-start.12
  273.8 1.7 copy-start.13
  273.8 1.7 copy-start.15
  277.7 7.3 %copy-start = (bf16[128,1024]{1,0:T(8,128)(2,1)S(1)}, bf16[128,1024]{1,0:T(8,128)(2,1)}, u32[]{:S(2)}) copy-start(bf16[128,1024]{1,0:T(8,128)(2,1)} %get-tuple-element.80.grad_ref) | copy-start | bytes 786436
  287.1 2.9 copy-start.19
  287.1 2.9 copy-start.21
  290.1 5.5 copy-start.8
  290.1 5.5 copy-start.22
  295.4 1.9 copy-start.4
  295.6 8.2 %copy-start.2 = (bf16[5,128,1024]{2,1,0:T(8,128)(2,1)}, bf16[5,128,1024]{2,1,0:T(8,128)(2,1)S(1)}, u32[]{:S(2)}) copy-start(bf16[5,128,1024]{2,1,0:T(8,128)(2,1)S(1)} %broadcast_dynamic-update-slice_fusion) | copy-start | bytes 3932164
  295.6 8.2 %copy-start.9 = (bf16[5,128,1024]{2,1,0:T(8,128)(2,1)}, bf16[5,128,1024]{2,1,0:T(8,128)(2,1)S(1)}, u32[]{:S(2)}) copy-start(bf16[5,128,1024]{2,1,0:T(8,128)(2,1)S(1)} %get-tuple-element.126) | copy-start | bytes 3932164
  298.3 5.5 copy-start.5
  298.3 5.9 copy-start.16
  303.8 31.8 %collective-permute-start = (bf16[5,1024,1024]{2,1,0:T(8,128)(2,1)}, bf16[5,1024,1024]{2,1,0:T(8,128)(2,1)}, u32[]{:S(2)}, u32[]{:S(2)}) collective-permute-start(bf16[5,1024,1024]{2,1,0:T(8,128)(2,1)} %convolution_convert_fusion), channel_id=1, source_target_pairs={{0,32},{32,0},{1,33},{33,1},{2,34},{34,2},{3,35},{35,3},{4,36},{36... | collective-permute-start | bytes 31457288 | tf_op jit(solution)/shard_map/ppermute | solution.py:405
  326.0 2.8 copy-start.14
  328.4 1.3 copy-start.3
  328.4 1.7 copy-start.6
  328.4 7.2 %collective-permute-start.1 = (bf16[2,1024,1024]{2,1,0:T(8,128)(2,1)S(1)}, bf16[2,1024,1024]{2,1,0:T(8,128)(2,1)S(1)}, u32[]{:S(2)}, u32[]{:S(2)}) collective-permute-start(bf16[2,1024,1024]{2,1,0:T(8,128)(2,1)S(1)} %convolution_convert_fusion.1), channel_id=1, source_target_pairs={{0,32},{32,0},{1,33},{33,1},{2,34},{34,2},{3,35},{35,3},{4,36},{36... | collective-permute-start | bytes 12582920 | tf_op jit(solution)/shard_map/ppermute | solution.py:405
  330.1 1.3 copy-start.10
  349.8 348.2 %copy-start.20 = (f32[128,1024]{1,0:T(8,128)S(1)}, f32[128,1024]{1,0:T(8,128)}, u32[]{:S(2)}) copy-start(f32[128,1024]{1,0:T(8,128)} %get-tuple-element.78) | copy-start | bytes 1572868
  349.8 348.1 %copy-start.23 = (bf16[1,128,16,64]{1,3,2,0:T(8,128)(2,1)S(1)}, bf16[1,128,16,64]{1,3,2,0:T(8,128)(2,1)}, u32[]{:S(2)}) copy-start(bf16[1,128,16,64]{1,3,2,0:T(8,128)(2,1)} %get-tuple-element.107) | copy-start | bytes 786436
  349.9 348.1 %copy-start.27 = (bf16[1,128,16,64]{1,3,2,0:T(8,128)(2,1)S(1)}, bf16[1,128,16,64]{1,3,2,0:T(8,128)(2,1)}, u32[]{:S(2)}) copy-start(bf16[1,128,16,64]{1,3,2,0:T(8,128)(2,1)} %get-tuple-element.105) | copy-start | bytes 786436
  349.9 348.1 %copy-start.28 = (bf16[16,64,128]{2,1,0:T(8,128)(2,1)S(1)}, bf16[16,64,128]{2,1,0:T(8,128)(2,1)}, u32[]{:S(2)}) copy-start(bf16[16,64,128]{2,1,0:T(8,128)(2,1)} %convolution_convert_fusion.2) | copy-start | bytes 786436
  672.1 23.0 %collective-permute-start.2 = (f32[7,32,1024]{2,1,0:T(8,128)}, f32[7,32,1024]{2,1,0:T(8,128)S(1)}, u32[]{:S(2)}, u32[]{:S(2)}) collective-permute-start(f32[7,32,1024]{2,1,0:T(8,128)} %reduce-scatter.2.cloned.1.call-done), channel_id=1, source_target_pairs={{0,64},{64,0},{1,65},{65,1},{2,66},{66,2},{3,67},{67,3},{4,68},{68... | collective-permute-start | bytes 2752520 | tf_op jit(solution)/shard_map/ppermute | solution.py:420
  696.4 7.4 %collective-permute-start.3 = (f32[7,32,1024]{2,1,0:T(8,128)S(1)}, f32[7,32,1024]{2,1,0:T(8,128)S(1)}, u32[]{:S(2)}, u32[]{:S(2)}) collective-permute-start(f32[7,32,1024]{2,1,0:T(8,128)S(1)} %add.149), channel_id=1, source_target_pairs={{0,32},{32,0},{1,33},{33,1},{2,34},{34,2},{3,35},{35,3},{4,36},{36... | collective-permute-start | bytes 2752520 | tf_op jit(solution)/shard_map/ppermute | solution.py:421
Sparse Core Ops, SparseCore 0:
  13.1 164.4 all-gather.3
  179.2 60.3 all-gather.5
  350.0 322.1 reduce-scatter.1
